TPU v7x, 256 devices: a whole 4x4x8 slice. The times are simulated.
256 devices in a mesh: user: 16 (over z, core), item: 16 (over y, x).
Axes of the slice: x: 4, y: 4, z: 8, core: 2. Of those that a mesh axis runs over, the one named last changes fastest.
Arguments:
- user_factors: float32 [8192, 256], P('user'), may hold values from -0.3 to 0.3, as said below
- item_factors: float32 [8192, 256], P('item'), may hold values from -0.6 to 0.6
- tile_user: int32 [16, 16, 16, 2], P('item', 'user'), may hold values from 0 to 3
- tile_item: int32 [16, 16, 16, 2], P('item', 'user'), may hold values from 0 to 3
- tile_count: int32 [16, 16, 16], P('item', 'user'), may hold values from 1 to 2, as said below
- tile_conf: bfloat16 [16, 16, 16, 2, 128, 128], P('item', 'user'), may hold values from 0.099609375 to 4
- held_user: int32 [16, 16, 16, 2], P('user', 'item'), may hold values from 0 to 1
- held_item: int32 [16, 16, 16, 2], P('user', 'item'), may hold values from 0 to 3
- held_count: int32 [16, 16, 16], P('user', 'item'), may hold values from 1 to 2, as said below
- held_conf: bfloat16 [16, 16, 16, 2, 128, 128], P('user', 'item'), may hold values from 0.099609375 to 4
Outputs:
- new_items: float32 [8192, 256], P('item')
- folded_users: float32 [4096, 256], P('user')
Inputs may be any that keep to these rules, and one draw needn't show every extreme that they name: `user_factors`: user factors; the scale of a factor column varies by up to a factor of ten. `tile_count`: some device has an owner with all 2 slots live and one with a single live slot. `held_count`: some device has an owner with all 2 slots live and one with a single live slot.
All inputs are finite; a program needn't handle non-finite values.
Results may differ from a plain program's by a relative error of at most 0.0003.
Values may be sent and summed in bfloat16 or wider, within the bound.
No kernel may reach another device: no remote copies, remote signals or barrier semaphores. Data moves between devices by JAX's collectives and lax.ppermute only.
A program may use at most 128 MiB of HBM per device.

v0:
```python
import jax
import jax.numpy as jnp
from jax import lax
from jax.sharding import PartitionSpec as P

HB_DEV = 2
ITERS = 2


highest = lax.Precision.HIGHEST
ridge_weight = 1.0
epsilon = 1e-06


def local_gram(rows):
    return jnp.einsum("nk,nm->km", rows, rows, precision=highest)


def gram_apply(vector, gram):
    return jnp.einsum("jck,km->jcm", vector, gram, precision=highest) + ridge_weight * vector


def block_onehot(positions, blocks):
    return (positions[:, None] == jnp.arange(blocks, dtype=jnp.int32)[None, :]).astype(jnp.float32)


def item_terms(factors, weights, positions, onehot, vector):
    picked = vector[positions]
    scores = jnp.einsum("tuk,tik->tui", factors, picked, precision=highest) * weights
    terms = jnp.einsum("tui,tuk->tik", scores, factors, precision=highest)
    return jnp.einsum("tj,tik->jik", onehot, terms, precision=highest)


def item_right(factors, right_weights, onehot):
    terms = jnp.einsum("tui,tuk->tik", right_weights, factors, precision=highest)
    return jnp.einsum("tj,tik->jik", onehot, terms, precision=highest)


def held_terms(factors, weights, positions, onehot, vector):
    picked = vector[positions]
    scores = jnp.einsum("tik,thk->thi", factors, picked, precision=highest) * weights
    terms = jnp.einsum("thi,tik->thk", scores, factors, precision=highest)
    return jnp.einsum("tj,thk->jhk", onehot, terms, precision=highest)


def held_right(factors, right_weights, onehot):
    terms = jnp.einsum("thi,tik->thk", right_weights, factors, precision=highest)
    return jnp.einsum("tj,thk->jhk", onehot, terms, precision=highest)


def conjugate(operator, residual, start):
    solution = start
    direction = residual
    norm_now = jnp.sum(residual * residual, axis=-1, keepdims=True)
    for iteration in range(ITERS):
        image = operator(direction)
        alpha = norm_now / (jnp.sum(direction * image, axis=-1, keepdims=True) + epsilon)
        solution = solution + alpha * direction
        residual = residual - alpha * image
        norm_next = jnp.sum(residual * residual, axis=-1, keepdims=True)
        direction = residual + norm_next / (norm_now + epsilon) * direction
        norm_now = norm_next
    return solution


def user_total(partial_value):
    return lax.psum(partial_value, "user")


def item_total(partial_value):
    return lax.psum(partial_value, "item")


def tile_weights(confidence, live_slots, tile_width):
    live_flat = live_slots.reshape(-1).astype(jnp.float32)[:, None, None]
    conf_flat = confidence.reshape(-1, tile_width, tile_width).astype(jnp.float32)
    return (conf_flat * live_flat, (1.0 + conf_flat) * live_flat)


def shards(
    user_factors,
    item_factors,
    tile_user,
    tile_item,
    tile_count,
    tile_conf,
    held_user,
    held_item,
    held_count,
    held_conf,
):
    factor_rank = user_factors.shape[1]
    tile_width = tile_conf.shape[-1]
    user_peers = lax.axis_size("user")
    item_peers = lax.axis_size("item")
    user_index = tile_user[0, 0]
    item_index = tile_item[0, 0]
    slot_count = user_index.shape[1]
    live_slots = (
        jnp.arange(slot_count, dtype=jnp.int32)[None, :] < tile_count[0, 0][:, None]
    ).astype(jnp.int32)
    confidence = tile_conf[0, 0]
    whole_users = lax.all_gather(user_factors, "user", axis=0, tiled=True)
    gram_users = lax.psum(local_gram(user_factors), "user")
    user_table = whole_users.reshape(user_peers, -1, tile_width, factor_rank)
    tile_factors = user_table[jnp.arange(user_peers, dtype=jnp.int32)[:, None], user_index]
    factors = tile_factors.reshape(-1, tile_width, factor_rank)
    weights, right_weights = tile_weights(confidence, live_slots, tile_width)
    item_blocks = item_factors.shape[0] // tile_width
    positions = item_index.reshape(-1)
    onehot = block_onehot(positions, item_blocks)
    warm_start = item_factors.reshape(item_blocks, tile_width, factor_rank)

    def item_operator(direction):
        return user_total(item_terms(factors, weights, positions, onehot, direction)) + gram_apply(
            direction, gram_users
        )

    start_total = user_total(
        item_right(factors, right_weights, onehot)
        - item_terms(factors, weights, positions, onehot, warm_start)
    )
    residual = start_total - gram_apply(warm_start, gram_users)
    own_items = conjugate(item_operator, residual, warm_start)
    new_items = own_items.reshape(-1, factor_rank)
    held_index = held_user[0, 0]
    owner_index = held_item[0, 0]
    held_slots = owner_index.shape[1]
    held_live = (
        jnp.arange(held_slots, dtype=jnp.int32)[None, :] < held_count[0, 0][:, None]
    ).astype(jnp.int32)
    held_confidence = held_conf[0, 0]
    whole_items = lax.all_gather(new_items, "item", axis=0, tiled=True)
    gram_items = lax.psum(local_gram(new_items), "item")
    item_table = whole_items.reshape(item_peers, -1, tile_width, factor_rank)
    held_factors = item_table[jnp.arange(item_peers, dtype=jnp.int32)[:, None], owner_index]
    held_flat = held_factors.reshape(-1, tile_width, factor_rank)
    held_weights, held_right_weights = tile_weights(held_confidence, held_live, tile_width)
    held_positions = held_index.reshape(-1)
    held_onehot = block_onehot(held_positions, HB_DEV)

    def held_operator(direction):
        return item_total(
            held_terms(held_flat, held_weights, held_positions, held_onehot, direction)
        ) + gram_apply(direction, gram_items)

    held_residual = item_total(held_right(held_flat, held_right_weights, held_onehot))
    zero_start = jnp.zeros((HB_DEV, tile_width, factor_rank), jnp.float32)
    folded_users = conjugate(held_operator, held_residual, zero_start).reshape(-1, factor_rank)
    return (new_items, folded_users)


def solution(mesh):
    in_specs = (
        P("user", None),
        P("item", None),
        P("item", "user", None, None),
        P("item", "user", None, None),
        P("item", "user", None),
        P("item", "user", None, None, None, None),
        P("user", "item", None, None),
        P("user", "item", None, None),
        P("user", "item", None),
        P("user", "item", None, None, None, None),
    )
    out_specs = (P("item", None), P("user", None))
    return jax.shard_map(shards, mesh=mesh, in_specs=in_specs, out_specs=out_specs, check_vma=False)
```

profile of v0, /device:TPU:1, one launch (start us, length us, event | category | flops | bytes accessed | tf_op | source)
XLA Modules:
  0.0 905.0 jit_solution(9983996490653584908)
XLA Ops:
  16.2 53.8 %all-gather.3.cloned.1.call-done = f32[8192,256]{1,0:T(8,128)} async-done(((f32[512,256]{1,0:T(8,128)}), f32[8192,256]{1,0:T(8,128)}) %all-gather.3.cloned.1.call-update) | async-done | bytes 8388624 | tf_op jit(solution)/shard_map/all_gather | solution.py:103
  70.0 6.1 gather_fusion
  76.1 8.0 fusion.80
  84.1 4.5 fusion.30
  88.6 4.7 fusion.23
  102.4 108.6 %all-reduce.19.cloned.1.call-done = (f32[4,128,256]{2,1,0:T(8,128)}, f32[256,256]{1,0:T(8,128)}) async-done(((f32[4,128,256]{2,1,0:T(8,128)}, f32[256,256]{1,0:T(8,128)}), (f32[4,128,256]{2,1,0:T(8,128)}, f32[256,256]{1,0:T(8,128)})) %all-reduce.19.cloned.1.call-update) | async-done | bytes 786448 | tf_op jit(solution)/shard_map/psum | solution.py:67
  215.5 8.0 fusion.82
  223.5 4.5 fusion.25
  228.1 4.0 fusion.8
  233.0 110.1 %all-reduce.9.cloned.1.call-done = f32[4,128,256]{2,1,0:T(8,128)} async-done(((f32[4,128,256]{2,1,0:T(8,128)}), f32[4,128,256]{2,1,0:T(8,128)}) %all-reduce.9.cloned.1.call-update) | async-done | bytes 524304 | tf_op jit(solution)/shard_map/psum | solution.py:67
  348.1 8.0 fusion.83
  356.1 4.5 fusion.27
  360.7 4.0 fusion.6
  365.7 109.9 %all-reduce.11.cloned.1.call-done = f32[4,128,256]{2,1,0:T(8,128)} async-done(((f32[4,128,256]{2,1,0:T(8,128)}), f32[4,128,256]{2,1,0:T(8,128)}) %all-reduce.11.cloned.1.call-update) | async-done | bytes 524304 | tf_op jit(solution)/shard_map/psum | solution.py:67
  479.0 75.9 %all-gather.5.cloned.1.call-done = f32[8192,256]{1,0:T(8,128)} async-done(((f32[512,256]{1,0:T(8,128)}), f32[8192,256]{1,0:T(8,128)}) %all-gather.5.cloned.1.call-update) | async-done | bytes 8388624 | tf_op jit(solution)/shard_map/all_gather | solution.py:133
  554.9 6.2 gather_fusion.4
  561.1 5.6 fusion.33
  573.6 90.7 %all-reduce.13.cloned.1.call-done = f32[2,128,256]{2,1,0:T(8,128)} async-done(((f32[2,128,256]{2,1,0:T(8,128)}), f32[2,128,256]{2,1,0:T(8,128)}) %all-reduce.13.cloned.1.call-update) | async-done | bytes 262160 | tf_op jit(solution)/shard_map/psum | solution.py:71
  668.0 8.0 fusion.84
  676.0 4.5 fusion.19
  685.3 94.8 %all-reduce.17.cloned.1.call-done = (f32[2,128,256]{2,1,0:T(8,128)}, f32[256,256]{1,0:T(8,128)}) async-done(((f32[2,128,256]{2,1,0:T(8,128)}, f32[256,256]{1,0:T(8,128)}), (f32[2,128,256]{2,1,0:T(8,128)}, f32[256,256]{1,0:T(8,128)})) %all-reduce.17.cloned.1.call-update) | async-done | bytes 524304 | tf_op jit(solution)/shard_map/psum | solution.py:71
  784.7 8.0 fusion.85
  792.7 4.5 fusion.21
  801.8 93.9 %all-reduce.15.cloned.1.call-done = f32[2,128,256]{2,1,0:T(8,128)} async-done(((f32[2,128,256]{2,1,0:T(8,128)}), f32[2,128,256]{2,1,0:T(8,128)}) %all-reduce.15.cloned.1.call-update) | async-done | bytes 262160 | tf_op jit(solution)/shard_map/psum | solution.py:71
  (103 shorter events, 59.5 us)
Async XLA Ops:
  7.2 62.8 %all-gather.3.cloned.1.call-start = ((), (), s32[]{:S(2)}) async-start(), calls=%async_computation | async-start | bytes 8912896 | tf_op jit(solution)/shard_map/all_gather | solution.py:103
  7.9 203.1 %all-reduce.19.cloned.1.call-start = ((), (), s32[]{:S(2)}) async-start(), calls=%async_computation.7 | async-start | bytes 1572864 | tf_op jit(solution)/shard_map/psum | solution.py:67
  10.6 3.9 copy-start.10
  76.1 8.0 copy-start
  76.1 8.0 copy-start.7
  97.2 113.9 %copy-start.6 = (f32[512,256]{1,0:T(8,128)S(1)}, f32[512,256]{1,0:T(8,128)}, u32[]{:S(2)}) copy-start(f32[512,256]{1,0:T(8,128)} %param.11) | copy-start | bytes 1572868
  102.0 241.1 %all-reduce.9.cloned.1.call-start = ((), (), s32[]{:S(2)}) async-start(), calls=%async_computation.1 | async-start | bytes 1048576 | tf_op jit(solution)/shard_map/psum | solution.py:67
  215.5 8.0 copy-start.1
  228.1 115.0 %copy-start.11 = (f32[256,256]{1,0:T(8,128)S(1)}, f32[256,256]{1,0:T(8,128)}, u32[]{:S(2)}) copy-start(f32[256,256]{1,0:T(8,128)} %get-tuple-element.9) | copy-start | bytes 786436
  233.0 242.6 %all-reduce.11.cloned.1.call-start = ((), (), s32[]{:S(2)}) async-start(), calls=%async_computation.2 | async-start | bytes 1048576 | tf_op jit(solution)/shard_map/psum | solution.py:67
  348.1 8.0 copy-start.2
  360.7 117.7 %copy-start.13 = (s32[1,1,16,2]{2,3,1,0:T(2,128)S(1)}, s32[1,1,16,2]{2,3,1,0:T(2,128)}, u32[]{:S(2)}) copy-start(s32[1,1,16,2]{2,3,1,0:T(2,128)} %param.16) | copy-start | bytes 388
  360.7 118.0 %copy-start.14 = (s32[1,1,16,2]{2,3,1,0:T(2,128)S(1)}, s32[1,1,16,2]{2,3,1,0:T(2,128)}, u32[]{:S(2)}) copy-start(s32[1,1,16,2]{2,3,1,0:T(2,128)} %param.17) | copy-start | bytes 388
  360.7 118.2 %copy-start.15 = (s32[1,1,16]{2,1,0:T(1,128)S(1)}, s32[1,1,16]{2,1,0:T(1,128)}, u32[]{:S(2)}) copy-start(s32[1,1,16]{2,1,0:T(1,128)} %param.18) | copy-start | bytes 196
  365.6 189.3 %all-gather.5.cloned.1.call-start = ((), (), s32[]{:S(2)}) async-start(), calls=%async_computation.3 | async-start | bytes 8912896 | tf_op jit(solution)/shard_map/all_gather | solution.py:133
  478.3 185.9 %all-reduce.13.cloned.1.call-start = ((), (), s32[]{:S(2)}) async-start(), calls=%async_computation.4 | async-start | bytes 524288 | tf_op jit(solution)/shard_map/psum | solution.py:71
  554.9 6.2 copy-start.8
  566.7 5.1 copy-start.9
  571.3 208.8 %all-reduce.17.cloned.1.call-start = ((), (), s32[]{:S(2)}) async-start(), calls=%async_computation.6 | async-start | bytes 1048576 | tf_op jit(solution)/shard_map/psum | solution.py:71
  668.0 8.0 copy-start.3
  680.5 99.6 %copy-start.5 = (f32[2,128,256]{2,1,0:T(8,128)S(1)}, f32[2,128,256]{2,1,0:T(8,128)}, u32[]{:S(2)}) copy-start(f32[2,128,256]{2,1,0:T(8,128)} %all-reduce.13.cloned.1.call-done) | copy-start | bytes 786436
  685.2 210.5 %all-reduce.15.cloned.1.call-start = ((), (), s32[]{:S(2)}) async-start(), calls=%async_computation.5 | async-start | bytes 524288 | tf_op jit(solution)/shard_map/psum | solution.py:71
  784.7 8.0 copy-start.4
  797.2 98.5 %copy-start.12 = (f32[256,256]{1,0:T(8,128)S(1)}, f32[256,256]{1,0:T(8,128)}, u32[]{:S(2)}) copy-start(f32[256,256]{1,0:T(8,128)} %get-tuple-element.7) | copy-start | bytes 786436
Sparse Core Ops, SparseCore 0:
  9.8 60.1 all-gather.2
  102.1 108.8 all-reduce.18
  233.1 109.9 all-reduce.8
  365.8 109.7 all-reduce.10
  478.7 76.1 all-gather.4
  571.4 92.7 all-reduce.12
  685.3 94.6 all-reduce.16
  801.9 93.7 all-reduce.14
where the time goes:
time: 914 us; the launch traced here: 905 us
  waiting for transfers between devices  738 us (81%)
  matrix products  112 us (12%)
  local copies, waits for them, and re-layouts  33.9 us (4%)
  between operations  14.7 us (2%)
    psum x3, waiting for transfers between devices, user_total(): return lax.psum(partial_value, 'user')  329 us
    psum x3, waiting for transfers between devices, item_total(): return lax.psum(partial_value, 'item')  279 us
    all_gather x1, waiting for transfers between devices, shards(): whole_items = lax.all_gather(new_items, 'item', axis=0, tiled=True)  75.9 us
    all_gather x1, waiting for transfers between devices, shards(): whole_users = lax.all_gather(user_factors, 'user', axis=0, tiled=True)  53.8 us
    dot_general x3, matrix products, item_terms(): jnp.einsum('tuk,tik->tui', factors, picked, precision=highest) * weights  24 us
  transfers between devices with their start and end apart: 8, of which 8 were waited for; matrix products, arithmetic and copies ran while one was open for 1% of the time, Pallas kernels for 0%

commit v1 on v0

v1 whole, which is shorter than its diff:
```python
import functools

import jax
import jax.numpy as jnp
from jax import lax
from jax.experimental import pallas as pl
from jax.experimental.pallas import tpu as pltpu
from jax.sharding import PartitionSpec as P

ITERS = 2
LAM = 1.0
EPS = 1e-6
BL = 128
SUB = 8
VMEM = 56 * 1024 * 1024

i32 = jnp.int32
f32 = jnp.float32
bf16 = jnp.bfloat16


def params():
    return pltpu.CompilerParams(vmem_limit_bytes=VMEM)


def vspec():
    return pl.BlockSpec(memory_space=pltpu.VMEM)


def power_of_two(exponent):
    bits = exponent + 126
    value = jnp.full(exponent.shape, 2.0**-126, f32)
    for k, power in enumerate((1, 2, 4, 8, 16, 32, 64)):
        value = value * jnp.where((bits >> k) & 1 == 1, f32(2.0**power), f32(1.0))
    high = jnp.where(bits >= 128, f32(2.0**64), f32(1.0))
    return value * high * high


def column_exponents(peak):
    rest = jnp.clip(peak, 2.0**-45, 2.0**60) * f32(2.0**60)
    found = jnp.zeros(peak.shape, i32)
    for k in (64, 32, 16, 8, 4, 2, 1):
        big = rest >= f32(2.0**k)
        rest = jnp.where(big, rest * f32(2.0**-k), rest)
        found = found + jnp.where(big, k, 0)
    return found - 74


def fixed_point(rows, inverse_step):
    return jnp.clip(jnp.round(rows * inverse_step), -32767.0, 32767.0).astype(i32)


def pack_users_kernel(rows_ref, out_ref):
    half = rows_ref.shape[0] // 2
    rows = rows_ref[...]
    exponent = column_exponents(jnp.max(jnp.abs(rows), axis=0, keepdims=True))
    inverse = power_of_two(-exponent)
    upper = fixed_point(rows_ref[:half, :], inverse)
    lower = fixed_point(rows_ref[half:, :], inverse)
    out_ref[:half, :] = (upper << 16) | (lower & 0xFFFF)
    out_ref[half:, :] = jnp.broadcast_to(exponent, (8, rows.shape[1]))


def pack_users(rows):
    half = rows.shape[0] // 2
    return pl.pallas_call(
        pack_users_kernel,
        out_shape=jax.ShapeDtypeStruct((half + 8, rows.shape[1]), i32),
        in_specs=[vspec()],
        out_specs=vspec(),
        name="pack_users",
    )(rows)


def pack_items_kernel(rows_ref, out_ref):
    peers, rows, rank = rows_ref.shape
    blocks = rows // SUB
    peak = jnp.max(jnp.max(jnp.abs(rows_ref[...]), axis=0), axis=0, keepdims=True)
    exponent = column_exponents(peak)
    inverse = power_of_two(-exponent)
    for b in range(blocks):
        for z in range(0, peers, 2):
            pair = jnp.concatenate(
                [rows_ref[z, b * SUB : (b + 1) * SUB, :], rows_ref[z + 1, b * SUB : (b + 1) * SUB, :]], axis=0
            )
            start = (b * peers + z) * SUB
            out_ref[start : start + 2 * SUB, :] = fixed_point(pair, inverse).astype(jnp.int16)
    out_ref[peers * rows :, :] = jnp.broadcast_to(exponent, (16, rank)).astype(jnp.int16)


def pack_items(rows):
    peers, count, rank = rows.shape
    return pl.pallas_call(
        pack_items_kernel,
        out_shape=jax.ShapeDtypeStruct((peers * count + 16, rank), jnp.int16),
        in_specs=[vspec()],
        out_specs=vspec(),
        name="pack_items",
    )(rows)


def dense_kernel(blocks, slots, codes_ref, strips_ref, ones_ref, right_ref, sums_ref, live_ref):
    sources = strips_ref.shape[0]
    sums_ref[...] = jnp.zeros_like(sums_ref)

    def clear(b, carry):
        live_ref[b] = 0
        return carry

    lax.fori_loop(0, blocks + 1, clear, 0)

    def add(s, carry):
        for pair in range(slots // 2):
            two = strips_ref[s, pair * 2 * SUB : (pair + 1) * 2 * SUB, :].astype(f32)
            for k in range(2):
                code = codes_ref[s * slots + pair * 2 + k]
                sums_ref[code] += two[k * SUB : (k + 1) * SUB, :]
                live_ref[code] = live_ref[code] + 1
        return carry

    lax.fori_loop(0, sources, add, 0)

    def finish(b, carry):
        total = sums_ref[b]
        ones_ref[b] = total + 1.0
        right_ref[b] = total + live_ref[b].astype(f32)
        return carry

    lax.fori_loop(0, blocks, finish, 0)


def dense(codes, strips, blocks, slots, name):
    shape = jax.ShapeDtypeStruct((blocks, SUB, BL), f32)
    return pl.pallas_call(
        functools.partial(dense_kernel, blocks, slots),
        out_shape=(shape, shape),
        in_specs=[pl.BlockSpec(memory_space=pltpu.SMEM), vspec()],
        out_specs=(vspec(), vspec()),
        scratch_shapes=[pltpu.VMEM((blocks + 1, SUB, BL), f32), pltpu.SMEM((blocks + 1,), i32)],
        compiler_params=params(),
        cost_estimate=pl.CostEstimate(flops=10**6, bytes_accessed=3 * 10**6, transcendentals=0),
        name=name,
    )(codes, strips)


NT = (((1,), (1,)), ((), ()))
NN = (((1,), (0,)), ((), ()))


def two_planes(value):
    upper = value.astype(bf16)
    return jnp.concatenate([upper, (value - upper.astype(f32)).astype(bf16)], axis=0)


def fold(both):
    rows = both.shape[0] // 2
    return both[:rows] + both[rows:]


def scores(direction, upper, lower):
    return fold(
        lax.dot_general(direction, upper, NT, preferred_element_type=f32)
        + lax.dot_general(direction, lower, NT, preferred_element_type=f32)
    )


def combine(weighted, upper, lower):
    planes = two_planes(weighted)
    return lax.dot_general(planes, upper, NN, preferred_element_type=f32) + lax.dot_general(
        planes, lower, NN, preferred_element_type=f32
    )


def pair_of(ref, t):
    return jnp.concatenate([ref[2 * t], ref[2 * t + 1]], axis=1)


def store_planes(upper_ref, lower_ref, start, codes, step, step256):
    count = codes.shape[0]
    rows = pl.ds(pl.multiple_of(start, count), count)
    upper = (codes + 128) >> 8
    upper_ref[rows, :] = (upper.astype(f32) * step256).astype(bf16)
    lower_ref[rows, :] = ((codes - (upper << 8)).astype(f32) * step).astype(bf16)


def iterate(ones_ref, upper_ref, lower_ref, residual, start):
    chunks = upper_ref.shape[0] // (2 * BL)
    rows, rank = residual.shape

    def operator(direction):
        planes = two_planes(direction)

        def chunk(t, total):
            span = pl.ds(pl.multiple_of(t * 2 * BL, 2 * BL), 2 * BL)
            upper, lower = upper_ref[span, :], lower_ref[span, :]
            weighted = pair_of(ones_ref, t) * scores(planes, upper, lower)
            return total + combine(weighted, upper, lower)

        total = lax.fori_loop(0, chunks, chunk, jnp.zeros((2 * rows, rank), f32), unroll=4)
        return fold(total) + LAM * direction

    solution = start
    direction = residual
    norm_now = jnp.sum(residual * residual, axis=-1, keepdims=True)
    for iteration in range(ITERS):
        image = operator(direction)
        alpha = norm_now / (jnp.sum(direction * image, axis=-1, keepdims=True) + EPS)
        solution = solution + alpha * direction
        if iteration + 1 < ITERS:
            residual = residual - alpha * image
            norm_next = jnp.sum(residual * residual, axis=-1, keepdims=True)
            direction = residual + norm_next / (norm_now + EPS) * direction
            norm_now = norm_next
    return solution


def item_kernel(start_ref, ones_ref, right_ref, words_ref, out_ref, upper_ref, lower_ref, total_ref):
    source = pl.program_id(0)
    half = words_ref.shape[1] - 8
    per = half // (2 * BL)
    exponent = words_ref[0, half : half + 1, :]
    step = power_of_two(exponent)
    step256 = step * 256.0
    base = source * 2 * half
    planes = two_planes(start_ref[...])

    @pl.when(source == 0)
    def _():
        total_ref[...] = jnp.zeros_like(total_ref)

    for c in range(per):
        words = words_ref[0, c * 2 * BL : (c + 1) * 2 * BL, :]
        store_planes(upper_ref, lower_ref, base + c * 2 * BL, words >> 16, step, step256)
        store_planes(upper_ref, lower_ref, base + half + c * 2 * BL, (words << 16) >> 16, step, step256)
    for c in range(2 * per):
        t = source * 2 * per + c
        span = pl.ds(pl.multiple_of(base + c * 2 * BL, 2 * BL), 2 * BL)
        upper, lower = upper_ref[span, :], lower_ref[span, :]
        weighted = pair_of(right_ref, t) - pair_of(ones_ref, t) * scores(planes, upper, lower)
        total_ref[...] += combine(weighted, upper, lower)

    @pl.when(source == pl.num_programs(0) - 1)
    def _():
        start = start_ref[...]
        residual = fold(total_ref[...]) - LAM * start
        out_ref[...] = iterate(ones_ref, upper_ref, lower_ref, residual, start)


def solve_items(start, ones, right, words):
    sources, depth, rank = words.shape
    rows = start.shape[0]
    whole = 2 * (depth - 8) * sources
    ones = ones.reshape(-1, rows, BL)
    right = right.reshape(-1, rows, BL)
    fixed3 = pl.BlockSpec(ones.shape, lambda s: (0, 0, 0), pipeline_mode=pl.Buffered(1))
    return pl.pallas_call(
        item_kernel,
        grid=(sources,),
        out_shape=jax.ShapeDtypeStruct((rows, rank), f32),
        in_specs=[
            pl.BlockSpec((rows, rank), lambda s: (0, 0)),
            fixed3,
            fixed3,
            pl.BlockSpec((1, depth, rank), lambda s: (s, 0, 0)),
        ],
        out_specs=pl.BlockSpec((rows, rank), lambda s: (0, 0)),
        scratch_shapes=[
            pltpu.VMEM((whole, rank), bf16),
            pltpu.VMEM((whole, rank), bf16),
            pltpu.VMEM((2 * rows, rank), f32),
        ],
        compiler_params=params(),
        name="solve_items",
    )(start, ones, right, words)


def held_kernel(
    core_ref, ones_ref, right_ref, own_ref, other_ref, out_ref, upper_ref, lower_ref, total_ref
):
    source = pl.program_id(0)
    half = own_ref.shape[1] - 16
    lanes = BL // 2
    blocks = half // lanes
    core = core_ref[0]

    @pl.when(source == 0)
    def _():
        total_ref[...] = jnp.zeros_like(total_ref)

    for ref, which in ((own_ref, core), (other_ref, 1 - core)):
        exponent = ref[0, half : half + 16, :].astype(i32)[:1]
        step = power_of_two(exponent)
        step256 = step * 256.0
        for b in range(blocks):
            codes = ref[0, b * lanes : (b + 1) * lanes, :].astype(i32)
            start = (source * blocks + b) * BL + which * lanes
            store_planes(upper_ref, lower_ref, start, codes, step, step256)
    for c in range(blocks // 2):
        t = source * (blocks // 2) + c
        span = pl.ds(pl.multiple_of(t * 2 * BL, 2 * BL), 2 * BL)
        total_ref[...] += combine(pair_of(right_ref, t), upper_ref[span, :], lower_ref[span, :])

    @pl.when(source == pl.num_programs(0) - 1)
    def _():
        residual = fold(total_ref[...])
        out_ref[...] = iterate(ones_ref, upper_ref, lower_ref, residual, jnp.zeros_like(residual))


def solve_held(core, ones, right, own, other, rows):
    sources, depth, rank = own.shape
    whole = 2 * (depth - 16) * sources
    ones = ones.reshape(-1, rows, BL)
    right = right.reshape(-1, rows, BL)
    fixed3 = pl.BlockSpec(ones.shape, lambda s: (0, 0, 0), pipeline_mode=pl.Buffered(1))
    codes = pl.BlockSpec((1, depth, rank), lambda s: (s, 0, 0))
    return pl.pallas_call(
        held_kernel,
        grid=(sources,),
        out_shape=jax.ShapeDtypeStruct((rows, rank), f32),
        in_specs=[pl.BlockSpec(memory_space=pltpu.SMEM), fixed3, fixed3, codes, codes],
        out_specs=pl.BlockSpec((rows, rank), lambda s: (0, 0)),
        scratch_shapes=[
            pltpu.VMEM((whole, rank), bf16),
            pltpu.VMEM((whole, rank), bf16),
            pltpu.VMEM((2 * rows, rank), f32),
        ],
        compiler_params=params(),
        name="solve_held",
    )(core, ones, right, own, other)


def with_codes(strips, codes):
    peers, _, lanes = strips.shape
    row = jnp.pad(codes.reshape(1, 1, -1), ((0, 0), (0, 15), (0, lanes - codes.size)))
    return jnp.concatenate([strips, jnp.broadcast_to(row.astype(bf16), (peers, 16, lanes))], axis=1)


def codes_of(received, slots):
    return received[:, -16, :slots].astype(i32).reshape(-1)


def shards(
    user_factors,
    item_factors,
    tile_user,
    tile_item,
    tile_count,
    tile_conf,
    held_user,
    held_item,
    held_count,
    held_conf,
):
    rank = user_factors.shape[1]
    peers = lax.axis_size("user")
    item_peers = lax.axis_size("item")
    chips = peers // 2
    me = lax.axis_index("user")
    core = me % 2
    chip = me // 2
    slots = tile_user.shape[-1]
    held_slots = held_user.shape[-1]
    user_blocks = user_factors.shape[0] // BL
    item_blocks = item_factors.shape[0] // BL
    held_blocks = 2

    words = lax.all_gather(pack_users(user_factors), "user", axis=0, tiled=False)

    live = jnp.arange(slots, dtype=i32)[None, :] < tile_count[0, 0][:, None]
    owner = jnp.arange(peers, dtype=i32)[:, None] * user_blocks
    code = jnp.where(live, (owner + tile_user[0, 0]) * item_blocks + tile_item[0, 0], peers * user_blocks * item_blocks)
    strips = tile_conf[0, 0].reshape(peers * slots, BL, 2, chips, SUB).transpose(3, 2, 0, 4, 1)
    strips = with_codes(strips.reshape(peers, peers * slots * SUB, BL), code)
    strips = lax.all_to_all(strips, "user", 0, 0, tiled=True)
    ones, right = dense(
        codes_of(strips, peers * slots), strips, peers * user_blocks * item_blocks, peers * slots, "dense_items"
    )

    held_live = jnp.arange(held_slots, dtype=i32)[None, :] < held_count[0, 0][:, None]
    held_owner = jnp.arange(item_peers, dtype=i32)[:, None] * item_blocks
    held_code = jnp.where(
        held_live, (held_owner + held_item[0, 0]) * held_blocks + held_user[0, 0], item_peers * item_blocks * held_blocks
    )
    held_strips = held_conf[0, 0].reshape(item_peers * held_slots, item_peers, SUB, BL).transpose(1, 0, 2, 3)
    held_strips = with_codes(held_strips.reshape(item_peers, item_peers * held_slots * SUB, BL), held_code)
    held_strips = lax.all_to_all(held_strips, "item", 0, 0, tiled=True)
    held_ones, held_right = dense(
        codes_of(held_strips, item_peers * held_slots),
        held_strips,
        item_peers * item_blocks * held_blocks,
        item_peers * held_slots,
        "dense_held",
    )

    start = lax.dynamic_slice_in_dim(
        item_factors.reshape(item_blocks, peers, SUB, rank), core * chips + chip, 1, axis=1
    ).reshape(item_blocks * SUB, rank)
    mine = solve_items(start, ones, right, words)

    same_core = [[c + 2 * z for z in range(chips)] for c in range(2)]
    siblings = [(d, d ^ 1) for d in range(peers)]
    half = lax.all_to_all(
        jnp.broadcast_to(mine[None], (chips,) + mine.shape), "user", 0, 0, tiled=True, axis_index_groups=same_core
    )
    own = lax.all_gather(pack_items(half), "item", axis=0, tiled=False)
    other = lax.ppermute(own, "user", siblings)
    folded = solve_held(core.reshape(1), held_ones, held_right, own, other, held_blocks * SUB)
    folded = lax.all_to_all(
        jnp.broadcast_to(folded[None], (item_peers,) + folded.shape), "item", 0, 0, tiled=True
    )
    folded = folded.reshape(item_peers, held_blocks, SUB, rank).transpose(1, 0, 2, 3).reshape(-1, rank)

    half = half.reshape(chips, item_blocks, SUB, rank).transpose(1, 0, 2, 3).reshape(item_blocks, 1, BL // 2, rank)
    sibling = lax.ppermute(half, "user", siblings)
    new_items = jnp.where(
        core == 0, jnp.concatenate([half, sibling], axis=1), jnp.concatenate([sibling, half], axis=1)
    ).reshape(-1, rank)
    return new_items, folded


def solution(mesh):
    in_specs = (
        P("user", None),
        P("item", None),
        P("item", "user", None, None),
        P("item", "user", None, None),
        P("item", "user", None),
        P("item", "user", None, None, None, None),
        P("user", "item", None, None),
        P("user", "item", None, None),
        P("user", "item", None),
        P("user", "item", None, None, None, None),
    )
    out_specs = (P("item", None), P("user", None))
    return jax.shard_map(shards, mesh=mesh, in_specs=in_specs, out_specs=out_specs, check_vma=False)
```

time: 914 us -> 221 us (0.24)
  waiting for transfers between devices: 738 us -> 48.8 us
  matrix products: 112 us -> 0 us
  Pallas kernels: 0 us -> 77.1 us
  blocking collectives: 0 us -> 36.9 us
  starting transfers between devices: 1.2 us -> 29.9 us
  local copies, waits for them, and re-layouts: 33.9 us -> 10.7 us
    psum x6 -> x0, waiting for transfers between devices: 608 us -> none  [the longest x3 329 us: user_total(): return lax.psum(partial_value, 'user')]
    all_gather x2 -> x1, waiting for transfers between devices: 130 us -> 0.01 us  [shards(): lax.all_gather(pack_users(user_factors), 'user', axis=0, tiled=False)]
    dot_general x26 -> x0, matrix products: 112 us -> none  [the longest x3 24 us: item_terms(): jnp.einsum('tuk,tik->tui', factors, picked, precision=highest) * weights]
    pallas_call x0 -> x6, Pallas kernels: none -> 77.1 us  [the longest x1 32.3 us: solve_items(): pl.pallas_call(item_kernel, grid=(sources,), out_shape=jax.ShapeDtypeStru...]
    all_to_all x0 -> x3, waiting for transfers between devices: none -> 48.8 us  [the longest x1 28 us: shards(): strips = lax.all_to_all(strips, 'user', 0, 0, tiled=True)]
    gather x7 -> x0, local copies, waits for them, and re-layouts: 28.2 us -> none  [the longest x3 9.36 us: item_terms(): picked = vector[positions]]
    all_to_all x0 -> x3, starting transfers between devices: none -> 22.5 us  [the longest x1 11.2 us: shards(): strips = lax.all_to_all(strips, 'user', 0, 0, tiled=True)]
    all_gather x0 -> x1, blocking collectives: none -> 21.8 us  [shards(): own = lax.all_gather(pack_items(half), 'item', axis=0, tiled=False)]
  transfers between devices with their start and end apart: 8 -> 6, of which waited for: 8 -> 3; matrix products, arithmetic and copies ran while one was open for 1% -> 5% of each run, Pallas kernels for 0% -> 19%
where the time goes in v1:
time: 221 us; the launch traced here: 220 us
  Pallas kernels  77.1 us (35%)
  waiting for transfers between devices  48.8 us (22%)
  blocking collectives  36.9 us (17%)
  starting transfers between devices  29.9 us (14%)
  between operations  14.3 us (6%)
  local copies, waits for them, and re-layouts  10.7 us (5%)
  other arithmetic  2.44 us (1%)
    pallas_call x1, Pallas kernels, solve_items(): pl.pallas_call(item_kernel, grid=(sources,), out_shape=jax.ShapeDtypeStru...  32.3 us
    all_to_all x1, waiting for transfers between devices, shards(): strips = lax.all_to_all(strips, 'user', 0, 0, tiled=True)  28 us
    pallas_call x1, Pallas kernels, solve_held(): pl.pallas_call(held_kernel, grid=(sources,), out_shape=jax.ShapeDtypeStru...  26.4 us
    all_gather x1, blocking collectives, shards(): own = lax.all_gather(pack_items(half), 'item', axis=0, tiled=False)  21.8 us
    all_to_all x1, blocking collectives, shards(): lax.all_to_all(jnp.broadcast_to(mine[None], (chips,) + mine.shape), 'user...  15.1 us
    pallas_call x2, Pallas kernels, dense(): pl.pallas_call(functools.partial(dense_kernel, blocks, slots), out_shape=...  14.7 us
    all_to_all x1, waiting for transfers between devices, shards(): held_strips = lax.all_to_all(held_strips, 'item', 0, 0, tiled=True)  13.7 us
    all_to_all x1, starting transfers between devices, shards(): strips = lax.all_to_all(strips, 'user', 0, 0, tiled=True)  11.2 us
  transfers between devices with their start and end apart: 6, of which 3 were waited for; matrix products, arithmetic and copies ran while one was open for 5% of the time, Pallas kernels for 19%

profile of v1, /device:TPU:1, one launch (start us, length us, event | category | flops | bytes accessed | tf_op | source)
XLA Modules:
  0.0 220.2 jit_solution(15982798144374282162)
XLA Ops:
  7.3 2.0 pack_users.1
  9.5 0.8 copy.31
  10.3 0.8 copy.32
  12.2 1.1 pad_maximum_fusion.1
  13.3 7.6 %all-to-all-start.2 = ((bf16[16,272,128]{2,1,0:T(8,128)(2,1)}), bf16[16,272,128]{2,1,0:T(8,128)(2,1)S(1)}, u32[]{:S(2)}, u32[]{:S(2)}) async-start(bf16[16,272,128]{2,1,0:T(8,128)(2,1)} %pad_maximum_fusion.1), calls=%async_computation.2 | async-start | bytes 2228224 | tf_op jit(solution)/shard_map/all_to_all | solution.py:386
  20.9 1.6 copy.29
  22.9 1.1 pad_maximum_fusion
  24.0 13.7 %all-to-all-done.2.strips_ref = bf16[16,272,128]{2,1,0:T(8,128)(2,1)S(1)} async-done(((bf16[16,272,128]{2,1,0:T(8,128)(2,1)}), bf16[16,272,128]{2,1,0:T(8,128)(2,1)S(1)}, u32[]{:S(2)}, u32[]{:S(2)}) %all-to-all-start.2) | async-done | bytes 1114144 | tf_op jit(solution)/shard_map/all_to_all | solution.py:386
  37.6 11.2 %all-to-all-start = ((bf16[16,272,128]{2,1,0:T(8,128)(2,1)}), bf16[16,272,128]{2,1,0:T(8,128)(2,1)S(1)}, u32[]{:S(2)}, u32[]{:S(2)}) async-start(bf16[16,272,128]{2,1,0:T(8,128)(2,1)} %pad_maximum_fusion), calls=%async_computation | async-start | bytes 2228224 | tf_op jit(solution)/shard_map/all_to_all | solution.py:374
  49.4 28.0 %all-to-all-done.strips_ref = bf16[16,272,128]{2,1,0:T(8,128)(2,1)S(1)} async-done(((bf16[16,272,128]{2,1,0:T(8,128)(2,1)}), bf16[16,272,128]{2,1,0:T(8,128)(2,1)S(1)}, u32[]{:S(2)}, u32[]{:S(2)}) %all-to-all-start) | async-done | bytes 1114144 | tf_op jit(solution)/shard_map/all_to_all | solution.py:374
  77.5 0.7 reshape.194.codes_ref
  78.5 8.4 %dense_items.1 = (f32[256,8,128]{2,1,0:T(8,128)}, f32[256,8,128]{2,1,0:T(8,128)}) custom-call(s32[512]{0:T(512)} %reshape.194.codes_ref, bf16[16,272,128]{2,1,0:T(8,128)(2,1)} %copy-done.3), custom_call_target="tpu_custom_call" | custom-call | flops 1000000 | bytes 3000000 | tf_op jit(solution)/shard_map/dense_items/pallas_call | solution.py:134
  86.9 32.3 %solve_items.1 = f32[32,256]{1,0:T(8,128)} custom-call(f32[32,256]{1,0:T(8,128)} %dynamic-slice_bitcast_fusion.start_ref, f32[64,32,128]{2,1,0:T(8,128)} %bitcast.55, f32[64,32,128]{2,1,0:T(8,128)} %bitcast.56, s32[16,264,256]{2,1,0:T(8,128)} %bitcast.51), custom_call_target="tpu_custom_call" | custom-call | tf_op jit(solution)/shard_map/solve_items/pallas_call | solution.py:256
  119.2 0.8 broadcast_in_dim.40
  120.0 15.1 %all_to_all.20.rows_ref = f32[8,32,256]{2,1,0:T(8,128)} all-to-all(f32[8,32,256]{2,1,0:T(8,128)S(1)} %broadcast_in_dim.40), channel_id=1, replica_groups={{0,32,64,96,128,160,192,224},{16,48,80,112,144,176,208,240},{1,33,65,97..., dimensions={0} | all-to-all | bytes 524288 | tf_op jit(solution)/shard_map/all_to_all | solution.py:402
  135.1 1.7 pack_items.1
  136.8 21.8 %all-gather.6 = s16[4352,256]{1,0:T(8,128)(2,1)S(1)} all-gather(s16[272,256]{1,0:T(8,128)(2,1)} %pack_items.1), channel_id=3, replica_groups=mesh['user'=16,'item'=16] {'item'}, dimensions={0}, use_global_device_ids=true | all-gather | bytes 2367488 | tf_op jit(solution)/shard_map/all_gather | solution.py:405
  158.6 7.2 %collective-permute-start.1 = (s16[16,272,256]{2,1,0:T(8,128)(2,1)S(1)}, s16[16,272,256]{2,1,0:T(8,128)(2,1)}, u32[]{:S(2)}, u32[]{:S(2)}) collective-permute-start(s16[16,272,256]{2,1,0:T(8,128)(2,1)S(1)} %bitcast.49), channel_id=1, source_target_pairs={{0,16},{16,0},{32,48},{48,32},{64,80},{80,64},{96,112},{112,96},{1... | collective-permute-start | bytes 6684680 | tf_op jit(solution)/shard_map/ppermute | solution.py:406
  166.6 6.3 %dense_held.1 = (f32[128,8,128]{2,1,0:T(8,128)}, f32[128,8,128]{2,1,0:T(8,128)}) custom-call(s32[512]{0:T(512)} %reshape.195.codes_ref, bf16[16,272,128]{2,1,0:T(8,128)(2,1)} %copy-done.2), custom_call_target="tpu_custom_call" | custom-call | flops 1000000 | bytes 3000000 | tf_op jit(solution)/shard_map/dense_held/pallas_call | solution.py:134
  173.0 26.4 %solve_held.1 = f32[16,256]{1,0:T(8,128)} custom-call(s32[1]{0:T(128)} %bitcast.15.core_ref, f32[64,16,128]{2,1,0:T(8,128)} %bitcast.60, f32[64,16,128]{2,1,0:T(8,128)} %bitcast.61, s16[16,272,256]{2,1,0:T(8,128)(2,1)} %bitcast.50, s16[16,272,256]{2,1,0:T(8,128)(2,1)} %collective-permute-done.1.other_ref), custom_call_target="tpu_custom_call" | custom-call | tf_op jit(solution)/shard_map/solve_held/pallas_call | solution.py:316
  199.4 1.4 broadcast_in_dim.44
  200.8 3.8 %all-to-all-start.3 = ((f32[16,16,256]{2,1,0:T(8,128)}), f32[16,16,256]{2,1,0:T(8,128)S(1)}, u32[]{:S(2)}, u32[]{:S(2)}) async-start(f32[16,16,256]{2,1,0:T(8,128)} %broadcast_in_dim.44), calls=%async_computation.3 | async-start | bytes 524288 | tf_op jit(solution)/shard_map/all_to_all | solution.py:408
  204.7 0.8 copy.34
  205.5 7.1 %all-to-all-done.3 = f32[16,16,256]{2,1,0:T(8,128)S(1)} async-done(((f32[16,16,256]{2,1,0:T(8,128)}), f32[16,16,256]{2,1,0:T(8,128)S(1)}, u32[]{:S(2)}, u32[]{:S(2)}) %all-to-all-start.3) | async-done | bytes 262176 | tf_op jit(solution)/shard_map/all_to_all | solution.py:408
  (52 shorter events, 4.2 us)
Async XLA Ops:
  7.2 41.6 %copy-start = (f32[512,256]{1,0:T(8,128)S(1)}, f32[512,256]{1,0:T(8,128)}, u32[]{:S(2)}) copy-start(f32[512,256]{1,0:T(8,128)} %param.11) | copy-start | bytes 1572868
  7.2 4.0 %copy-start.6 = (s32[1,1,16,2]{2,3,1,0:T(2,128)S(1)}, s32[1,1,16,2]{2,3,1,0:T(2,128)}, u32[]{:S(2)}) copy-start(s32[1,1,16,2]{2,3,1,0:T(2,128)} %param.17) | copy-start | bytes 388
  7.2 4.2 %copy-start.7 = (s32[1,1,16,2]{2,3,1,0:T(2,128)S(1)}, s32[1,1,16,2]{2,3,1,0:T(2,128)}, u32[]{:S(2)}) copy-start(s32[1,1,16,2]{2,3,1,0:T(2,128)} %param.16) | copy-start | bytes 388
  7.2 4.3 %copy-start.8 = (s32[1,1,16]{2,1,0:T(1,128)S(1)}, s32[1,1,16]{2,1,0:T(1,128)}, u32[]{:S(2)}) copy-start(s32[1,1,16]{2,1,0:T(1,128)} %param.14) | copy-start | bytes 196
  7.2 4.5 %copy-start.9 = (s32[1,1,16]{2,1,0:T(1,128)S(1)}, s32[1,1,16]{2,1,0:T(1,128)}, u32[]{:S(2)}) copy-start(s32[1,1,16]{2,1,0:T(1,128)} %param.18) | copy-start | bytes 196
  7.2 4.7 %copy-start.5 = (bf16[1,1,16,2,128,128]{5,4,3,2,1,0:T(8,128)(2,1)S(1)}, bf16[1,1,16,2,128,128]{5,4,3,2,1,0:T(8,128)(2,1)}, u32[]{:S(2)}) copy-start(bf16[1,1,16,2,128,128]{5,4,3,2,1,0:T(8,128)(2,1)} %param.19) | copy-start | bytes 3145732
  7.2 79.7 %all-gather.5.cloned.1.call-start = ((), (), s32[]{:S(2)}) async-start(), calls=%async_computation.4 | async-start | bytes 4595712 | tf_op jit(solution)/shard_map/all_gather | solution.py:367
  13.3 24.3 %all-to-all-start.2 = ((bf16[16,272,128]{2,1,0:T(8,128)(2,1)}), bf16[16,272,128]{2,1,0:T(8,128)(2,1)S(1)}, u32[]{:S(2)}, u32[]{:S(2)}) async-start(bf16[16,272,128]{2,1,0:T(8,128)(2,1)} %pad_maximum_fusion.1), calls=%async_computation.2 | async-start | bytes 2228224 | tf_op jit(solution)/shard_map/all_to_all | solution.py:386
  37.6 39.8 %copy-start.2 = (bf16[16,272,128]{2,1,0:T(8,128)(2,1)}, bf16[16,272,128]{2,1,0:T(8,128)(2,1)S(1)}, u32[]{:S(2)}) copy-start(bf16[16,272,128]{2,1,0:T(8,128)(2,1)S(1)} %all-to-all-done.2.strips_ref) | copy-start | bytes 3342340
  37.6 39.8 %all-to-all-start = ((bf16[16,272,128]{2,1,0:T(8,128)(2,1)}), bf16[16,272,128]{2,1,0:T(8,128)(2,1)S(1)}, u32[]{:S(2)}, u32[]{:S(2)}) async-start(bf16[16,272,128]{2,1,0:T(8,128)(2,1)} %pad_maximum_fusion), calls=%async_computation | async-start | bytes 2228224 | tf_op jit(solution)/shard_map/all_to_all | solution.py:374
  77.4 1.1 copy-start.3
  136.8 29.0 %copy-start.4 = (f32[8,32,256]{2,1,0:T(8,128)S(1)}, f32[8,32,256]{2,1,0:T(8,128)}, u32[]{:S(2)}) copy-start(f32[8,32,256]{2,1,0:T(8,128)} %all_to_all.20.rows_ref) | copy-start | bytes 786436
  158.6 14.4 %copy-start.1 = (s16[4352,256]{1,0:T(8,128)(2,1)}, s16[4352,256]{1,0:T(8,128)(2,1)S(1)}, u32[]{:S(2)}) copy-start(s16[4352,256]{1,0:T(8,128)(2,1)S(1)} %all-gather.6) | copy-start | bytes 6684676
  158.6 14.4 %collective-permute-start.1 = (s16[16,272,256]{2,1,0:T(8,128)(2,1)S(1)}, s16[16,272,256]{2,1,0:T(8,128)(2,1)}, u32[]{:S(2)}, u32[]{:S(2)}) collective-permute-start(s16[16,272,256]{2,1,0:T(8,128)(2,1)S(1)} %bitcast.49), channel_id=1, source_target_pairs={{0,16},{16,0},{32,48},{48,32},{64,80},{80,64},{96,112},{112,96},{1... | collective-permute-start | bytes 6684680 | tf_op jit(solution)/shard_map/ppermute | solution.py:406
  165.9 38.8 %collective-permute-start = (f32[4,1,64,256]{3,2,0,1:T(8,128)S(1)}, f32[4,1,64,256]{3,2,0,1:T(8,128)S(1)}, u32[]{:S(2)}, u32[]{:S(2)}) collective-permute-start(f32[4,1,64,256]{3,2,0,1:T(8,128)S(1)} %copy_bitcast_fusion.1), channel_id=1, source_target_pairs={{0,16},{16,0},{32,48},{48,32},{64,80},{80,64},{96,112},{112,96},{1... | collective-permute-start | bytes 786440 | tf_op jit(solution)/shard_map/ppermute | solution.py:414
  200.8 11.8 %all-to-all-start.3 = ((f32[16,16,256]{2,1,0:T(8,128)}), f32[16,16,256]{2,1,0:T(8,128)S(1)}, u32[]{:S(2)}, u32[]{:S(2)}) async-start(f32[16,16,256]{2,1,0:T(8,128)} %broadcast_in_dim.44), calls=%async_computation.3 | async-start | bytes 524288 | tf_op jit(solution)/shard_map/all_to_all | solution.py:408
Sparse Core Ops, SparseCore 0:
  10.5 52.4 all-gather.4

commit v2 on v1

v2 whole, which is shorter than its diff:
```python
import functools

import jax
import jax.numpy as jnp
from jax import lax
from jax.experimental import pallas as pl
from jax.experimental.pallas import tpu as pltpu
from jax.sharding import PartitionSpec as P

ITERS = 2
LAM = 1.0
EPS = 1e-6
BL = 128
SUB = 8
VMEM = 28 * 1024 * 1024

i32 = jnp.int32
f32 = jnp.float32
bf16 = jnp.bfloat16


def params():
    return pltpu.CompilerParams(vmem_limit_bytes=VMEM)


def vspec():
    return pl.BlockSpec(memory_space=pltpu.VMEM)


def power_of_two(exponent):
    bits = exponent + 126
    value = jnp.full(exponent.shape, 2.0**-126, f32)
    for k, power in enumerate((1, 2, 4, 8, 16, 32, 64)):
        value = value * jnp.where((bits >> k) & 1 == 1, f32(2.0**power), f32(1.0))
    high = jnp.where(bits >= 128, f32(2.0**64), f32(1.0))
    return value * high * high


def column_exponents(peak):
    rest = jnp.clip(peak, 2.0**-45, 2.0**60) * f32(2.0**60)
    found = jnp.zeros(peak.shape, i32)
    for k in (64, 32, 16, 8, 4, 2, 1):
        big = rest >= f32(2.0**k)
        rest = jnp.where(big, rest * f32(2.0**-k), rest)
        found = found + jnp.where(big, k, 0)
    return found - 74


def fixed_point(rows, inverse_step):
    return jnp.clip(jnp.round(rows * inverse_step), -32767.0, 32767.0).astype(i32)


def pack_users_kernel(place_ref, rows_ref, out_ref, exponent_ref):
    exponent = column_exponents(jnp.max(jnp.abs(rows_ref[...]), axis=0, keepdims=True))
    peers, part, rank = out_ref.shape
    first = pl.multiple_of(place_ref[0] * part, part)
    codes = fixed_point(rows_ref[pl.ds(first, part), :], power_of_two(-exponent)).astype(jnp.int16)
    for z in range(peers):
        out_ref[z] = codes
    exponent_ref[...] = exponent.astype(f32)


def pack_users(rows, place, peers, part):
    rank = rows.shape[1]
    return pl.pallas_call(
        pack_users_kernel,
        out_shape=(jax.ShapeDtypeStruct((peers, part, rank), jnp.int16), jax.ShapeDtypeStruct((1, rank), f32)),
        in_specs=[pl.BlockSpec(memory_space=pltpu.SMEM), vspec()],
        out_specs=(vspec(), vspec()),
        name="pack_users",
    )(place.reshape(1), rows)


def strips_kernel(turn, order, owner_scale, slot_scale, dead, place_ref, outer_ref, inner_ref, count_ref, tiles_ref, extra_ref, out_ref):
    owners, slots = outer_ref.shape
    total = owners * slots
    for t in range(0, total, 2):
        pair = [tiles_ref[t + k].astype(f32) for k in range(2)]
        if turn:
            pair = [tile.T for tile in pair]
        for d in range(len(order)):
            q = order[d] * SUB
            both = jnp.concatenate([pair[0][q : q + SUB], pair[1][q : q + SUB]], axis=0)
            out_ref[d, t * SUB : (t + 2) * SUB, :] = both.astype(bf16)
    outer_scale, owner_scale = owner_scale
    per = BL // total
    row = lax.broadcasted_iota(i32, (16, BL), 0)
    lane = lax.broadcasted_iota(i32, (16, BL), 1)
    place = place_ref[0]
    mine = jnp.where(row == place // per, lane - lax.rem(place, per) * total, -1)
    codes = jnp.zeros((16, BL), f32)
    for o in range(owners):
        for c in range(slots):
            code = (outer_ref[o, c] * outer_scale + o * owner_scale) * slot_scale + inner_ref[o, c]
            code = jnp.where(c < count_ref[o], code, dead)
            codes = jnp.where(mine == o * slots + c, code.astype(f32), codes)
    below = owners * total // BL
    for k in range(extra_ref.shape[1] // BL):
        codes = jnp.where(row == below + k, extra_ref[:, k * BL : (k + 1) * BL], codes)
    codes = codes.astype(bf16)
    for d in range(len(order)):
        out_ref[d, total * SUB :, :] = codes


def cut_strips(place, outer, inner, count, tiles, extra, turn, order, owner_scale, slot_scale, dead, name):
    owners, slots = outer.shape
    smem = pl.BlockSpec(memory_space=pltpu.SMEM)
    return pl.pallas_call(
        functools.partial(strips_kernel, turn, order, owner_scale, slot_scale, dead),
        out_shape=jax.ShapeDtypeStruct((len(order), owners * slots * SUB + 16, BL), bf16),
        in_specs=[smem, smem, smem, smem, vspec(), vspec()],
        out_specs=vspec(),
        compiler_params=params(),
        cost_estimate=pl.CostEstimate(flops=10**6, bytes_accessed=2 * 10**6, transcendentals=0),
        name=name,
    )(place.reshape(1), outer, inner, count, tiles.reshape(-1, BL, BL), extra)


def pack_items_kernel(rows_ref, out_ref):
    peers, rows, rank = rows_ref.shape
    blocks = rows // SUB
    peak = jnp.max(jnp.max(jnp.abs(rows_ref[...]), axis=0), axis=0, keepdims=True)
    exponent = column_exponents(peak)
    inverse = power_of_two(-exponent)
    for b in range(blocks):
        for z in range(0, peers, 2):
            pair = jnp.concatenate(
                [rows_ref[z, b * SUB : (b + 1) * SUB, :], rows_ref[z + 1, b * SUB : (b + 1) * SUB, :]], axis=0
            )
            start = (b * peers + z) * SUB
            out_ref[start : start + 2 * SUB, :] = fixed_point(pair, inverse).astype(jnp.int16)
    out_ref[peers * rows :, :] = jnp.broadcast_to(exponent, (16, rank)).astype(jnp.int16)


def pack_items(rows):
    peers, count, rank = rows.shape
    return pl.pallas_call(
        pack_items_kernel,
        out_shape=jax.ShapeDtypeStruct((peers * count + 16, rank), jnp.int16),
        in_specs=[vspec()],
        out_specs=vspec(),
        name="pack_items",
    )(rows)


def dense_kernel(blocks, slots, strips_ref, ones_ref, right_ref, step_ref, wide_ref):
    sources, depth, _ = strips_ref.shape
    count = slots * SUB
    table = strips_ref[0, count:depth, :].astype(f32)
    for s in range(1, sources):
        table = table + strips_ref[s, count:depth, :].astype(f32)
    held = sources * slots // BL
    codes = jnp.concatenate([table[k : k + 1, :] for k in range(held)], axis=1).astype(i32)
    rows = [strips_ref[s, count:depth, :].astype(f32) for s in range(sources)]
    rows = [jnp.concatenate([row[held : held + 1], row[held + 1 : held + 2]], axis=1) for row in rows]
    step_ref[...] = power_of_two(jnp.concatenate(rows, axis=0).astype(i32))
    named = lax.broadcasted_iota(i32, (blocks, sources * slots), 0) == codes
    named = jnp.where(named, f32(1.0), f32(0.0))
    live = jnp.sum(named, axis=1, keepdims=True)
    named = named.astype(bf16)
    for s in range(sources):
        wide_ref[s * count : (s + 1) * count, :] = strips_ref[s, :count, :].astype(f32)
    for r in range(SUB):
        rows = wide_ref[pl.ds(r, sources * slots, stride=SUB), :].astype(bf16)
        total = jnp.dot(named, rows, preferred_element_type=f32)
        ones_ref[pl.ds(r, blocks, stride=SUB), :] = total + 1.0
        right_ref[pl.ds(r, blocks, stride=SUB), :] = total + live


def dense(strips, blocks, slots, name):
    shape = jax.ShapeDtypeStruct((blocks * SUB, BL), f32)
    return pl.pallas_call(
        functools.partial(dense_kernel, blocks, slots),
        out_shape=(shape, shape, jax.ShapeDtypeStruct((strips.shape[0], 2 * BL), f32)),
        in_specs=[vspec()],
        out_specs=(vspec(), vspec(), vspec()),
        scratch_shapes=[pltpu.VMEM((strips.shape[0] * slots * SUB, BL), f32)],
        compiler_params=params(),
        cost_estimate=pl.CostEstimate(flops=4 * 10**8, bytes_accessed=3 * 10**6, transcendentals=0),
        name=name,
    )(strips)


NT = (((1,), (1,)), ((), ()))
NN = (((1,), (0,)), ((), ()))


def two_planes(value):
    upper = value.astype(bf16)
    return jnp.concatenate([upper, (value - upper.astype(f32)).astype(bf16)], axis=0)


def fold(both):
    rows = both.shape[0] // 2
    return both[:rows] + both[rows:]


def scores(direction, upper, lower):
    return fold(
        lax.dot_general(direction, upper, NT, preferred_element_type=f32)
        + lax.dot_general(direction, lower, NT, preferred_element_type=f32)
    )


def combine(weighted, upper, lower):
    planes = two_planes(weighted)
    return lax.dot_general(planes, upper, NN, preferred_element_type=f32) + lax.dot_general(
        planes, lower, NN, preferred_element_type=f32
    )


def columns(ref, first, count):
    return jnp.concatenate([ref[first + k] for k in range(count)], axis=1)


def high_part(codes):
    return (codes & -256).astype(f32)


def low_part(codes):
    return (codes & 255).astype(f32)


def iterate(ones_ref, upper_ref, lower_ref, residual, start):
    rows, rank = residual.shape
    group = 16 * BL
    steps = upper_ref.shape[0] // group

    def part(g, planes):
        span = pl.ds(pl.multiple_of(g * group, group), group)
        upper, lower = upper_ref[span, :], lower_ref[span, :]
        score = scores(planes, upper, lower)
        return score, columns(ones_ref, g * 16, 16) * score, upper, lower

    def operator(direction):
        planes = two_planes(direction)

        def step(g, total):
            _, weighted, upper, lower = part(g, planes)
            return total + combine(weighted, upper, lower)

        total = lax.fori_loop(0, steps, step, jnp.zeros((2 * rows, rank), f32))
        return fold(total) + LAM * direction

    def energy(direction):
        planes = two_planes(direction)

        def step(g, total):
            score, weighted, _, _ = part(g, planes)
            return total + jnp.sum(score * weighted, axis=-1, keepdims=True)

        total = lax.fori_loop(0, steps, step, jnp.zeros((rows, 1), f32))
        return total + LAM * jnp.sum(direction * direction, axis=-1, keepdims=True)

    solution = start
    direction = residual
    norm_now = jnp.sum(residual * residual, axis=-1, keepdims=True)
    for iteration in range(ITERS):
        if iteration + 1 == ITERS:
            return solution + norm_now / (energy(direction) + EPS) * direction
        image = operator(direction)
        alpha = norm_now / (jnp.sum(direction * image, axis=-1, keepdims=True) + EPS)
        solution = solution + alpha * direction
        residual = residual - alpha * image
        norm_next = jnp.sum(residual * residual, axis=-1, keepdims=True)
        direction = residual + norm_next / (norm_now + EPS) * direction
        norm_now = norm_next


def item_kernel(start_ref, ones_ref, right_ref, step_ref, core_ref, own_ref, other_ref, out_ref, upper_ref, lower_ref, total_ref):
    g = pl.program_id(0)
    parts, depth, _ = own_ref.shape
    part = BL // parts
    chips = depth // part
    group = chips * 2 * BL
    core = core_ref[0]
    planes = two_planes(start_ref[...])

    @pl.when(g == 0)
    def _():
        total_ref[...] = jnp.zeros_like(total_ref)

    for ref, which in ((own_ref, core), (other_ref, 1 - core)):
        for z in range(chips):
            step = step_ref[pl.ds(2 * z + which, 1), :]
            for k in range(parts):
                codes = ref[k, z * part : (z + 1) * part, :].astype(i32)
                rows = pl.ds(pl.multiple_of(g * group + (2 * z + which) * BL + k * part, part), part)
                upper_ref[rows, :] = (high_part(codes) * step).astype(bf16)
                lower_ref[rows, :] = (low_part(codes) * step).astype(bf16)
    span = pl.ds(pl.multiple_of(g * group, group), group)
    upper, lower = upper_ref[span, :], lower_ref[span, :]
    count = group // BL
    weighted = columns(right_ref, g * count, count) - columns(ones_ref, g * count, count) * scores(planes, upper, lower)
    total_ref[...] += combine(weighted, upper, lower)

    @pl.when(g == pl.num_programs(0) - 1)
    def _():
        start = start_ref[...]
        residual = fold(total_ref[...]) - LAM * start
        out_ref[...] = iterate(ones_ref, upper_ref, lower_ref, residual, start)


def solve_items(start, ones, right, step, core, own, other, user_blocks):
    sources, depth, rank = own.shape
    rows = start.shape[0]
    whole = 2 * depth * sources
    ones = ones.reshape(-1, rows, BL)
    right = right.reshape(-1, rows, BL)
    fixed3 = pl.BlockSpec(ones.shape, lambda s: (0, 0, 0), pipeline_mode=pl.Buffered(1))
    codes = pl.BlockSpec((sources // user_blocks, depth, rank), lambda s: (s, 0, 0))
    return pl.pallas_call(
        item_kernel,
        grid=(user_blocks,),
        out_shape=jax.ShapeDtypeStruct((rows, rank), f32),
        in_specs=[
            pl.BlockSpec((rows, rank), lambda s: (0, 0)),
            fixed3,
            fixed3,
            pl.BlockSpec(step.shape, lambda s: (0, 0)),
            pl.BlockSpec(memory_space=pltpu.SMEM),
            codes,
            codes,
        ],
        out_specs=pl.BlockSpec((rows, rank), lambda s: (0, 0)),
        scratch_shapes=[
            pltpu.VMEM((whole, rank), bf16),
            pltpu.VMEM((whole, rank), bf16),
            pltpu.VMEM((2 * rows, rank), f32),
        ],
        compiler_params=params(),
        cost_estimate=pl.CostEstimate(flops=12 * 10**9, bytes_accessed=10**7, transcendentals=0),
        name="solve_items",
    )(start, ones, right, step, core, own, other)


def held_kernel(
    core_ref, ones_ref, right_ref, own_ref, other_ref, out_ref, upper_ref, lower_ref, total_ref
):
    g = pl.program_id(0)
    sources, depth, _ = own_ref.shape
    half = depth - 16
    lanes = BL // 2
    blocks = half // lanes
    group = sources * 2 * half
    core = core_ref[0]

    @pl.when(g == 0)
    def _():
        total_ref[...] = jnp.zeros_like(total_ref)

    for s in range(sources):
        for ref, which in ((own_ref, core), (other_ref, 1 - core)):
            step = power_of_two(ref[s, half : half + 16, :].astype(i32)[:1])
            for b in range(blocks):
                codes = ref[s, b * lanes : (b + 1) * lanes, :].astype(i32)
                rows = pl.ds(pl.multiple_of(g * group + (s * blocks + b) * BL + which * lanes, lanes), lanes)
                upper_ref[rows, :] = (high_part(codes) * step).astype(bf16)
                lower_ref[rows, :] = (low_part(codes) * step).astype(bf16)
    span = pl.ds(pl.multiple_of(g * group, group), group)
    count = group // BL
    total_ref[...] += combine(columns(right_ref, g * count, count), upper_ref[span, :], lower_ref[span, :])

    @pl.when(g == pl.num_programs(0) - 1)
    def _():
        residual = fold(total_ref[...])
        out_ref[...] = iterate(ones_ref, upper_ref, lower_ref, residual, jnp.zeros_like(residual))


def solve_held(core, ones, right, own, other, rows):
    sources, depth, rank = own.shape
    whole = 2 * (depth - 16) * sources
    ones = ones.reshape(-1, rows, BL)
    right = right.reshape(-1, rows, BL)
    fixed3 = pl.BlockSpec(ones.shape, lambda s: (0, 0, 0), pipeline_mode=pl.Buffered(1))
    codes = pl.BlockSpec((4, depth, rank), lambda s: (s, 0, 0))
    return pl.pallas_call(
        held_kernel,
        grid=(sources // 4,),
        out_shape=jax.ShapeDtypeStruct((rows, rank), f32),
        in_specs=[pl.BlockSpec(memory_space=pltpu.SMEM), fixed3, fixed3, codes, codes],
        out_specs=pl.BlockSpec((rows, rank), lambda s: (0, 0)),
        scratch_shapes=[
            pltpu.VMEM((whole, rank), bf16),
            pltpu.VMEM((whole, rank), bf16),
            pltpu.VMEM((2 * rows, rank), f32),
        ],
        compiler_params=params(),
        name="solve_held",
    )(core, ones, right, own, other)


def shards(
    user_factors,
    item_factors,
    tile_user,
    tile_item,
    tile_count,
    tile_conf,
    held_user,
    held_item,
    held_count,
    held_conf,
):
    rank = user_factors.shape[1]
    peers = lax.axis_size("user")
    item_peers = lax.axis_size("item")
    chips = peers // 2
    me = lax.axis_index("user")
    core = me % 2
    chip = me // 2
    slots = tile_user.shape[-1]
    held_slots = held_user.shape[-1]
    user_blocks = user_factors.shape[0] // BL
    item_blocks = item_factors.shape[0] // BL
    held_blocks = 2

    same_core = [[c + 2 * z for z in range(chips)] for c in range(2)]
    siblings = [(d, d ^ 1) for d in range(peers)]

    part = user_factors.shape[0] // item_peers
    column = lax.axis_index("item")
    piece, exponent = pack_users(user_factors, column, chips, part)
    piece = lax.all_to_all(piece, "user", 0, 0, tiled=True, axis_index_groups=same_core).reshape(chips * part, rank)

    blocks = peers * user_blocks * item_blocks
    order = [c * chips + z for z in range(chips) for c in range(2)]
    strips = cut_strips(
        me, tile_user[0, 0], tile_item[0, 0], tile_count[0, 0], tile_conf, exponent,
        True, order, (peers, 1), item_blocks, blocks, "cut_items",
    )
    held_all = item_peers * item_blocks * held_blocks
    held_strips = cut_strips(
        column, held_item[0, 0], held_user[0, 0], held_count[0, 0], held_conf, jnp.zeros_like(exponent),
        False, list(range(item_peers)), (1, item_blocks), held_blocks, held_all, "cut_held",
    )
    strips, held_strips, piece = lax.optimization_barrier((strips, held_strips, piece))
    strips = lax.all_to_all(strips, "user", 0, 0, tiled=True)
    own_users = lax.all_gather(piece, "item", axis=0, tiled=False)
    strips, own_users, held_strips = lax.optimization_barrier((strips, own_users, held_strips))
    other_users = lax.ppermute(own_users, "user", siblings)
    held_strips = lax.all_to_all(held_strips, "item", 0, 0, tiled=True)
    ones, right, step = dense(strips, blocks, peers * slots, "dense_items")

    start = lax.dynamic_slice_in_dim(
        item_factors.reshape(item_blocks, peers, SUB, rank), core * chips + chip, 1, axis=1
    ).reshape(item_blocks * SUB, rank)
    mine = solve_items(start, ones, right, step, core.reshape(1), own_users, other_users, user_blocks)
    mine, held_strips = lax.optimization_barrier((mine, held_strips))
    held_ones, held_right, _ = dense(held_strips, held_all, item_peers * held_slots, "dense_held")

    half = lax.all_to_all(
        jnp.broadcast_to(mine[None], (chips,) + mine.shape), "user", 0, 0, tiled=True, axis_index_groups=same_core
    )
    own = lax.all_gather(pack_items(half), "item", axis=0, tiled=False)
    other = lax.ppermute(own, "user", siblings)
    folded = solve_held(core.reshape(1), held_ones, held_right, own, other, held_blocks * SUB)
    folded = lax.all_to_all(
        jnp.broadcast_to(folded[None], (item_peers,) + folded.shape), "item", 0, 0, tiled=True
    )
    folded = folded.reshape(item_peers, held_blocks, SUB, rank).transpose(1, 0, 2, 3).reshape(-1, rank)

    half = half.reshape(chips, item_blocks, SUB, rank).transpose(1, 0, 2, 3).reshape(item_blocks, 1, BL // 2, rank)
    sibling = lax.ppermute(half, "user", siblings)
    new_items = jnp.where(
        core == 0, jnp.concatenate([half, sibling], axis=1), jnp.concatenate([sibling, half], axis=1)
    ).reshape(-1, rank)
    return new_items, folded


def solution(mesh):
    in_specs = (
        P("user", None),
        P("item", None),
        P("item", "user", None, None),
        P("item", "user", None, None),
        P("item", "user", None),
        P("item", "user", None, None, None, None),
        P("user", "item", None, None),
        P("user", "item", None, None),
        P("user", "item", None),
        P("user", "item", None, None, None, None),
    )
    out_specs = (P("item", None), P("user", None))
    return jax.shard_map(shards, mesh=mesh, in_specs=in_specs, out_specs=out_specs, check_vma=False)
```

time: 221 us -> 164 us (0.74)
  waiting for transfers between devices: 48.8 us -> 12.8 us
  Pallas kernels: 77.1 us -> 45.3 us
  blocking collectives: 36.9 us -> 61.6 us
  between operations: 14.3 us -> 0.76 us
  starting transfers between devices: 29.9 us -> 35.8 us
  local copies, waits for them, and re-layouts: 10.7 us -> 7.28 us
  other arithmetic: 2.44 us -> 0.04 us
    all_gather x0 -> x1, blocking collectives: none -> 24.9 us  [shards(): own_users = lax.all_gather(piece, 'item', axis=0, tiled=False)]
    all_to_all x1, waiting for transfers between devices: 28 us -> 4.45 us  [shards(): strips = lax.all_to_all(strips, 'user', 0, 0, tiled=True)]
    pallas_call x3 -> x5, Pallas kernels: 60.7 us -> 38.2 us  [the longest x1 18.6 us: solve_items(): pl.pallas_call(item_kernel, grid=(user_blocks,), out_shape=jax.ShapeDtype...]
    all_to_all x1, waiting for transfers between devices: 13.7 us -> 0.01 us  [shards(): held_strips = lax.all_to_all(held_strips, 'item', 0, 0, tiled=True)]
    pallas_call x2, Pallas kernels: 14.7 us -> 5.32 us  [dense(): pl.pallas_call(functools.partial(dense_kernel, blocks, slots), out_shape=...]
    all_to_all x0 -> x1, starting transfers between devices: none -> 9.15 us  [shards(): lax.all_to_all(piece, 'user', 0, 0, tiled=True, axis_index_groups=same_core)]
    all_to_all x1, starting transfers between devices: 11.2 us -> 8.17 us  [shards(): strips = lax.all_to_all(strips, 'user', 0, 0, tiled=True)]
  transfers between devices with their start and end apart: 6 -> 7, of which waited for: 3 -> 3; matrix products, arithmetic and copies ran while one was open for 5% -> 3% of each run, Pallas kernels for 19% -> 25%
where the time goes in v2:
time: 164 us; the launch traced here: 163 us
  blocking collectives  61.6 us (38%)
  Pallas kernels  45.3 us (28%)
  starting transfers between devices  35.8 us (22%)
  waiting for transfers between devices  12.8 us (8%)
  local copies, waits for them, and re-layouts  7.28 us (4%)
    all_gather x1, blocking collectives, shards(): own_users = lax.all_gather(piece, 'item', axis=0, tiled=False)  24.9 us
    all_gather x1, blocking collectives, shards(): own = lax.all_gather(pack_items(half), 'item', axis=0, tiled=False)  22.7 us
    pallas_call x1, Pallas kernels, solve_items(): pl.pallas_call(item_kernel, grid=(user_blocks,), out_shape=jax.ShapeDtype...  18.6 us
    all_to_all x1, blocking collectives, shards(): lax.all_to_all(jnp.broadcast_to(mine[None], (chips,) + mine.shape), 'user...  14 us
    pallas_call x1, Pallas kernels, solve_held(): pl.pallas_call(held_kernel, grid=(sources // 4,), out_shape=jax.ShapeDtyp...  13.5 us
    all_to_all x1, starting transfers between devices, shards(): lax.all_to_all(piece, 'user', 0, 0, tiled=True, axis_index_groups=same_core)  9.15 us
    all_to_all x1, starting transfers between devices, shards(): strips = lax.all_to_all(strips, 'user', 0, 0, tiled=True)  8.17 us
    ppermute x1, starting transfers between devices, shards(): other = lax.ppermute(own, 'user', siblings)  7.46 us
  transfers between devices with their start and end apart: 7, of which 3 were waited for; matrix products, arithmetic and copies ran while one was open for 3% of the time, Pallas kernels for 25%

profile of v2, /device:TPU:1, one launch (start us, length us, event | category | flops | bytes accessed | tf_op | source)
XLA Modules:
  0.0 163.5 jit_solution(6636541102734889697)
XLA Ops:
  0.7 1.8 %pack_users.1 = (s16[8,32,256]{2,1,0:T(8,128)(2,1)}, f32[1,256]{1,0:T(1,128)}) custom-call(s32[1]{0:T(128)} %bitcast.7.place_ref, f32[512,256]{1,0:T(8,128)} %rows_ref.1), custom_call_target="tpu_custom_call" | custom-call | tf_op jit(solution)/shard_map/pack_users/pallas_call | solution.py:65
  2.5 9.1 %all-to-all-start = ((s16[8,32,256]{2,1,0:T(8,128)(2,1)}), s16[8,32,256]{2,1,0:T(8,128)(2,1)S(1)}, u32[]{:S(2)}, u32[]{:S(2)}) async-start(s16[8,32,256]{2,1,0:T(8,128)(2,1)} %get-tuple-element.18), calls=%async_computation | async-start | bytes 262144 | tf_op jit(solution)/shard_map/all_to_all | solution.py:424
  12.4 0.8 copy.25.inner_ref
  13.2 0.8 copy.26.outer_ref
  14.7 1.2 copy-done.1
  16.5 2.1 %cut_held.1 = bf16[16,272,128]{2,1,0:T(8,128)(2,1)} custom-call(s32[1]{0:T(128)} %bitcast.7.place_ref, s32[16,2]{1,0:T(8,128)S(1)} %copy.26.outer_ref, s32[16,2]{1,0:T(8,128)S(1)} %copy.27.inner_ref, s32[16]{0:T(128)S(1)} %bitcast.44, bf16[32,128,128]{2,1,0:T(8,128)(2,1)S(1)} %bitcast.40, f32[1,256]{1,0:T(1,128)S(1)} %broadcast_in_dim.6.extra_ref), custom_call_target="tpu_custom_call" | custom-call | flops 1000000 | bytes 2000000 | tf_op jit(solution)/shard_map/cut_held/pallas_call | solution.py:108
  18.6 2.1 %cut_items.1 = bf16[16,272,128]{2,1,0:T(8,128)(2,1)} custom-call(s32[1]{0:T(128)} %bitcast.2.place_ref, s32[16,2]{1,0:T(8,128)S(1)} %copy.24.outer_ref, s32[16,2]{1,0:T(8,128)S(1)} %copy.25.inner_ref, s32[16]{0:T(128)S(1)} %bitcast.45, bf16[32,128,128]{2,1,0:T(8,128)(2,1)S(1)} %bitcast.41, f32[1,256]{1,0:T(1,128)S(1)} %copy-done.3), custom_call_target="tpu_custom_call" | custom-call | flops 1000000 | bytes 2000000 | tf_op jit(solution)/shard_map/cut_items/pallas_call | solution.py:108
  20.8 8.2 %all-to-all-start.1 = ((bf16[16,272,128]{2,1,0:T(8,128)(2,1)}), bf16[16,272,128]{2,1,0:T(8,128)(2,1)}, u32[]{:S(2)}, u32[]{:S(2)}) async-start(bf16[16,272,128]{2,1,0:T(8,128)(2,1)} %cut_items.1), calls=%async_computation.1 | async-start | bytes 2228224 | tf_op jit(solution)/shard_map/all_to_all | solution.py:438
  29.0 24.9 %all-gather.4 = s16[4096,256]{1,0:T(8,128)(2,1)S(1)} all-gather(s16[256,256]{1,0:T(8,128)(2,1)S(1)} %bitcast.49), channel_id=2, replica_groups=mesh['user'=16,'item'=16] {'item'}, dimensions={0}, use_global_device_ids=true | all-gather | bytes 2228224 | tf_op jit(solution)/shard_map/all_gather | solution.py:439
  53.9 4.4 %all-to-all-done.1.strips_ref = bf16[16,272,128]{2,1,0:T(8,128)(2,1)} async-done(((bf16[16,272,128]{2,1,0:T(8,128)(2,1)}), bf16[16,272,128]{2,1,0:T(8,128)(2,1)}, u32[]{:S(2)}, u32[]{:S(2)}) %all-to-all-start.1) | async-done | bytes 1114144 | tf_op jit(solution)/shard_map/all_to_all | solution.py:438
  58.3 6.8 %all-to-all-start.2 = ((bf16[16,272,128]{2,1,0:T(8,128)(2,1)}), bf16[16,272,128]{2,1,0:T(8,128)(2,1)}, u32[]{:S(2)}, u32[]{:S(2)}) async-start(bf16[16,272,128]{2,1,0:T(8,128)(2,1)} %cut_held.1), calls=%async_computation.2 | async-start | bytes 2228224 | tf_op jit(solution)/shard_map/all_to_all | solution.py:442
  65.1 2.6 %dense_items.1 = (f32[2048,128]{1,0:T(8,128)S(1)}, f32[2048,128]{1,0:T(8,128)S(1)}, f32[16,256]{1,0:T(8,128)S(1)}) custom-call(bf16[16,272,128]{2,1,0:T(8,128)(2,1)} %all-to-all-done.1.strips_ref), custom_call_target="tpu_custom_call" | custom-call | flops 400000000 | bytes 3000000 | tf_op jit(solution)/shard_map/dense_items/pallas_call | solution.py:172
  67.7 18.6 %solve_items.1 = f32[32,256]{1,0:T(8,128)S(1)} custom-call(f32[32,256]{1,0:T(8,128)S(1)} %dynamic-slice_bitcast_fusion.start_ref, f32[64,32,128]{2,1,0:T(8,128)S(1)} %bitcast.46, f32[64,32,128]{2,1,0:T(8,128)S(1)} %bitcast.47, f32[16,256]{1,0:T(8,128)S(1)} %get-tuple-element.25.step_ref, s32[1]{0:T(128)} %bitcast.16.core_ref, ...), custom_call_target="tpu_custom_call" | custom-call | flops 12000000000 | bytes 10000000 | tf_op jit(solution)/shard_map/solve_items/pallas_call | solution.py:312
  86.4 14.0 %all_to_all.25.rows_ref = f32[8,32,256]{2,1,0:T(8,128)} all-to-all(f32[8,32,256]{2,1,0:T(8,128)S(1)} %broadcast_in_dim.7), channel_id=1, replica_groups={{0,32,64,96,128,160,192,224},{16,48,80,112,144,176,208,240},{1,33,65,97..., dimensions={0} | all-to-all | bytes 524288 | tf_op jit(solution)/shard_map/all_to_all | solution.py:452
  100.4 1.8 %pack_items.1 = s16[272,256]{1,0:T(8,128)(2,1)} custom-call(f32[8,32,256]{2,1,0:T(8,128)} %all_to_all.25.rows_ref), custom_call_target="tpu_custom_call" | custom-call | tf_op jit(solution)/shard_map/pack_items/pallas_call | solution.py:137
  102.2 22.7 %all-gather.5 = s16[4352,256]{1,0:T(8,128)(2,1)S(1)} all-gather(s16[272,256]{1,0:T(8,128)(2,1)} %pack_items.1), channel_id=3, replica_groups=mesh['user'=16,'item'=16] {'item'}, dimensions={0}, use_global_device_ids=true | all-gather | bytes 2367488 | tf_op jit(solution)/shard_map/all_gather | solution.py:455
  124.9 7.5 %collective-permute-start.2 = (s16[16,272,256]{2,1,0:T(8,128)(2,1)S(1)}, s16[16,272,256]{2,1,0:T(8,128)(2,1)S(1)}, u32[]{:S(2)}, u32[]{:S(2)}) collective-permute-start(s16[16,272,256]{2,1,0:T(8,128)(2,1)S(1)} %bitcast.36), channel_id=1, source_target_pairs={{0,16},{16,0},{32,48},{48,32},{64,80},{80,64},{96,112},{112,96},{1... | collective-permute-start | bytes 6684680 | tf_op jit(solution)/shard_map/ppermute | solution.py:456
  132.4 2.7 %dense_held.1 = (f32[1024,128]{1,0:T(8,128)S(1)}, f32[1024,128]{1,0:T(8,128)S(1)}, f32[16,256]{1,0:T(8,128)}) custom-call(bf16[16,272,128]{2,1,0:T(8,128)(2,1)} %all-to-all-done.2.strips_ref), custom_call_target="tpu_custom_call" | custom-call | flops 400000000 | bytes 3000000 | tf_op jit(solution)/shard_map/dense_held/pallas_call | solution.py:172
  135.2 1.1 collective-permute-done.2.other_ref
  136.3 13.5 %solve_held.1 = f32[16,256]{1,0:T(8,128)S(1)} custom-call(s32[1]{0:T(128)} %bitcast.16.core_ref, f32[64,16,128]{2,1,0:T(8,128)S(1)} %bitcast.42, f32[64,16,128]{2,1,0:T(8,128)S(1)} %bitcast.43, s16[16,272,256]{2,1,0:T(8,128)(2,1)S(1)} %bitcast.37, s16[16,272,256]{2,1,0:T(8,128)(2,1)S(1)} %collective-permute-done.2.other_ref), custom_call_target="tpu_custom_call" | custom-call | tf_op jit(solution)/shard_map/solve_held/pallas_call | solution.py:377
  149.8 0.8 broadcast_in_dim.8
  150.6 4.1 %all-to-all-start.4 = ((f32[16,16,256]{2,1,0:T(8,128)}), f32[16,16,256]{2,1,0:T(8,128)S(1)}, u32[]{:S(2)}, u32[]{:S(2)}) async-start(f32[16,16,256]{2,1,0:T(8,128)} %broadcast_in_dim.8), calls=%async_computation.4 | async-start | bytes 524288 | tf_op jit(solution)/shard_map/all_to_all | solution.py:458
  154.7 0.8 copy.29
  155.6 7.2 %all-to-all-done.4 = f32[16,16,256]{2,1,0:T(8,128)S(1)} async-done(((f32[16,16,256]{2,1,0:T(8,128)}), f32[16,16,256]{2,1,0:T(8,128)S(1)}, u32[]{:S(2)}, u32[]{:S(2)}) %all-to-all-start.4) | async-done | bytes 262176 | tf_op jit(solution)/shard_map/all_to_all | solution.py:458
  (27 shorter events, 3.1 us)
Async XLA Ops:
  0.6 57.7 %copy-start = (f32[512,256]{1,0:T(8,128)S(1)}, f32[512,256]{1,0:T(8,128)}, u32[]{:S(2)}) copy-start(f32[512,256]{1,0:T(8,128)} %param.11) | copy-start | bytes 1572868
  0.6 18.0 %copy-start.5 = (s32[1,1,16]{2,1,0:T(1,128)S(1)}, s32[1,1,16]{2,1,0:T(1,128)}, u32[]{:S(2)}) copy-start(s32[1,1,16]{2,1,0:T(1,128)} %param.14) | copy-start | bytes 196
  2.5 16.1 %copy-start.3 = (f32[1,256]{1,0:T(1,128)S(1)}, f32[1,256]{1,0:T(1,128)}, u32[]{:S(2)}) copy-start(f32[1,256]{1,0:T(1,128)} %get-tuple-element.17.extra_ref) | copy-start | bytes 3076
  2.5 18.3 %all-to-all-start = ((s16[8,32,256]{2,1,0:T(8,128)(2,1)}), s16[8,32,256]{2,1,0:T(8,128)(2,1)S(1)}, u32[]{:S(2)}, u32[]{:S(2)}) async-start(s16[8,32,256]{2,1,0:T(8,128)(2,1)} %get-tuple-element.18), calls=%async_computation | async-start | bytes 262144 | tf_op jit(solution)/shard_map/all_to_all | solution.py:424
  14.7 1.2 copy-start.1
  15.9 0.7 copy-start.4
  16.5 2.1 %copy-start.2 = (bf16[1,1,16,2,128,128]{5,4,3,2,1,0:T(8,128)(2,1)S(1)}, bf16[1,1,16,2,128,128]{5,4,3,2,1,0:T(8,128)(2,1)}, u32[]{:S(2)}) copy-start(bf16[1,1,16,2,128,128]{5,4,3,2,1,0:T(8,128)(2,1)} %param.15) | copy-start | bytes 3145732
  20.8 37.5 %all-to-all-start.1 = ((bf16[16,272,128]{2,1,0:T(8,128)(2,1)}), bf16[16,272,128]{2,1,0:T(8,128)(2,1)}, u32[]{:S(2)}, u32[]{:S(2)}) async-start(bf16[16,272,128]{2,1,0:T(8,128)(2,1)} %cut_items.1), calls=%async_computation.1 | async-start | bytes 2228224 | tf_op jit(solution)/shard_map/all_to_all | solution.py:438
  58.3 9.4 %collective-permute-start = (s16[16,256,256]{2,1,0:T(8,128)(2,1)S(1)}, s16[16,256,256]{2,1,0:T(8,128)(2,1)}, u32[]{:S(2)}, u32[]{:S(2)}) collective-permute-start(s16[16,256,256]{2,1,0:T(8,128)(2,1)S(1)} %bitcast.38), channel_id=1, source_target_pairs={{0,16},{16,0},{32,48},{48,32},{64,80},{80,64},{96,112},{112,96},{1... | collective-permute-start | bytes 6291464 | tf_op jit(solution)/shard_map/ppermute | solution.py:441
  58.3 28.0 %all-to-all-start.2 = ((bf16[16,272,128]{2,1,0:T(8,128)(2,1)}), bf16[16,272,128]{2,1,0:T(8,128)(2,1)}, u32[]{:S(2)}, u32[]{:S(2)}) async-start(bf16[16,272,128]{2,1,0:T(8,128)(2,1)} %cut_held.1), calls=%async_computation.2 | async-start | bytes 2228224 | tf_op jit(solution)/shard_map/all_to_all | solution.py:442
  100.4 31.9 %copy-start.6 = (f32[8,32,256]{2,1,0:T(8,128)S(1)}, f32[8,32,256]{2,1,0:T(8,128)}, u32[]{:S(2)}) copy-start(f32[8,32,256]{2,1,0:T(8,128)} %all_to_all.25.rows_ref) | copy-start | bytes 786436
  124.9 11.4 %collective-permute-start.2 = (s16[16,272,256]{2,1,0:T(8,128)(2,1)S(1)}, s16[16,272,256]{2,1,0:T(8,128)(2,1)S(1)}, u32[]{:S(2)}, u32[]{:S(2)}) collective-permute-start(s16[16,272,256]{2,1,0:T(8,128)(2,1)S(1)} %bitcast.36), channel_id=1, source_target_pairs={{0,16},{16,0},{32,48},{48,32},{64,80},{80,64},{96,112},{112,96},{1... | collective-permute-start | bytes 6684680 | tf_op jit(solution)/shard_map/ppermute | solution.py:456
  132.3 22.3 %collective-permute-start.1 = (f32[4,1,64,256]{3,2,0,1:T(8,128)S(1)}, f32[4,1,64,256]{3,2,0,1:T(8,128)S(1)}, u32[]{:S(2)}, u32[]{:S(2)}) collective-permute-start(f32[4,1,64,256]{3,2,0,1:T(8,128)S(1)} %copy_bitcast_fusion), channel_id=1, source_target_pairs={{0,16},{16,0},{32,48},{48,32},{64,80},{80,64},{96,112},{112,96},{1... | collective-permute-start | bytes 786440 | tf_op jit(solution)/shard_map/ppermute | solution.py:464
  150.6 12.2 %all-to-all-start.4 = ((f32[16,16,256]{2,1,0:T(8,128)}), f32[16,16,256]{2,1,0:T(8,128)S(1)}, u32[]{:S(2)}, u32[]{:S(2)}) async-start(f32[16,16,256]{2,1,0:T(8,128)} %broadcast_in_dim.8), calls=%async_computation.4 | async-start | bytes 524288 | tf_op jit(solution)/shard_map/all_to_all | solution.py:458

commit v3 on v2

--- a/solution.py
+++ b/solution.py
@@ -12,6 +12,7 @@
 EPS = 1e-6
 BL = 128
 SUB = 8
+GROUP = 32
 VMEM = 28 * 1024 * 1024
 
 i32 = jnp.int32
@@ -72,7 +73,7 @@
 
 
 def strips_kernel(turn, order, owner_scale, slot_scale, dead, place_ref, outer_ref, inner_ref, count_ref, tiles_ref, extra_ref, out_ref):
-    owners, slots = outer_ref.shape
+    slots, owners = outer_ref.shape
     total = owners * slots
     for t in range(0, total, 2):
         pair = [tiles_ref[t + k].astype(f32) for k in range(2)]
@@ -91,7 +92,7 @@
     codes = jnp.zeros((16, BL), f32)
     for o in range(owners):
         for c in range(slots):
-            code = (outer_ref[o, c] * outer_scale + o * owner_scale) * slot_scale + inner_ref[o, c]
+            code = (outer_ref[c, o] * outer_scale + o * owner_scale) * slot_scale + inner_ref[c, o]
             code = jnp.where(c < count_ref[o], code, dead)
             codes = jnp.where(mine == o * slots + c, code.astype(f32), codes)
     below = owners * total // BL
@@ -103,7 +104,7 @@
 
 
 def cut_strips(place, outer, inner, count, tiles, extra, turn, order, owner_scale, slot_scale, dead, name):
-    owners, slots = outer.shape
+    slots, owners = outer.shape
     smem = pl.BlockSpec(memory_space=pltpu.SMEM)
     return pl.pallas_call(
         functools.partial(strips_kernel, turn, order, owner_scale, slot_scale, dead),
@@ -195,18 +196,21 @@
     return both[:rows] + both[rows:]
 
 
-def scores(direction, upper, lower):
-    return fold(
-        lax.dot_general(direction, upper, NT, preferred_element_type=f32)
-        + lax.dot_general(direction, lower, NT, preferred_element_type=f32)
-    )
-
-
-def combine(weighted, upper, lower):
-    planes = two_planes(weighted)
-    return lax.dot_general(planes, upper, NN, preferred_element_type=f32) + lax.dot_general(
-        planes, lower, NN, preferred_element_type=f32
-    )
+def twice(planes):
+    return jnp.concatenate([planes, planes], axis=1)
+
+
+def scores(planes, factors):
+    return fold(lax.dot_general(planes, factors, NT, preferred_element_type=f32))
+
+
+def combine(weighted, factors):
+    return jnp.dot(two_planes(weighted), factors, preferred_element_type=f32)
+
+
+def join(both):
+    rank = both.shape[1] // 2
+    return fold(both[:, :rank] + both[:, rank:])
 
 
 def columns(ref, first, count):
@@ -221,32 +225,31 @@
     return (codes & 255).astype(f32)
 
 
-def iterate(ones_ref, upper_ref, lower_ref, residual, start):
+def iterate(ones_ref, factors_ref, residual, start):
     rows, rank = residual.shape
-    group = 16 * BL
-    steps = upper_ref.shape[0] // group
+    group = GROUP * BL
+    steps = factors_ref.shape[0] // group
 
     def part(g, planes):
-        span = pl.ds(pl.multiple_of(g * group, group), group)
-        upper, lower = upper_ref[span, :], lower_ref[span, :]
-        score = scores(planes, upper, lower)
-        return score, columns(ones_ref, g * 16, 16) * score, upper, lower
+        factors = factors_ref[pl.ds(pl.multiple_of(g * group, group), group), :]
+        score = scores(planes, factors)
+        return score, columns(ones_ref, g * GROUP, GROUP) * score, factors
 
     def operator(direction):
-        planes = two_planes(direction)
+        planes = twice(two_planes(direction))
 
         def step(g, total):
-            _, weighted, upper, lower = part(g, planes)
-            return total + combine(weighted, upper, lower)
-
-        total = lax.fori_loop(0, steps, step, jnp.zeros((2 * rows, rank), f32))
-        return fold(total) + LAM * direction
+            _, weighted, factors = part(g, planes)
+            return total + combine(weighted, factors)
+
+        total = lax.fori_loop(0, steps, step, jnp.zeros((2 * rows, 2 * rank), f32))
+        return join(total) + LAM * direction
 
     def energy(direction):
-        planes = two_planes(direction)
+        planes = twice(two_planes(direction))
 
         def step(g, total):
-            score, weighted, _, _ = part(g, planes)
+            score, weighted, _ = part(g, planes)
             return total + jnp.sum(score * weighted, axis=-1, keepdims=True)
 
         total = lax.fori_loop(0, steps, step, jnp.zeros((rows, 1), f32))
@@ -267,14 +270,13 @@
         norm_now = norm_next
 
 
-def item_kernel(start_ref, ones_ref, right_ref, step_ref, core_ref, own_ref, other_ref, out_ref, upper_ref, lower_ref, total_ref):
+def item_kernel(chips, start_ref, ones_ref, right_ref, step_ref, core_ref, own_ref, other_ref, out_ref, factors_ref, total_ref):
     g = pl.program_id(0)
-    parts, depth, _ = own_ref.shape
-    part = BL // parts
-    chips = depth // part
-    group = chips * 2 * BL
+    sources, depth, rank = own_ref.shape
+    part = depth // chips
+    per = BL // part
+    group = sources * 2 * depth
     core = core_ref[0]
-    planes = two_planes(start_ref[...])
 
     @pl.when(g == 0)
     def _():
@@ -283,36 +285,39 @@
     for ref, which in ((own_ref, core), (other_ref, 1 - core)):
         for z in range(chips):
             step = step_ref[pl.ds(2 * z + which, 1), :]
-            for k in range(parts):
+            for k in range(sources):
                 codes = ref[k, z * part : (z + 1) * part, :].astype(i32)
-                rows = pl.ds(pl.multiple_of(g * group + (2 * z + which) * BL + k * part, part), part)
-                upper_ref[rows, :] = (high_part(codes) * step).astype(bf16)
-                lower_ref[rows, :] = (low_part(codes) * step).astype(bf16)
-    span = pl.ds(pl.multiple_of(g * group, group), group)
-    upper, lower = upper_ref[span, :], lower_ref[span, :]
+                start = g * group + (k // per * 2 * chips + 2 * z + which) * BL + k % per * part
+                rows = pl.ds(pl.multiple_of(start, part), part)
+                factors_ref[rows, :rank] = (high_part(codes) * step).astype(bf16)
+                factors_ref[rows, rank:] = (low_part(codes) * step).astype(bf16)
+    factors = factors_ref[pl.ds(pl.multiple_of(g * group, group), group), :]
     count = group // BL
-    weighted = columns(right_ref, g * count, count) - columns(ones_ref, g * count, count) * scores(planes, upper, lower)
-    total_ref[...] += combine(weighted, upper, lower)
+    score = scores(twice(two_planes(start_ref[...])), factors)
+    weighted = columns(right_ref, g * count, count) - columns(ones_ref, g * count, count) * score
+    total_ref[...] += combine(weighted, factors)
 
     @pl.when(g == pl.num_programs(0) - 1)
     def _():
         start = start_ref[...]
-        residual = fold(total_ref[...]) - LAM * start
-        out_ref[...] = iterate(ones_ref, upper_ref, lower_ref, residual, start)
-
-
-def solve_items(start, ones, right, step, core, own, other, user_blocks):
+        found = iterate(ones_ref, factors_ref, join(total_ref[...]) - LAM * start, start)
+        for d in range(out_ref.shape[0]):
+            out_ref[d] = found
+
+
+def solve_items(start, ones, right, step, core, own, other, copies):
     sources, depth, rank = own.shape
     rows = start.shape[0]
     whole = 2 * depth * sources
+    grid = whole // (GROUP * BL)
     ones = ones.reshape(-1, rows, BL)
     right = right.reshape(-1, rows, BL)
     fixed3 = pl.BlockSpec(ones.shape, lambda s: (0, 0, 0), pipeline_mode=pl.Buffered(1))
-    codes = pl.BlockSpec((sources // user_blocks, depth, rank), lambda s: (s, 0, 0))
-    return pl.pallas_call(
-        item_kernel,
-        grid=(user_blocks,),
-        out_shape=jax.ShapeDtypeStruct((rows, rank), f32),
+    codes = pl.BlockSpec((sources // grid, depth, rank), lambda s: (s, 0, 0))
+    return pl.pallas_call(
+        functools.partial(item_kernel, copies),
+        grid=(grid,),
+        out_shape=jax.ShapeDtypeStruct((copies, rows, rank), f32),
         in_specs=[
             pl.BlockSpec((rows, rank), lambda s: (0, 0)),
             fixed3,
@@ -322,23 +327,17 @@
             codes,
             codes,
         ],
-        out_specs=pl.BlockSpec((rows, rank), lambda s: (0, 0)),
-        scratch_shapes=[
-            pltpu.VMEM((whole, rank), bf16),
-            pltpu.VMEM((whole, rank), bf16),
-            pltpu.VMEM((2 * rows, rank), f32),
-        ],
+        out_specs=pl.BlockSpec((copies, rows, rank), lambda s: (0, 0, 0)),
+        scratch_shapes=[pltpu.VMEM((whole, 2 * rank), bf16), pltpu.VMEM((2 * rows, 2 * rank), f32)],
         compiler_params=params(),
         cost_estimate=pl.CostEstimate(flops=12 * 10**9, bytes_accessed=10**7, transcendentals=0),
         name="solve_items",
     )(start, ones, right, step, core, own, other)
 
 
-def held_kernel(
-    core_ref, ones_ref, right_ref, own_ref, other_ref, out_ref, upper_ref, lower_ref, total_ref
-):
+def held_kernel(core_ref, ones_ref, right_ref, own_ref, other_ref, out_ref, factors_ref, total_ref):
     g = pl.program_id(0)
-    sources, depth, _ = own_ref.shape
+    sources, depth, rank = own_ref.shape
     half = depth - 16
     lanes = BL // 2
     blocks = half // lanes
@@ -354,37 +353,37 @@
             step = power_of_two(ref[s, half : half + 16, :].astype(i32)[:1])
             for b in range(blocks):
                 codes = ref[s, b * lanes : (b + 1) * lanes, :].astype(i32)
-                rows = pl.ds(pl.multiple_of(g * group + (s * blocks + b) * BL + which * lanes, lanes), lanes)
-                upper_ref[rows, :] = (high_part(codes) * step).astype(bf16)
-                lower_ref[rows, :] = (low_part(codes) * step).astype(bf16)
-    span = pl.ds(pl.multiple_of(g * group, group), group)
+                start = g * group + (s * blocks + b) * BL + which * lanes
+                rows = pl.ds(pl.multiple_of(start, lanes), lanes)
+                factors_ref[rows, :rank] = (high_part(codes) * step).astype(bf16)
+                factors_ref[rows, rank:] = (low_part(codes) * step).astype(bf16)
+    factors = factors_ref[pl.ds(pl.multiple_of(g * group, group), group), :]
     count = group // BL
-    total_ref[...] += combine(columns(right_ref, g * count, count), upper_ref[span, :], lower_ref[span, :])
+    total_ref[...] += combine(columns(right_ref, g * count, count), factors)
 
     @pl.when(g == pl.num_programs(0) - 1)
     def _():
-        residual = fold(total_ref[...])
-        out_ref[...] = iterate(ones_ref, upper_ref, lower_ref, residual, jnp.zeros_like(residual))
-
-
-def solve_held(core, ones, right, own, other, rows):
+        residual = join(total_ref[...])
+        found = iterate(ones_ref, factors_ref, residual, jnp.zeros_like(residual))
+        for d in range(out_ref.shape[0]):
+            out_ref[d] = found
+
+
+def solve_held(core, ones, right, own, other, rows, copies):
     sources, depth, rank = own.shape
     whole = 2 * (depth - 16) * sources
+    grid = whole // (GROUP * BL)
     ones = ones.reshape(-1, rows, BL)
     right = right.reshape(-1, rows, BL)
     fixed3 = pl.BlockSpec(ones.shape, lambda s: (0, 0, 0), pipeline_mode=pl.Buffered(1))
-    codes = pl.BlockSpec((4, depth, rank), lambda s: (s, 0, 0))
+    codes = pl.BlockSpec((sources // grid, depth, rank), lambda s: (s, 0, 0))
     return pl.pallas_call(
         held_kernel,
-        grid=(sources // 4,),
-        out_shape=jax.ShapeDtypeStruct((rows, rank), f32),
+        grid=(grid,),
+        out_shape=jax.ShapeDtypeStruct((copies, rows, rank), f32),
         in_specs=[pl.BlockSpec(memory_space=pltpu.SMEM), fixed3, fixed3, codes, codes],
-        out_specs=pl.BlockSpec((rows, rank), lambda s: (0, 0)),
-        scratch_shapes=[
-            pltpu.VMEM((whole, rank), bf16),
-            pltpu.VMEM((whole, rank), bf16),
-            pltpu.VMEM((2 * rows, rank), f32),
-        ],
+        out_specs=pl.BlockSpec((copies, rows, rank), lambda s: (0, 0, 0)),
+        scratch_shapes=[pltpu.VMEM((whole, 2 * rank), bf16), pltpu.VMEM((2 * rows, 2 * rank), f32)],
         compiler_params=params(),
         name="solve_held",
     )(core, ones, right, own, other)
@@ -426,12 +425,12 @@
     blocks = peers * user_blocks * item_blocks
     order = [c * chips + z for z in range(chips) for c in range(2)]
     strips = cut_strips(
-        me, tile_user[0, 0], tile_item[0, 0], tile_count[0, 0], tile_conf, exponent,
+        me, tile_user[0, 0].T, tile_item[0, 0].T, tile_count[0, 0], tile_conf, exponent,
         True, order, (peers, 1), item_blocks, blocks, "cut_items",
     )
     held_all = item_peers * item_blocks * held_blocks
     held_strips = cut_strips(
-        column, held_item[0, 0], held_user[0, 0], held_count[0, 0], held_conf, jnp.zeros_like(exponent),
+        column, held_item[0, 0].T, held_user[0, 0].T, held_count[0, 0], held_conf, jnp.zeros_like(exponent),
         False, list(range(item_peers)), (1, item_blocks), held_blocks, held_all, "cut_held",
     )
     strips, held_strips, piece = lax.optimization_barrier((strips, held_strips, piece))
@@ -445,19 +444,15 @@
     start = lax.dynamic_slice_in_dim(
         item_factors.reshape(item_blocks, peers, SUB, rank), core * chips + chip, 1, axis=1
     ).reshape(item_blocks * SUB, rank)
-    mine = solve_items(start, ones, right, step, core.reshape(1), own_users, other_users, user_blocks)
+    mine = solve_items(start, ones, right, step, core.reshape(1), own_users, other_users, chips)
     mine, held_strips = lax.optimization_barrier((mine, held_strips))
     held_ones, held_right, _ = dense(held_strips, held_all, item_peers * held_slots, "dense_held")
 
-    half = lax.all_to_all(
-        jnp.broadcast_to(mine[None], (chips,) + mine.shape), "user", 0, 0, tiled=True, axis_index_groups=same_core
-    )
+    half = lax.all_to_all(mine, "user", 0, 0, tiled=True, axis_index_groups=same_core)
     own = lax.all_gather(pack_items(half), "item", axis=0, tiled=False)
     other = lax.ppermute(own, "user", siblings)
-    folded = solve_held(core.reshape(1), held_ones, held_right, own, other, held_blocks * SUB)
-    folded = lax.all_to_all(
-        jnp.broadcast_to(folded[None], (item_peers,) + folded.shape), "item", 0, 0, tiled=True
-    )
+    folded = solve_held(core.reshape(1), held_ones, held_right, own, other, held_blocks * SUB, item_peers)
+    folded = lax.all_to_all(folded, "item", 0, 0, tiled=True)
     folded = folded.reshape(item_peers, held_blocks, SUB, rank).transpose(1, 0, 2, 3).reshape(-1, rank)
 
     half = half.reshape(chips, item_blocks, SUB, rank).transpose(1, 0, 2, 3).reshape(item_blocks, 1, BL // 2, rank)

time: 164 us -> 157 us (0.957)
  Pallas kernels: 45.3 us -> 39.9 us
  local copies, waits for them, and re-layouts: 7.28 us -> 4.84 us
    pallas_call x2, Pallas kernels: 32.1 us -> 27.2 us  [the longest x1 15.2 us: solve_items(): pl.pallas_call(functools.partial(item_kernel, copies), grid=(grid,), out_...]
    squeeze x4 -> x0, local copies, waits for them, and re-layouts: 3.02 us -> none  [the longest x1 0.75 us: shards(): tile_item[0, 0]]
  transfers between devices with their start and end apart: 7 -> 7, of which waited for: 3 -> 4; matrix products, arithmetic and copies ran while one was open for 3% -> 1% of each run, Pallas kernels for 25% -> 23%
where the time goes in v3:
time: 157 us; the launch traced here: 156 us
  blocking collectives  61.6 us (39%)
  Pallas kernels  39.9 us (25%)
  starting transfers between devices  35.3 us (22%)
  waiting for transfers between devices  13.3 us (8%)
  local copies, waits for them, and re-layouts  4.84 us (3%)
    all_gather x1, blocking collectives, shards(): own_users = lax.all_gather(piece, 'item', axis=0, tiled=False)  24.9 us
    all_gather x1, blocking collectives, shards(): own = lax.all_gather(pack_items(half), 'item', axis=0, tiled=False)  22.3 us
    pallas_call x1, Pallas kernels, solve_items(): pl.pallas_call(functools.partial(item_kernel, copies), grid=(grid,), out_...  15.2 us
    all_to_all x1, blocking collectives, shards(): lax.all_to_all(mine, 'user', 0, 0, tiled=True, axis_index_groups=same_core)  14.4 us
    pallas_call x1, Pallas kernels, solve_held(): pl.pallas_call(held_kernel, grid=(grid,), out_shape=jax.ShapeDtypeStruct(...  12 us
    all_to_all x1, starting transfers between devices, shards(): lax.all_to_all(piece, 'user', 0, 0, tiled=True, axis_index_groups=same_core)  9.15 us
    all_to_all x1, starting transfers between devices, shards(): strips = lax.all_to_all(strips, 'user', 0, 0, tiled=True)  7.48 us
    ppermute x1, starting transfers between devices, shards(): other = lax.ppermute(own, 'user', siblings)  7.46 us
  transfers between devices with their start and end apart: 7, of which 4 were waited for; matrix products, arithmetic and copies ran while one was open for 1% of the time, Pallas kernels for 23%

profile of v3, /device:TPU:1, one launch (start us, length us, event | category | flops | bytes accessed | tf_op | source)
XLA Modules:
  0.0 155.8 jit_solution(147375018764332610)
XLA Ops:
  0.7 1.8 %pack_users.1 = (s16[8,32,256]{2,1,0:T(8,128)(2,1)}, f32[1,256]{1,0:T(1,128)}) custom-call(s32[1]{0:T(128)} %bitcast.9.place_ref, f32[512,256]{1,0:T(8,128)} %rows_ref.1), custom_call_target="tpu_custom_call" | custom-call | tf_op jit(solution)/shard_map/pack_users/pallas_call | solution.py:66
  2.5 9.1 %all-to-all-start = ((s16[8,32,256]{2,1,0:T(8,128)(2,1)}), s16[8,32,256]{2,1,0:T(8,128)(2,1)S(1)}, u32[]{:S(2)}, u32[]{:S(2)}) async-start(s16[8,32,256]{2,1,0:T(8,128)(2,1)} %get-tuple-element.18), calls=%async_computation | async-start | bytes 262144 | tf_op jit(solution)/shard_map/all_to_all | solution.py:423
  11.7 1.2 copy-done.1
  12.9 0.7 copy-done.3
  14.9 1.9 %cut_held.1 = bf16[16,272,128]{2,1,0:T(8,128)(2,1)} custom-call(s32[1]{0:T(128)} %bitcast.9.place_ref, s32[2,16]{1,0:T(2,128)S(1)} %bitcast.52, s32[2,16]{1,0:T(2,128)S(1)} %bitcast.53, s32[16]{0:T(128)S(1)} %bitcast.56, bf16[32,128,128]{2,1,0:T(8,128)(2,1)S(1)} %bitcast.48, f32[1,256]{1,0:T(1,128)S(1)} %broadcast_in_dim.3.extra_ref), custom_call_target="tpu_custom_call" | custom-call | flops 1000000 | bytes 2000000 | tf_op jit(solution)/shard_map/cut_held/pallas_call | solution.py:109
  16.8 1.9 %cut_items.1 = bf16[16,272,128]{2,1,0:T(8,128)(2,1)} custom-call(s32[1]{0:T(128)} %bitcast.2.place_ref, s32[2,16]{1,0:T(2,128)S(1)} %bitcast.54, s32[2,16]{1,0:T(2,128)S(1)} %bitcast.55, s32[16]{0:T(128)S(1)} %bitcast.57, bf16[32,128,128]{2,1,0:T(8,128)(2,1)S(1)} %bitcast.49, f32[1,256]{1,0:T(1,128)S(1)} %copy-done.7), custom_call_target="tpu_custom_call" | custom-call | flops 1000000 | bytes 2000000 | tf_op jit(solution)/shard_map/cut_items/pallas_call | solution.py:109
  18.7 0.7 all-to-all-done
  19.4 7.5 %all-to-all-start.1 = ((bf16[16,272,128]{2,1,0:T(8,128)(2,1)}), bf16[16,272,128]{2,1,0:T(8,128)(2,1)}, u32[]{:S(2)}, u32[]{:S(2)}) async-start(bf16[16,272,128]{2,1,0:T(8,128)(2,1)} %cut_items.1), calls=%async_computation.1 | async-start | bytes 2228224 | tf_op jit(solution)/shard_map/all_to_all | solution.py:437
  26.9 24.9 %all-gather.4 = s16[4096,256]{1,0:T(8,128)(2,1)S(1)} all-gather(s16[256,256]{1,0:T(8,128)(2,1)S(1)} %bitcast.61), channel_id=2, replica_groups=mesh['user'=16,'item'=16] {'item'}, dimensions={0}, use_global_device_ids=true | all-gather | bytes 2228224 | tf_op jit(solution)/shard_map/all_gather | solution.py:438
  51.8 4.4 %all-to-all-done.1.strips_ref = bf16[16,272,128]{2,1,0:T(8,128)(2,1)} async-done(((bf16[16,272,128]{2,1,0:T(8,128)(2,1)}), bf16[16,272,128]{2,1,0:T(8,128)(2,1)}, u32[]{:S(2)}, u32[]{:S(2)}) %all-to-all-start.1) | async-done | bytes 1114144 | tf_op jit(solution)/shard_map/all_to_all | solution.py:437
  56.3 6.8 %all-to-all-start.2 = ((bf16[16,272,128]{2,1,0:T(8,128)(2,1)}), bf16[16,272,128]{2,1,0:T(8,128)(2,1)}, u32[]{:S(2)}, u32[]{:S(2)}) async-start(bf16[16,272,128]{2,1,0:T(8,128)(2,1)} %cut_held.1), calls=%async_computation.2 | async-start | bytes 2228224 | tf_op jit(solution)/shard_map/all_to_all | solution.py:441
  63.1 2.6 %dense_items.1 = (f32[2048,128]{1,0:T(8,128)S(1)}, f32[2048,128]{1,0:T(8,128)S(1)}, f32[16,256]{1,0:T(8,128)S(1)}) custom-call(bf16[16,272,128]{2,1,0:T(8,128)(2,1)} %all-to-all-done.1.strips_ref), custom_call_target="tpu_custom_call" | custom-call | flops 400000000 | bytes 3000000 | tf_op jit(solution)/shard_map/dense_items/pallas_call | solution.py:173
  65.7 15.2 %solve_items.1 = f32[8,32,256]{2,1,0:T(8,128)S(1)} custom-call(f32[32,256]{1,0:T(8,128)S(1)} %dynamic-slice_bitcast_fusion.start_ref, f32[64,32,128]{2,1,0:T(8,128)S(1)} %bitcast.58, f32[64,32,128]{2,1,0:T(8,128)S(1)} %bitcast.59, f32[16,256]{1,0:T(8,128)S(1)} %get-tuple-element.25.step_ref, s32[1]{0:T(128)} %bitcast.20.core_ref, ...), custom_call_target="tpu_custom_call" | custom-call | flops 12000000000 | bytes 10000000 | tf_op jit(solution)/shard_map/solve_items/pallas_call | solution.py:317
  80.9 14.4 %all_to_all.25.rows_ref = f32[8,32,256]{2,1,0:T(8,128)} all-to-all(f32[8,32,256]{2,1,0:T(8,128)S(1)} %solve_items.1), channel_id=1, replica_groups={{0,32,64,96,128,160,192,224},{16,48,80,112,144,176,208,240},{1,33,65,97..., dimensions={0} | all-to-all | bytes 524288 | tf_op jit(solution)/shard_map/all_to_all | solution.py:451
  95.3 1.8 %pack_items.1 = s16[272,256]{1,0:T(8,128)(2,1)} custom-call(f32[8,32,256]{2,1,0:T(8,128)} %all_to_all.25.rows_ref), custom_call_target="tpu_custom_call" | custom-call | tf_op jit(solution)/shard_map/pack_items/pallas_call | solution.py:138
  97.0 22.3 %all-gather.5 = s16[4352,256]{1,0:T(8,128)(2,1)S(1)} all-gather(s16[272,256]{1,0:T(8,128)(2,1)} %pack_items.1), channel_id=3, replica_groups=mesh['user'=16,'item'=16] {'item'}, dimensions={0}, use_global_device_ids=true | all-gather | bytes 2367488 | tf_op jit(solution)/shard_map/all_gather | solution.py:452
  119.4 7.5 %collective-permute-start.2 = (s16[16,272,256]{2,1,0:T(8,128)(2,1)S(1)}, s16[16,272,256]{2,1,0:T(8,128)(2,1)S(1)}, u32[]{:S(2)}, u32[]{:S(2)}) collective-permute-start(s16[16,272,256]{2,1,0:T(8,128)(2,1)S(1)} %bitcast.44), channel_id=1, source_target_pairs={{0,16},{16,0},{32,48},{48,32},{64,80},{80,64},{96,112},{112,96},{1... | collective-permute-start | bytes 6684680 | tf_op jit(solution)/shard_map/ppermute | solution.py:453
  127.1 2.7 %dense_held.1 = (f32[1024,128]{1,0:T(8,128)S(1)}, f32[1024,128]{1,0:T(8,128)S(1)}, f32[16,256]{1,0:T(8,128)}) custom-call(bf16[16,272,128]{2,1,0:T(8,128)(2,1)} %all-to-all-done.2.strips_ref), custom_call_target="tpu_custom_call" | custom-call | flops 400000000 | bytes 3000000 | tf_op jit(solution)/shard_map/dense_held/pallas_call | solution.py:173
  129.9 0.9 collective-permute-done.2.other_ref
  130.8 12.0 %solve_held.1 = f32[16,16,256]{2,1,0:T(8,128)} custom-call(s32[1]{0:T(128)} %bitcast.20.core_ref, f32[64,16,128]{2,1,0:T(8,128)S(1)} %bitcast.50, f32[64,16,128]{2,1,0:T(8,128)S(1)} %bitcast.51, s16[16,272,256]{2,1,0:T(8,128)(2,1)S(1)} %bitcast.45, s16[16,272,256]{2,1,0:T(8,128)(2,1)S(1)} %collective-permute-done.2.other_ref), custom_call_target="tpu_custom_call" | custom-call | tf_op jit(solution)/shard_map/solve_held/pallas_call | solution.py:380
  142.9 4.1 %all-to-all-start.4 = ((f32[16,16,256]{2,1,0:T(8,128)}), f32[16,16,256]{2,1,0:T(8,128)S(1)}, u32[]{:S(2)}, u32[]{:S(2)}) async-start(f32[16,16,256]{2,1,0:T(8,128)} %solve_held.1), calls=%async_computation.4 | async-start | bytes 524288 | tf_op jit(solution)/shard_map/all_to_all | solution.py:455
  147.0 0.8 copy.19
  147.9 7.2 %all-to-all-done.4 = f32[16,16,256]{2,1,0:T(8,128)S(1)} async-done(((f32[16,16,256]{2,1,0:T(8,128)}), f32[16,16,256]{2,1,0:T(8,128)S(1)}, u32[]{:S(2)}, u32[]{:S(2)}) %all-to-all-start.4) | async-done | bytes 262176 | tf_op jit(solution)/shard_map/all_to_all | solution.py:455
  155.1 0.7 copy.20
  (29 shorter events, 1.7 us)
Async XLA Ops:
  0.6 55.6 %copy-start = (f32[512,256]{1,0:T(8,128)S(1)}, f32[512,256]{1,0:T(8,128)}, u32[]{:S(2)}) copy-start(f32[512,256]{1,0:T(8,128)} %param.11) | copy-start | bytes 1572868
  0.6 16.1 %copy-start.5 = (s32[1,1,16,2]{2,3,1,0:T(2,128)S(1)}, s32[1,1,16,2]{2,3,1,0:T(2,128)}, u32[]{:S(2)}) copy-start(s32[1,1,16,2]{2,3,1,0:T(2,128)} %param.12) | copy-start | bytes 388
  0.7 16.1 %copy-start.6 = (s32[1,1,16,2]{2,3,1,0:T(2,128)S(1)}, s32[1,1,16,2]{2,3,1,0:T(2,128)}, u32[]{:S(2)}) copy-start(s32[1,1,16,2]{2,3,1,0:T(2,128)} %param.13) | copy-start | bytes 388
  0.7 16.1 %copy-start.9 = (s32[1,1,16]{2,1,0:T(1,128)S(1)}, s32[1,1,16]{2,1,0:T(1,128)}, u32[]{:S(2)}) copy-start(s32[1,1,16]{2,1,0:T(1,128)} %param.14) | copy-start | bytes 196
  2.5 14.3 %copy-start.7 = (f32[1,256]{1,0:T(1,128)S(1)}, f32[1,256]{1,0:T(1,128)}, u32[]{:S(2)}) copy-start(f32[1,256]{1,0:T(1,128)} %get-tuple-element.17.extra_ref) | copy-start | bytes 3076
  2.5 16.9 %all-to-all-start = ((s16[8,32,256]{2,1,0:T(8,128)(2,1)}), s16[8,32,256]{2,1,0:T(8,128)(2,1)S(1)}, u32[]{:S(2)}, u32[]{:S(2)}) async-start(s16[8,32,256]{2,1,0:T(8,128)(2,1)} %get-tuple-element.18), calls=%async_computation | async-start | bytes 262144 | tf_op jit(solution)/shard_map/all_to_all | solution.py:423
  11.7 1.2 copy-start.1
  12.9 0.7 copy-start.3
  13.6 0.7 copy-start.4
  14.2 0.7 copy-start.8
  14.9 1.9 %copy-start.2 = (bf16[1,1,16,2,128,128]{5,4,3,2,1,0:T(8,128)(2,1)S(1)}, bf16[1,1,16,2,128,128]{5,4,3,2,1,0:T(8,128)(2,1)}, u32[]{:S(2)}) copy-start(bf16[1,1,16,2,128,128]{5,4,3,2,1,0:T(8,128)(2,1)} %param.15) | copy-start | bytes 3145732
  19.4 36.8 %all-to-all-start.1 = ((bf16[16,272,128]{2,1,0:T(8,128)(2,1)}), bf16[16,272,128]{2,1,0:T(8,128)(2,1)}, u32[]{:S(2)}, u32[]{:S(2)}) async-start(bf16[16,272,128]{2,1,0:T(8,128)(2,1)} %cut_items.1), calls=%async_computation.1 | async-start | bytes 2228224 | tf_op jit(solution)/shard_map/all_to_all | solution.py:437
  56.3 9.4 %collective-permute-start = (s16[16,256,256]{2,1,0:T(8,128)(2,1)S(1)}, s16[16,256,256]{2,1,0:T(8,128)(2,1)}, u32[]{:S(2)}, u32[]{:S(2)}) collective-permute-start(s16[16,256,256]{2,1,0:T(8,128)(2,1)S(1)} %bitcast.46), channel_id=1, source_target_pairs={{0,16},{16,0},{32,48},{48,32},{64,80},{80,64},{96,112},{112,96},{1... | collective-permute-start | bytes 6291464 | tf_op jit(solution)/shard_map/ppermute | solution.py:440
  56.3 24.6 %all-to-all-start.2 = ((bf16[16,272,128]{2,1,0:T(8,128)(2,1)}), bf16[16,272,128]{2,1,0:T(8,128)(2,1)}, u32[]{:S(2)}, u32[]{:S(2)}) async-start(bf16[16,272,128]{2,1,0:T(8,128)(2,1)} %cut_held.1), calls=%async_computation.2 | async-start | bytes 2228224 | tf_op jit(solution)/shard_map/all_to_all | solution.py:441
  95.3 31.6 %copy-start.10 = (f32[8,32,256]{2,1,0:T(8,128)S(1)}, f32[8,32,256]{2,1,0:T(8,128)}, u32[]{:S(2)}) copy-start(f32[8,32,256]{2,1,0:T(8,128)} %all_to_all.25.rows_ref) | copy-start | bytes 786436
  119.4 11.4 %collective-permute-start.2 = (s16[16,272,256]{2,1,0:T(8,128)(2,1)S(1)}, s16[16,272,256]{2,1,0:T(8,128)(2,1)S(1)}, u32[]{:S(2)}, u32[]{:S(2)}) collective-permute-start(s16[16,272,256]{2,1,0:T(8,128)(2,1)S(1)} %bitcast.44), channel_id=1, source_target_pairs={{0,16},{16,0},{32,48},{48,32},{64,80},{80,64},{96,112},{112,96},{1... | collective-permute-start | bytes 6684680 | tf_op jit(solution)/shard_map/ppermute | solution.py:453
  126.9 20.1 %collective-permute-start.1 = (f32[4,1,64,256]{3,2,0,1:T(8,128)S(1)}, f32[4,1,64,256]{3,2,0,1:T(8,128)S(1)}, u32[]{:S(2)}, u32[]{:S(2)}) collective-permute-start(f32[4,1,64,256]{3,2,0,1:T(8,128)S(1)} %copy_bitcast_fusion), channel_id=1, source_target_pairs={{0,16},{16,0},{32,48},{48,32},{64,80},{80,64},{96,112},{112,96},{1... | collective-permute-start | bytes 786440 | tf_op jit(solution)/shard_map/ppermute | solution.py:459
  142.9 12.2 %all-to-all-start.4 = ((f32[16,16,256]{2,1,0:T(8,128)}), f32[16,16,256]{2,1,0:T(8,128)S(1)}, u32[]{:S(2)}, u32[]{:S(2)}) async-start(f32[16,16,256]{2,1,0:T(8,128)} %solve_held.1), calls=%async_computation.4 | async-start | bytes 524288 | tf_op jit(solution)/shard_map/all_to_all | solution.py:455

commit v4 on v3

--- a/solution.py
+++ b/solution.py
@@ -13,6 +13,8 @@
 BL = 128
 SUB = 8
 GROUP = 32
+USER = ("z", "c")
+ITEM = ("y", "x")
 VMEM = 28 * 1024 * 1024
 
 i32 = jnp.int32
@@ -117,33 +119,6 @@
     )(place.reshape(1), outer, inner, count, tiles.reshape(-1, BL, BL), extra)
 
 
-def pack_items_kernel(rows_ref, out_ref):
-    peers, rows, rank = rows_ref.shape
-    blocks = rows // SUB
-    peak = jnp.max(jnp.max(jnp.abs(rows_ref[...]), axis=0), axis=0, keepdims=True)
-    exponent = column_exponents(peak)
-    inverse = power_of_two(-exponent)
-    for b in range(blocks):
-        for z in range(0, peers, 2):
-            pair = jnp.concatenate(
-                [rows_ref[z, b * SUB : (b + 1) * SUB, :], rows_ref[z + 1, b * SUB : (b + 1) * SUB, :]], axis=0
-            )
-            start = (b * peers + z) * SUB
-            out_ref[start : start + 2 * SUB, :] = fixed_point(pair, inverse).astype(jnp.int16)
-    out_ref[peers * rows :, :] = jnp.broadcast_to(exponent, (16, rank)).astype(jnp.int16)
-
-
-def pack_items(rows):
-    peers, count, rank = rows.shape
-    return pl.pallas_call(
-        pack_items_kernel,
-        out_shape=jax.ShapeDtypeStruct((peers * count + 16, rank), jnp.int16),
-        in_specs=[vspec()],
-        out_specs=vspec(),
-        name="pack_items",
-    )(rows)
-
-
 def dense_kernel(blocks, slots, strips_ref, ones_ref, right_ref, step_ref, wide_ref):
     sources, depth, _ = strips_ref.shape
     count = slots * SUB
@@ -217,12 +192,10 @@
     return jnp.concatenate([ref[first + k] for k in range(count)], axis=1)
 
 
-def high_part(codes):
-    return (codes & -256).astype(f32)
-
-
-def low_part(codes):
-    return (codes & 255).astype(f32)
+def split(codes, step):
+    value = codes.astype(f32) * step
+    upper = value.astype(bf16)
+    return upper, (value - upper.astype(f32)).astype(bf16)
 
 
 def iterate(ones_ref, factors_ref, residual, start):
@@ -270,12 +243,11 @@
         norm_now = norm_next
 
 
-def item_kernel(chips, start_ref, ones_ref, right_ref, step_ref, core_ref, own_ref, other_ref, out_ref, factors_ref, total_ref):
+def item_kernel(start_ref, ones_ref, right_ref, step_ref, core_ref, own_ref, other_ref, out_ref, factors_ref, total_ref):
     g = pl.program_id(0)
-    sources, depth, rank = own_ref.shape
-    part = depth // chips
+    sources, chips, part, rank = own_ref.shape
     per = BL // part
-    group = sources * 2 * depth
+    group = sources * 2 * chips * part
     core = core_ref[0]
 
     @pl.when(g == 0)
@@ -286,11 +258,10 @@
         for z in range(chips):
             step = step_ref[pl.ds(2 * z + which, 1), :]
             for k in range(sources):
-                codes = ref[k, z * part : (z + 1) * part, :].astype(i32)
+                codes = ref[k, z].astype(i32)
                 start = g * group + (k // per * 2 * chips + 2 * z + which) * BL + k % per * part
                 rows = pl.ds(pl.multiple_of(start, part), part)
-                factors_ref[rows, :rank] = (high_part(codes) * step).astype(bf16)
-                factors_ref[rows, rank:] = (low_part(codes) * step).astype(bf16)
+                factors_ref[rows, :rank], factors_ref[rows, rank:] = split(codes, step)
     factors = factors_ref[pl.ds(pl.multiple_of(g * group, group), group), :]
     count = group // BL
     score = scores(twice(two_planes(start_ref[...])), factors)
@@ -301,23 +272,30 @@
     def _():
         start = start_ref[...]
         found = iterate(ones_ref, factors_ref, join(total_ref[...]) - LAM * start, start)
+        exponent = column_exponents(jnp.max(jnp.abs(found), axis=0, keepdims=True))
+        codes = fixed_point(found, power_of_two(-exponent)).astype(jnp.int16)
+        exponents = jnp.broadcast_to(exponent, (16, rank)).astype(jnp.int16)[:SUB]
         for d in range(out_ref.shape[0]):
-            out_ref[d] = found
+            out_ref[d, : found.shape[0], :] = codes
+            out_ref[d, found.shape[0] :, :] = exponents
+
+
+def gathered_spec(shape, grid):
+    return pl.BlockSpec((shape[0] // grid,) + shape[1:], lambda s: (s, 0, 0, 0))
 
 
 def solve_items(start, ones, right, step, core, own, other, copies):
-    sources, depth, rank = own.shape
-    rows = start.shape[0]
-    whole = 2 * depth * sources
+    rows, rank = start.shape
+    whole = 2 * own.size // rank
     grid = whole // (GROUP * BL)
     ones = ones.reshape(-1, rows, BL)
     right = right.reshape(-1, rows, BL)
     fixed3 = pl.BlockSpec(ones.shape, lambda s: (0, 0, 0), pipeline_mode=pl.Buffered(1))
-    codes = pl.BlockSpec((sources // grid, depth, rank), lambda s: (s, 0, 0))
+    codes = gathered_spec(own.shape, grid)
     return pl.pallas_call(
-        functools.partial(item_kernel, copies),
+        item_kernel,
         grid=(grid,),
-        out_shape=jax.ShapeDtypeStruct((copies, rows, rank), f32),
+        out_shape=jax.ShapeDtypeStruct((copies, rows + SUB, rank), jnp.int16),
         in_specs=[
             pl.BlockSpec((rows, rank), lambda s: (0, 0)),
             fixed3,
@@ -327,7 +305,7 @@
             codes,
             codes,
         ],
-        out_specs=pl.BlockSpec((copies, rows, rank), lambda s: (0, 0, 0)),
+        out_specs=pl.BlockSpec((copies, rows + SUB, rank), lambda s: (0, 0, 0)),
         scratch_shapes=[pltpu.VMEM((whole, 2 * rank), bf16), pltpu.VMEM((2 * rows, 2 * rank), f32)],
         compiler_params=params(),
         cost_estimate=pl.CostEstimate(flops=12 * 10**9, bytes_accessed=10**7, transcendentals=0),
@@ -335,58 +313,56 @@
     )(start, ones, right, step, core, own, other)
 
 
-def held_kernel(core_ref, ones_ref, right_ref, own_ref, other_ref, out_ref, factors_ref, total_ref):
-    g = pl.program_id(0)
-    sources, depth, rank = own_ref.shape
-    half = depth - 16
-    lanes = BL // 2
-    blocks = half // lanes
-    group = sources * 2 * half
-    core = core_ref[0]
-
-    @pl.when(g == 0)
-    def _():
-        total_ref[...] = jnp.zeros_like(total_ref)
-
-    for s in range(sources):
+def held_kernel(place_ref, ones_ref, right_ref, own_ref, other_ref, out_ref, items_ref, factors_ref):
+    sources, chips, depth, rank = own_ref.shape
+    part = depth - SUB
+    blocks = part // SUB
+    shard = blocks * BL
+    group = GROUP * BL
+    core = place_ref[0]
+
+    def decode(o, carry):
         for ref, which in ((own_ref, core), (other_ref, 1 - core)):
-            step = power_of_two(ref[s, half : half + 16, :].astype(i32)[:1])
-            for b in range(blocks):
-                codes = ref[s, b * lanes : (b + 1) * lanes, :].astype(i32)
-                start = g * group + (s * blocks + b) * BL + which * lanes
-                rows = pl.ds(pl.multiple_of(start, lanes), lanes)
-                factors_ref[rows, :rank] = (high_part(codes) * step).astype(bf16)
-                factors_ref[rows, rank:] = (low_part(codes) * step).astype(bf16)
-    factors = factors_ref[pl.ds(pl.multiple_of(g * group, group), group), :]
-    count = group // BL
-    total_ref[...] += combine(columns(right_ref, g * count, count), factors)
-
-    @pl.when(g == pl.num_programs(0) - 1)
-    def _():
-        residual = join(total_ref[...])
-        found = iterate(ones_ref, factors_ref, residual, jnp.zeros_like(residual))
-        for d in range(out_ref.shape[0]):
-            out_ref[d] = found
-
-
-def solve_held(core, ones, right, own, other, rows, copies):
-    sources, depth, rank = own.shape
-    whole = 2 * (depth - 16) * sources
-    grid = whole // (GROUP * BL)
-    ones = ones.reshape(-1, rows, BL)
-    right = right.reshape(-1, rows, BL)
-    fixed3 = pl.BlockSpec(ones.shape, lambda s: (0, 0, 0), pipeline_mode=pl.Buffered(1))
-    codes = pl.BlockSpec((sources // grid, depth, rank), lambda s: (s, 0, 0))
+            exponents = [ref[o, z, part:depth, :].astype(i32)[:1] for z in range(chips)]
+            step = power_of_two(jnp.concatenate(exponents, axis=0))
+            for z in range(0, chips, 2):
+                codes = [ref[o, n, :part, :].astype(i32).astype(f32) * step[n : n + 1] for n in (z, z + 1)]
+                for b in range(blocks):
+                    start = o * shard + b * BL + which * (BL // 2) + z * SUB
+                    rows = pl.ds(pl.multiple_of(start, 2 * SUB), 2 * SUB)
+                    span = slice(b * SUB, (b + 1) * SUB)
+                    value = jnp.concatenate([codes[0][span], codes[1][span]], axis=0)
+                    upper = value.astype(bf16)
+                    factors_ref[rows, :rank] = upper
+                    factors_ref[rows, rank:] = (value - upper.astype(f32)).astype(bf16)
+        return carry
+
+    lax.fori_loop(0, sources, decode, 0, unroll=4)
+    total = jnp.zeros((2 * out_ref.shape[1], 2 * rank), f32)
+    for g in range(factors_ref.shape[0] // group):
+        factors = factors_ref[g * group : (g + 1) * group, :]
+        total = total + combine(columns(right_ref, g * GROUP, GROUP), factors)
+    mine = factors_ref[pl.ds(pl.multiple_of(place_ref[1] * shard, shard), shard), :]
+    items_ref[...] = mine[:, :rank].astype(f32) + mine[:, rank:].astype(f32)
+    residual = join(total)
+    found = iterate(ones_ref, factors_ref, residual, jnp.zeros_like(residual))
+    for d in range(out_ref.shape[0]):
+        out_ref[d] = found
+
+
+def solve_held(place, ones, right, own, other, rows, copies):
+    sources, chips, depth, rank = own.shape
+    whole = 2 * sources * chips * (depth - SUB)
+    shard = whole // sources
     return pl.pallas_call(
         held_kernel,
-        grid=(grid,),
-        out_shape=jax.ShapeDtypeStruct((copies, rows, rank), f32),
-        in_specs=[pl.BlockSpec(memory_space=pltpu.SMEM), fixed3, fixed3, codes, codes],
-        out_specs=pl.BlockSpec((copies, rows, rank), lambda s: (0, 0, 0)),
-        scratch_shapes=[pltpu.VMEM((whole, 2 * rank), bf16), pltpu.VMEM((2 * rows, 2 * rank), f32)],
+        out_shape=(jax.ShapeDtypeStruct((copies, rows, rank), f32), jax.ShapeDtypeStruct((shard, rank), f32)),
+        in_specs=[pl.BlockSpec(memory_space=pltpu.SMEM), vspec(), vspec(), vspec(), vspec()],
+        out_specs=(vspec(), vspec()),
+        scratch_shapes=[pltpu.VMEM((whole, 2 * rank), bf16)],
         compiler_params=params(),
         name="solve_held",
-    )(core, ones, right, own, other)
+    )(place, ones.reshape(-1, rows, BL), right.reshape(-1, rows, BL), own, other)
 
 
 def shards(
@@ -402,25 +378,22 @@
     held_conf,
 ):
     rank = user_factors.shape[1]
-    peers = lax.axis_size("user")
-    item_peers = lax.axis_size("item")
-    chips = peers // 2
-    me = lax.axis_index("user")
-    core = me % 2
-    chip = me // 2
+    chips = lax.axis_size("z")
+    core = lax.axis_index("c")
+    chip = lax.axis_index("z")
+    me = lax.axis_index(USER)
+    column = lax.axis_index(ITEM)
+    peers, item_peers = lax.axis_size(USER), lax.axis_size(ITEM)
     slots = tile_user.shape[-1]
     held_slots = held_user.shape[-1]
     user_blocks = user_factors.shape[0] // BL
     item_blocks = item_factors.shape[0] // BL
     held_blocks = 2
-
-    same_core = [[c + 2 * z for z in range(chips)] for c in range(2)]
-    siblings = [(d, d ^ 1) for d in range(peers)]
+    siblings = [(0, 1), (1, 0)]
 
     part = user_factors.shape[0] // item_peers
-    column = lax.axis_index("item")
     piece, exponent = pack_users(user_factors, column, chips, part)
-    piece = lax.all_to_all(piece, "user", 0, 0, tiled=True, axis_index_groups=same_core).reshape(chips * part, rank)
+    piece = lax.all_to_all(piece, "z", 0, 0, tiled=True)
 
     blocks = peers * user_blocks * item_blocks
     order = [c * chips + z for z in range(chips) for c in range(2)]
@@ -434,11 +407,11 @@
         False, list(range(item_peers)), (1, item_blocks), held_blocks, held_all, "cut_held",
     )
     strips, held_strips, piece = lax.optimization_barrier((strips, held_strips, piece))
-    strips = lax.all_to_all(strips, "user", 0, 0, tiled=True)
-    own_users = lax.all_gather(piece, "item", axis=0, tiled=False)
+    strips = lax.all_to_all(strips, USER, 0, 0, tiled=True)
+    own_users = lax.all_gather(piece, ITEM, axis=0, tiled=False)
     strips, own_users, held_strips = lax.optimization_barrier((strips, own_users, held_strips))
-    other_users = lax.ppermute(own_users, "user", siblings)
-    held_strips = lax.all_to_all(held_strips, "item", 0, 0, tiled=True)
+    other_users = lax.ppermute(own_users, "c", siblings)
+    held_strips = lax.all_to_all(held_strips, ITEM, 0, 0, tiled=True)
     ones, right, step = dense(strips, blocks, peers * slots, "dense_items")
 
     start = lax.dynamic_slice_in_dim(
@@ -448,33 +421,30 @@
     mine, held_strips = lax.optimization_barrier((mine, held_strips))
     held_ones, held_right, _ = dense(held_strips, held_all, item_peers * held_slots, "dense_held")
 
-    half = lax.all_to_all(mine, "user", 0, 0, tiled=True, axis_index_groups=same_core)
-    own = lax.all_gather(pack_items(half), "item", axis=0, tiled=False)
-    other = lax.ppermute(own, "user", siblings)
-    folded = solve_held(core.reshape(1), held_ones, held_right, own, other, held_blocks * SUB, item_peers)
-    folded = lax.all_to_all(folded, "item", 0, 0, tiled=True)
+    mine = lax.all_to_all(mine, "z", 0, 0, tiled=True)
+    own = lax.all_gather(mine, ITEM, axis=0, tiled=False)
+    other = lax.ppermute(own, "c", siblings)
+    folded, new_items = solve_held(
+        jnp.stack([core, column]), held_ones, held_right, own, other, held_blocks * SUB, item_peers
+    )
+    folded = lax.all_to_all(folded, ITEM, 0, 0, tiled=True)
     folded = folded.reshape(item_peers, held_blocks, SUB, rank).transpose(1, 0, 2, 3).reshape(-1, rank)
-
-    half = half.reshape(chips, item_blocks, SUB, rank).transpose(1, 0, 2, 3).reshape(item_blocks, 1, BL // 2, rank)
-    sibling = lax.ppermute(half, "user", siblings)
-    new_items = jnp.where(
-        core == 0, jnp.concatenate([half, sibling], axis=1), jnp.concatenate([sibling, half], axis=1)
-    ).reshape(-1, rank)
     return new_items, folded
 
 
 def solution(mesh):
+    split = jax.sharding.Mesh(mesh.devices.reshape(mesh.shape["user"] // 2, 2, -1, 4), ("z", "c", "y", "x"))
     in_specs = (
-        P("user", None),
-        P("item", None),
-        P("item", "user", None, None),
-        P("item", "user", None, None),
-        P("item", "user", None),
-        P("item", "user", None, None, None, None),
-        P("user", "item", None, None),
-        P("user", "item", None, None),
-        P("user", "item", None),
-        P("user", "item", None, None, None, None),
+        P(USER, None),
+        P(ITEM, None),
+        P(ITEM, USER, None, None),
+        P(ITEM, USER, None, None),
+        P(ITEM, USER, None),
+        P(ITEM, USER, None, None, None, None),
+        P(USER, ITEM, None, None),
+        P(USER, ITEM, None, None),
+        P(USER, ITEM, None),
+        P(USER, ITEM, None, None, None, None),
     )
-    out_specs = (P("item", None), P("user", None))
-    return jax.shard_map(shards, mesh=mesh, in_specs=in_specs, out_specs=out_specs, check_vma=False)
+    out_specs = (P(ITEM, None), P(USER, None))
+    return jax.shard_map(shards, mesh=split, in_specs=in_specs, out_specs=out_specs, check_vma=False)

time: 157 us -> 153 us (0.975)
  blocking collectives: 61.6 us -> 73.5 us
  waiting for transfers between devices: 13.3 us -> 6.93 us
  starting transfers between devices: 35.3 us -> 29.8 us
  Pallas kernels: 39.9 us -> 37.7 us
    all_to_all x1 -> x2, blocking collectives: 14.4 us -> 25.2 us  [the longest x1 12.8 us: shards(): mine = lax.all_to_all(mine, 'z', 0, 0, tiled=True)]
    all_to_all x4 -> x3, waiting for transfers between devices: 12.4 us -> 5.21 us  [the longest x1 4.45 us: shards(): strips = lax.all_to_all(strips, USER, 0, 0, tiled=True)]
    all_to_all x4 -> x3, starting transfers between devices: 27.5 us -> 23.4 us  [the longest x1 9.15 us: shards(): piece = lax.all_to_all(piece, 'z', 0, 0, tiled=True)]
    pallas_call x3 -> x2, Pallas kernels: 29 us -> 26.8 us  [the longest x1 14.8 us: solve_items(): pl.pallas_call(item_kernel, grid=(grid,), out_shape=jax.ShapeDtypeStruct(...]
    ppermute x3 -> x2, starting transfers between devices: 7.75 us -> 6.45 us  [the longest x1 6.45 us: shards(): other = lax.ppermute(own, 'c', siblings)]
    unnamed x22 -> x20, local copies, waits for them, and re-layouts: 3.26 us -> 3.26 us
  transfers between devices with their start and end apart: 7 -> 5, of which waited for: 4 -> 3; matrix products, arithmetic and copies ran while one was open for 1% -> 0% of each run, Pallas kernels for 23% -> 16%
where the time goes in v4:
time: 153 us
  blocking collectives  73.5 us (48%)
  Pallas kernels  37.7 us (25%)
  starting transfers between devices  29.8 us (19%)
  waiting for transfers between devices  6.93 us (5%)
  local copies, waits for them, and re-layouts  3.99 us (3%)
    all_gather x1, blocking collectives, shards(): own_users = lax.all_gather(piece, ITEM, axis=0, tiled=False)  24.9 us
    all_gather x1, blocking collectives, shards(): own = lax.all_gather(mine, ITEM, axis=0, tiled=False)  23.4 us
    pallas_call x1, Pallas kernels, solve_items(): pl.pallas_call(item_kernel, grid=(grid,), out_shape=jax.ShapeDtypeStruct(...  14.8 us
    all_to_all x1, blocking collectives, shards(): mine = lax.all_to_all(mine, 'z', 0, 0, tiled=True)  12.8 us
    all_to_all x1, blocking collectives, shards(): folded = lax.all_to_all(folded, ITEM, 0, 0, tiled=True)  12.4 us
    pallas_call x1, Pallas kernels, solve_held(): pl.pallas_call(held_kernel, out_shape=(jax.ShapeDtypeStruct((copies, rows...  12 us
    all_to_all x1, starting transfers between devices, shards(): piece = lax.all_to_all(piece, 'z', 0, 0, tiled=True)  9.15 us
    all_to_all x1, starting transfers between devices, shards(): strips = lax.all_to_all(strips, USER, 0, 0, tiled=True)  7.41 us
  transfers between devices with their start and end apart: 5, of which 3 were waited for; matrix products, arithmetic and copies ran while one was open for 0% of the time, Pallas kernels for 16%

profile of v4, /device:TPU:1, one launch (start us, length us, event | category | flops | bytes accessed | tf_op | source)
XLA Modules:
  0.0 152.8 jit_solution(6448689418349451792)
XLA Ops:
  0.7 1.8 %pack_users.1 = (s16[8,32,256]{2,1,0:T(8,128)(2,1)}, f32[1,256]{1,0:T(1,128)}) custom-call(s32[1]{0:T(128)} %bitcast.1.place_ref, f32[512,256]{1,0:T(8,128)} %rows_ref.1), custom_call_target="tpu_custom_call" | custom-call | tf_op jit(solution)/shard_map/pack_users/pallas_call | solution.py:68
  2.5 9.1 %all-to-all-start = ((s16[8,32,256]{2,1,0:T(8,128)(2,1)}), s16[8,32,256]{2,1,0:T(8,128)(2,1)S(1)}, u32[]{:S(2)}, u32[]{:S(2)}) async-start(s16[8,32,256]{2,1,0:T(8,128)(2,1)} %get-tuple-element.20), calls=%async_computation | async-start | bytes 262144 | tf_op jit(solution)/shard_map/all_to_all | solution.py:396
  11.7 1.2 copy-done.1
  12.9 0.7 copy-done.3
  13.6 0.7 copy-done.4
  14.3 0.7 copy-done.8
  14.9 1.8 %cut_held.1 = bf16[16,272,128]{2,1,0:T(8,128)(2,1)} custom-call(s32[1]{0:T(128)} %bitcast.1.place_ref, s32[2,16]{1,0:T(2,128)S(1)} %bitcast.43, s32[2,16]{1,0:T(2,128)S(1)} %bitcast.44, s32[16]{0:T(128)S(1)} %bitcast.47, bf16[32,128,128]{2,1,0:T(8,128)(2,1)S(1)} %bitcast.39, f32[1,256]{1,0:T(1,128)S(1)} %broadcast_in_dim.3.extra_ref), custom_call_target="tpu_custom_call" | custom-call | flops 1000000 | bytes 2000000 | tf_op jit(solution)/shard_map/cut_held/pallas_call | solution.py:111
  16.8 1.9 %cut_items.1 = bf16[16,272,128]{2,1,0:T(8,128)(2,1)} custom-call(s32[1]{0:T(128)} %bitcast.4.place_ref, s32[2,16]{1,0:T(2,128)S(1)} %bitcast.45, s32[2,16]{1,0:T(2,128)S(1)} %bitcast.46, s32[16]{0:T(128)S(1)} %bitcast.48, bf16[32,128,128]{2,1,0:T(8,128)(2,1)S(1)} %bitcast.40, f32[1,256]{1,0:T(1,128)S(1)} %copy-done.7), custom_call_target="tpu_custom_call" | custom-call | flops 1000000 | bytes 2000000 | tf_op jit(solution)/shard_map/cut_items/pallas_call | solution.py:111
  18.7 0.8 all-to-all-done
  19.4 7.4 %all-to-all-start.1 = ((bf16[16,272,128]{2,1,0:T(8,128)(2,1)}), bf16[16,272,128]{2,1,0:T(8,128)(2,1)}, u32[]{:S(2)}, u32[]{:S(2)}) async-start(bf16[16,272,128]{2,1,0:T(8,128)(2,1)} %cut_items.1), calls=%async_computation.1 | async-start | bytes 2228224 | tf_op jit(solution)/shard_map/all_to_all | solution.py:410
  26.8 24.9 %all-gather.4 = s16[128,32,256]{2,1,0:T(8,128)(2,1)S(1)} all-gather(s16[8,32,256]{2,1,0:T(8,128)(2,1)S(1)} %all-to-all-done), channel_id=2, replica_groups=mesh['z'=8,'c'=2,'y'=4,'x'=4] {'y','x'}, dimensions={0}, use_global_device_ids=true | all-gather | bytes 2228224 | tf_op jit(solution)/shard_map/all_gather | solution.py:411
  51.7 4.4 %all-to-all-done.1.strips_ref = bf16[16,272,128]{2,1,0:T(8,128)(2,1)} async-done(((bf16[16,272,128]{2,1,0:T(8,128)(2,1)}), bf16[16,272,128]{2,1,0:T(8,128)(2,1)}, u32[]{:S(2)}, u32[]{:S(2)}) %all-to-all-start.1) | async-done | bytes 1114144 | tf_op jit(solution)/shard_map/all_to_all | solution.py:410
  56.2 6.8 %all-to-all-start.2 = ((bf16[16,272,128]{2,1,0:T(8,128)(2,1)}), bf16[16,272,128]{2,1,0:T(8,128)(2,1)}, u32[]{:S(2)}, u32[]{:S(2)}) async-start(bf16[16,272,128]{2,1,0:T(8,128)(2,1)} %cut_held.1), calls=%async_computation.2 | async-start | bytes 2228224 | tf_op jit(solution)/shard_map/all_to_all | solution.py:414
  63.0 2.6 %dense_items.1 = (f32[2048,128]{1,0:T(8,128)S(1)}, f32[2048,128]{1,0:T(8,128)S(1)}, f32[16,256]{1,0:T(8,128)S(1)}) custom-call(bf16[16,272,128]{2,1,0:T(8,128)(2,1)} %all-to-all-done.1.strips_ref), custom_call_target="tpu_custom_call" | custom-call | flops 400000000 | bytes 3000000 | tf_op jit(solution)/shard_map/dense_items/pallas_call | solution.py:148
  65.6 14.8 %solve_items.1 = s16[8,40,256]{2,1,0:T(8,128)(2,1)S(1)} custom-call(f32[32,256]{1,0:T(8,128)S(1)} %dynamic-slice_bitcast_fusion.start_ref, f32[64,32,128]{2,1,0:T(8,128)S(1)} %bitcast.49, f32[64,32,128]{2,1,0:T(8,128)S(1)} %bitcast.50, f32[16,256]{1,0:T(8,128)S(1)} %get-tuple-element.27.step_ref, s32[1]{0:T(128)} %bitcast.core_ref, ...), custom_call_target="tpu_custom_call" | custom-call | flops 12000000000 | bytes 10000000 | tf_op jit(solution)/shard_map/solve_items/pallas_call | solution.py:295
  80.5 12.8 %all_to_all.25 = s16[8,40,256]{2,1,0:T(8,128)(2,1)S(1)} all-to-all(s16[8,40,256]{2,1,0:T(8,128)(2,1)S(1)} %solve_items.1), channel_id=1, replica_groups=mesh['z'=8,'c'=2,'y'=4,'x'=4] {'z'}, dimensions={0} | all-to-all | bytes 327680 | tf_op jit(solution)/shard_map/all_to_all | solution.py:424
  93.3 23.4 %all-gather.5 = s16[128,40,256]{2,1,0:T(8,128)(2,1)S(1)} all-gather(s16[8,40,256]{2,1,0:T(8,128)(2,1)S(1)} %all_to_all.25), channel_id=3, replica_groups=mesh['z'=8,'c'=2,'y'=4,'x'=4] {'y','x'}, dimensions={0}, use_global_device_ids=true | all-gather | bytes 2785280 | tf_op jit(solution)/shard_map/all_gather | solution.py:425
  116.7 6.5 %collective-permute-start.1 = (s16[16,8,40,256]{3,2,1,0:T(8,128)(2,1)S(1)}, s16[16,8,40,256]{3,2,1,0:T(8,128)(2,1)S(1)}, u32[]{:S(2)}, u32[]{:S(2)}) collective-permute-start(s16[16,8,40,256]{3,2,1,0:T(8,128)(2,1)S(1)} %bitcast.35), channel_id=1, source_target_pairs={{0,16},{16,0},{1,17},{17,1},{2,18},{18,2},{3,19},{19,3},{4,20},{20... | collective-permute-start | bytes 7864328 | tf_op jit(solution)/shard_map/ppermute | solution.py:426
  123.1 0.1 pad_add_fusion.place_ref
  123.2 2.7 %dense_held.1 = (f32[1024,128]{1,0:T(8,128)S(1)}, f32[1024,128]{1,0:T(8,128)S(1)}, f32[16,256]{1,0:T(8,128)}) custom-call(bf16[16,272,128]{2,1,0:T(8,128)(2,1)} %all-to-all-done.2.strips_ref), custom_call_target="tpu_custom_call" | custom-call | flops 400000000 | bytes 3000000 | tf_op jit(solution)/shard_map/dense_held/pallas_call | solution.py:148
  126.0 1.7 %collective-permute-done.1.other_ref = s16[16,8,40,256]{3,2,1,0:T(8,128)(2,1)S(1)} collective-permute-done((s16[16,8,40,256]{3,2,1,0:T(8,128)(2,1)S(1)}, s16[16,8,40,256]{3,2,1,0:T(8,128)(2,1)S(1)}, u32[]{:S(2)}, u32[]{:S(2)}) %collective-permute-start.1) | collective-permute-done | bytes 2621472 | tf_op jit(solution)/shard_map/ppermute | solution.py:426
  127.7 12.0 %solve_held.1 = (f32[16,16,256]{2,1,0:T(8,128)S(1)}, f32[512,256]{1,0:T(8,128)}) custom-call(s32[2]{0:T(128)S(1)} %pad_add_fusion.place_ref, f32[64,16,128]{2,1,0:T(8,128)S(1)} %bitcast.41, f32[64,16,128]{2,1,0:T(8,128)S(1)} %bitcast.42, s16[16,8,40,256]{3,2,1,0:T(8,128)(2,1)S(1)} %bitcast.36, s16[16,8,40,256]{3,2,1,0:T(8,128)(2,1)S(1)} %collective-permute-done.1.other_ref), custom_call_target="tpu_custom_call" | custom-call | tf_op jit(solution)/shard_map/solve_held/pallas_call | solution.py:357
  139.7 12.4 %all_to_all.26 = f32[16,16,256]{2,1,0:T(8,128)S(1)} all-to-all(f32[16,16,256]{2,1,0:T(8,128)S(1)} %get-tuple-element.35), channel_id=1, replica_groups=mesh['z'=8,'c'=2,'y'=4,'x'=4] {'y','x'}, dimensions={0} | all-to-all | bytes 524288 | tf_op jit(solution)/shard_map/all_to_all | solution.py:430
  152.1 0.7 copy.15
  (21 shorter events, 0.1 us)
Async XLA Ops:
  0.6 55.6 %copy-start = (f32[512,256]{1,0:T(8,128)S(1)}, f32[512,256]{1,0:T(8,128)}, u32[]{:S(2)}) copy-start(f32[512,256]{1,0:T(8,128)} %param.11) | copy-start | bytes 1572868
  0.6 16.1 %copy-start.9 = (s32[1,1,16]{2,1,0:T(1,128)S(1)}, s32[1,1,16]{2,1,0:T(1,128)}, u32[]{:S(2)}) copy-start(s32[1,1,16]{2,1,0:T(1,128)} %param.14) | copy-start | bytes 196
  0.7 16.1 %copy-start.6 = (s32[1,1,16,2]{2,3,1,0:T(2,128)S(1)}, s32[1,1,16,2]{2,3,1,0:T(2,128)}, u32[]{:S(2)}) copy-start(s32[1,1,16,2]{2,3,1,0:T(2,128)} %param.13) | copy-start | bytes 388
  0.7 16.1 %copy-start.5 = (s32[1,1,16,2]{2,3,1,0:T(2,128)S(1)}, s32[1,1,16,2]{2,3,1,0:T(2,128)}, u32[]{:S(2)}) copy-start(s32[1,1,16,2]{2,3,1,0:T(2,128)} %param.12) | copy-start | bytes 388
  2.5 14.2 %copy-start.7 = (f32[1,256]{1,0:T(1,128)S(1)}, f32[1,256]{1,0:T(1,128)}, u32[]{:S(2)}) copy-start(f32[1,256]{1,0:T(1,128)} %get-tuple-element.19.extra_ref) | copy-start | bytes 3076
  2.5 16.9 %all-to-all-start = ((s16[8,32,256]{2,1,0:T(8,128)(2,1)}), s16[8,32,256]{2,1,0:T(8,128)(2,1)S(1)}, u32[]{:S(2)}, u32[]{:S(2)}) async-start(s16[8,32,256]{2,1,0:T(8,128)(2,1)} %get-tuple-element.20), calls=%async_computation | async-start | bytes 262144 | tf_op jit(solution)/shard_map/all_to_all | solution.py:396
  11.7 1.2 copy-start.1
  12.9 0.7 copy-start.3
  13.6 0.7 copy-start.4
  14.2 0.7 copy-start.8
  14.9 1.9 %copy-start.2 = (bf16[1,1,16,2,128,128]{5,4,3,2,1,0:T(8,128)(2,1)S(1)}, bf16[1,1,16,2,128,128]{5,4,3,2,1,0:T(8,128)(2,1)}, u32[]{:S(2)}) copy-start(bf16[1,1,16,2,128,128]{5,4,3,2,1,0:T(8,128)(2,1)} %param.15) | copy-start | bytes 3145732
  19.4 36.8 %all-to-all-start.1 = ((bf16[16,272,128]{2,1,0:T(8,128)(2,1)}), bf16[16,272,128]{2,1,0:T(8,128)(2,1)}, u32[]{:S(2)}, u32[]{:S(2)}) async-start(bf16[16,272,128]{2,1,0:T(8,128)(2,1)} %cut_items.1), calls=%async_computation.1 | async-start | bytes 2228224 | tf_op jit(solution)/shard_map/all_to_all | solution.py:410
  56.2 9.4 %collective-permute-start = (s16[16,8,32,256]{3,2,1,0:T(8,128)(2,1)S(1)}, s16[16,8,32,256]{3,2,1,0:T(8,128)(2,1)}, u32[]{:S(2)}, u32[]{:S(2)}) collective-permute-start(s16[16,8,32,256]{3,2,1,0:T(8,128)(2,1)S(1)} %bitcast.37), channel_id=1, source_target_pairs={{0,16},{16,0},{1,17},{17,1},{2,18},{18,2},{3,19},{19,3},{4,20},{20... | collective-permute-start | bytes 6291464 | tf_op jit(solution)/shard_map/ppermute | solution.py:413
  56.2 24.3 %all-to-all-start.2 = ((bf16[16,272,128]{2,1,0:T(8,128)(2,1)}), bf16[16,272,128]{2,1,0:T(8,128)(2,1)}, u32[]{:S(2)}, u32[]{:S(2)}) async-start(bf16[16,272,128]{2,1,0:T(8,128)(2,1)} %cut_held.1), calls=%async_computation.2 | async-start | bytes 2228224 | tf_op jit(solution)/shard_map/all_to_all | solution.py:414
  116.7 11.0 %collective-permute-start.1 = (s16[16,8,40,256]{3,2,1,0:T(8,128)(2,1)S(1)}, s16[16,8,40,256]{3,2,1,0:T(8,128)(2,1)S(1)}, u32[]{:S(2)}, u32[]{:S(2)}) collective-permute-start(s16[16,8,40,256]{3,2,1,0:T(8,128)(2,1)S(1)} %bitcast.35), channel_id=1, source_target_pairs={{0,16},{16,0},{1,17},{17,1},{2,18},{18,2},{3,19},{19,3},{4,20},{20... | collective-permute-start | bytes 7864328 | tf_op jit(solution)/shard_map/ppermute | solution.py:426

commit v5 on v4

--- a/solution.py
+++ b/solution.py
@@ -136,11 +136,13 @@
     named = named.astype(bf16)
     for s in range(sources):
         wide_ref[s * count : (s + 1) * count, :] = strips_ref[s, :count, :].astype(f32)
-    for r in range(SUB):
-        rows = wide_ref[pl.ds(r, sources * slots, stride=SUB), :].astype(bf16)
-        total = jnp.dot(named, rows, preferred_element_type=f32)
-        ones_ref[pl.ds(r, blocks, stride=SUB), :] = total + 1.0
-        right_ref[pl.ds(r, blocks, stride=SUB), :] = total + live
+    for r in range(0, SUB, 2):
+        rows = [wide_ref[pl.ds(r + k, sources * slots, stride=SUB), :].astype(bf16) for k in range(2)]
+        both = jnp.dot(named, jnp.concatenate(rows, axis=1), preferred_element_type=f32)
+        for k in range(2):
+            total = both[:, k * BL : (k + 1) * BL]
+            ones_ref[pl.ds(r + k, blocks, stride=SUB), :] = total + 1.0
+            right_ref[pl.ds(r + k, blocks, stride=SUB), :] = total + live
 
 
 def dense(strips, blocks, slots, name):
@@ -203,30 +205,23 @@
     group = GROUP * BL
     steps = factors_ref.shape[0] // group
 
-    def part(g, planes):
-        factors = factors_ref[pl.ds(pl.multiple_of(g * group, group), group), :]
-        score = scores(planes, factors)
-        return score, columns(ones_ref, g * GROUP, GROUP) * score, factors
-
     def operator(direction):
         planes = twice(two_planes(direction))
 
         def step(g, total):
-            _, weighted, factors = part(g, planes)
+            factors = factors_ref[pl.ds(pl.multiple_of(g * group, group), group), :]
+            weighted = columns(ones_ref, g * GROUP, GROUP) * scores(planes, factors)
             return total + combine(weighted, factors)
 
         total = lax.fori_loop(0, steps, step, jnp.zeros((2 * rows, 2 * rank), f32))
         return join(total) + LAM * direction
 
     def energy(direction):
-        planes = twice(two_planes(direction))
-
-        def step(g, total):
-            score, weighted, _ = part(g, planes)
-            return total + jnp.sum(score * weighted, axis=-1, keepdims=True)
-
-        total = lax.fori_loop(0, steps, step, jnp.zeros((rows, 1), f32))
-        return total + LAM * jnp.sum(direction * direction, axis=-1, keepdims=True)
+        score = scores(twice(two_planes(direction)), factors_ref[...])
+        weighted = columns(ones_ref, 0, factors_ref.shape[0] // BL) * score
+        return jnp.sum(score * weighted, axis=-1, keepdims=True) + LAM * jnp.sum(
+            direction * direction, axis=-1, keepdims=True
+        )
 
     solution = start
     direction = residual

time: 153 us -> 153 us (level)
  blocking collectives: 73.5 us -> 71.9 us
    all_gather x1, blocking collectives: 23.4 us -> 21.8 us  [shards(): own = lax.all_gather(mine, ITEM, axis=0, tiled=False)]
  transfers between devices with their start and end apart: 5 -> 5, of which waited for: 3 -> 4; matrix products, arithmetic and copies ran while one was open for 0% -> 0% of each run, Pallas kernels for 16% -> 15%
where the time goes in v5:
time: 153 us; the launch traced here: 152 us
  blocking collectives  71.9 us (47%)
  Pallas kernels  36.9 us (24%)
  starting transfers between devices  31 us (20%)
  waiting for transfers between devices  7.52 us (5%)
  local copies, waits for them, and re-layouts  3.99 us (3%)
    all_gather x1, blocking collectives, shards(): own_users = lax.all_gather(piece, ITEM, axis=0, tiled=False)  24.9 us
    all_gather x1, blocking collectives, shards(): own = lax.all_gather(mine, ITEM, axis=0, tiled=False)  21.8 us
    pallas_call x1, Pallas kernels, solve_items(): pl.pallas_call(item_kernel, grid=(grid,), out_shape=jax.ShapeDtypeStruct(...  14.5 us
    all_to_all x1, blocking collectives, shards(): mine = lax.all_to_all(mine, 'z', 0, 0, tiled=True)  13.3 us
    pallas_call x1, Pallas kernels, solve_held(): pl.pallas_call(held_kernel, out_shape=(jax.ShapeDtypeStruct((copies, rows...  12.2 us
    all_to_all x1, blocking collectives, shards(): folded = lax.all_to_all(folded, ITEM, 0, 0, tiled=True)  11.9 us
    all_to_all x1, starting transfers between devices, shards(): piece = lax.all_to_all(piece, 'z', 0, 0, tiled=True)  9.15 us
    ppermute x1, starting transfers between devices, shards(): other = lax.ppermute(own, 'c', siblings)  7.66 us
  transfers between devices with their start and end apart: 5, of which 4 were waited for; matrix products, arithmetic and copies ran while one was open for 0% of the time, Pallas kernels for 15%

profile of v5, /device:TPU:1, one launch (start us, length us, event | category | flops | bytes accessed | tf_op | source)
XLA Modules:
  0.0 152.1 jit_solution(417038119224586301)
XLA Ops:
  0.7 1.8 %pack_users.1 = (s16[8,32,256]{2,1,0:T(8,128)(2,1)}, f32[1,256]{1,0:T(1,128)}) custom-call(s32[1]{0:T(128)} %bitcast.1.place_ref, f32[512,256]{1,0:T(8,128)} %rows_ref.1), custom_call_target="tpu_custom_call" | custom-call | tf_op jit(solution)/shard_map/pack_users/pallas_call | solution.py:68
  2.5 9.1 %all-to-all-start = ((s16[8,32,256]{2,1,0:T(8,128)(2,1)}), s16[8,32,256]{2,1,0:T(8,128)(2,1)S(1)}, u32[]{:S(2)}, u32[]{:S(2)}) async-start(s16[8,32,256]{2,1,0:T(8,128)(2,1)} %get-tuple-element.20), calls=%async_computation | async-start | bytes 262144 | tf_op jit(solution)/shard_map/all_to_all | solution.py:391
  11.7 1.2 copy-done.1
  12.9 0.7 copy-done.3
  13.6 0.7 copy-done.4
  14.3 0.7 copy-done.8
  14.9 1.8 %cut_held.1 = bf16[16,272,128]{2,1,0:T(8,128)(2,1)} custom-call(s32[1]{0:T(128)} %bitcast.1.place_ref, s32[2,16]{1,0:T(2,128)S(1)} %bitcast.43, s32[2,16]{1,0:T(2,128)S(1)} %bitcast.44, s32[16]{0:T(128)S(1)} %bitcast.47, bf16[32,128,128]{2,1,0:T(8,128)(2,1)S(1)} %bitcast.39, f32[1,256]{1,0:T(1,128)S(1)} %broadcast_in_dim.3.extra_ref), custom_call_target="tpu_custom_call" | custom-call | flops 1000000 | bytes 2000000 | tf_op jit(solution)/shard_map/cut_held/pallas_call | solution.py:111
  16.8 1.9 %cut_items.1 = bf16[16,272,128]{2,1,0:T(8,128)(2,1)} custom-call(s32[1]{0:T(128)} %bitcast.4.place_ref, s32[2,16]{1,0:T(2,128)S(1)} %bitcast.45, s32[2,16]{1,0:T(2,128)S(1)} %bitcast.46, s32[16]{0:T(128)S(1)} %bitcast.48, bf16[32,128,128]{2,1,0:T(8,128)(2,1)S(1)} %bitcast.40, f32[1,256]{1,0:T(1,128)S(1)} %copy-done.7), custom_call_target="tpu_custom_call" | custom-call | flops 1000000 | bytes 2000000 | tf_op jit(solution)/shard_map/cut_items/pallas_call | solution.py:111
  18.7 0.8 all-to-all-done
  19.4 7.4 %all-to-all-start.1 = ((bf16[16,272,128]{2,1,0:T(8,128)(2,1)}), bf16[16,272,128]{2,1,0:T(8,128)(2,1)}, u32[]{:S(2)}, u32[]{:S(2)}) async-start(bf16[16,272,128]{2,1,0:T(8,128)(2,1)} %cut_items.1), calls=%async_computation.1 | async-start | bytes 2228224 | tf_op jit(solution)/shard_map/all_to_all | solution.py:405
  26.8 24.9 %all-gather.4 = s16[128,32,256]{2,1,0:T(8,128)(2,1)S(1)} all-gather(s16[8,32,256]{2,1,0:T(8,128)(2,1)S(1)} %all-to-all-done), channel_id=2, replica_groups=mesh['z'=8,'c'=2,'y'=4,'x'=4] {'y','x'}, dimensions={0}, use_global_device_ids=true | all-gather | bytes 2228224 | tf_op jit(solution)/shard_map/all_gather | solution.py:406
  51.7 4.4 %all-to-all-done.1.strips_ref = bf16[16,272,128]{2,1,0:T(8,128)(2,1)} async-done(((bf16[16,272,128]{2,1,0:T(8,128)(2,1)}), bf16[16,272,128]{2,1,0:T(8,128)(2,1)}, u32[]{:S(2)}, u32[]{:S(2)}) %all-to-all-start.1) | async-done | bytes 1114144 | tf_op jit(solution)/shard_map/all_to_all | solution.py:405
  56.2 6.8 %all-to-all-start.2 = ((bf16[16,272,128]{2,1,0:T(8,128)(2,1)}), bf16[16,272,128]{2,1,0:T(8,128)(2,1)}, u32[]{:S(2)}, u32[]{:S(2)}) async-start(bf16[16,272,128]{2,1,0:T(8,128)(2,1)} %cut_held.1), calls=%async_computation.2 | async-start | bytes 2228224 | tf_op jit(solution)/shard_map/all_to_all | solution.py:409
  63.0 2.1 %dense_items.1 = (f32[2048,128]{1,0:T(8,128)S(1)}, f32[2048,128]{1,0:T(8,128)S(1)}, f32[16,256]{1,0:T(8,128)S(1)}) custom-call(bf16[16,272,128]{2,1,0:T(8,128)(2,1)} %all-to-all-done.1.strips_ref), custom_call_target="tpu_custom_call" | custom-call | flops 400000000 | bytes 3000000 | tf_op jit(solution)/shard_map/dense_items/pallas_call | solution.py:150
  65.2 14.5 %solve_items.1 = s16[8,40,256]{2,1,0:T(8,128)(2,1)S(1)} custom-call(f32[32,256]{1,0:T(8,128)S(1)} %dynamic-slice_bitcast_fusion.start_ref, f32[64,32,128]{2,1,0:T(8,128)S(1)} %bitcast.49, f32[64,32,128]{2,1,0:T(8,128)S(1)} %bitcast.50, f32[16,256]{1,0:T(8,128)S(1)} %get-tuple-element.27.step_ref, s32[1]{0:T(128)} %bitcast.core_ref, ...), custom_call_target="tpu_custom_call" | custom-call | flops 12000000000 | bytes 10000000 | tf_op jit(solution)/shard_map/solve_items/pallas_call | solution.py:290
  79.7 0.3 all-to-all-done.2.strips_ref
  80.0 13.3 %all_to_all.25 = s16[8,40,256]{2,1,0:T(8,128)(2,1)S(1)} all-to-all(s16[8,40,256]{2,1,0:T(8,128)(2,1)S(1)} %solve_items.1), channel_id=1, replica_groups=mesh['z'=8,'c'=2,'y'=4,'x'=4] {'z'}, dimensions={0} | all-to-all | bytes 327680 | tf_op jit(solution)/shard_map/all_to_all | solution.py:419
  93.3 21.8 %all-gather.5 = s16[128,40,256]{2,1,0:T(8,128)(2,1)S(1)} all-gather(s16[8,40,256]{2,1,0:T(8,128)(2,1)S(1)} %all_to_all.25), channel_id=3, replica_groups=mesh['z'=8,'c'=2,'y'=4,'x'=4] {'y','x'}, dimensions={0}, use_global_device_ids=true | all-gather | bytes 2785280 | tf_op jit(solution)/shard_map/all_gather | solution.py:420
  115.1 7.7 %collective-permute-start.1 = (s16[16,8,40,256]{3,2,1,0:T(8,128)(2,1)S(1)}, s16[16,8,40,256]{3,2,1,0:T(8,128)(2,1)S(1)}, u32[]{:S(2)}, u32[]{:S(2)}) collective-permute-start(s16[16,8,40,256]{3,2,1,0:T(8,128)(2,1)S(1)} %bitcast.35), channel_id=1, source_target_pairs={{0,16},{16,0},{1,17},{17,1},{2,18},{18,2},{3,19},{19,3},{4,20},{20... | collective-permute-start | bytes 7864328 | tf_op jit(solution)/shard_map/ppermute | solution.py:421
  122.8 2.5 %dense_held.1 = (f32[1024,128]{1,0:T(8,128)S(1)}, f32[1024,128]{1,0:T(8,128)S(1)}, f32[16,256]{1,0:T(8,128)}) custom-call(bf16[16,272,128]{2,1,0:T(8,128)(2,1)} %all-to-all-done.2.strips_ref), custom_call_target="tpu_custom_call" | custom-call | flops 400000000 | bytes 3000000 | tf_op jit(solution)/shard_map/dense_held/pallas_call | solution.py:150
  125.3 2.0 %collective-permute-done.1.other_ref = s16[16,8,40,256]{3,2,1,0:T(8,128)(2,1)S(1)} collective-permute-done((s16[16,8,40,256]{3,2,1,0:T(8,128)(2,1)S(1)}, s16[16,8,40,256]{3,2,1,0:T(8,128)(2,1)S(1)}, u32[]{:S(2)}, u32[]{:S(2)}) %collective-permute-start.1) | collective-permute-done | bytes 2621472 | tf_op jit(solution)/shard_map/ppermute | solution.py:421
  127.3 12.2 %solve_held.1 = (f32[16,16,256]{2,1,0:T(8,128)S(1)}, f32[512,256]{1,0:T(8,128)}) custom-call(s32[2]{0:T(128)S(1)} %pad_add_fusion.place_ref, f32[64,16,128]{2,1,0:T(8,128)S(1)} %bitcast.41, f32[64,16,128]{2,1,0:T(8,128)S(1)} %bitcast.42, s16[16,8,40,256]{3,2,1,0:T(8,128)(2,1)S(1)} %bitcast.36, s16[16,8,40,256]{3,2,1,0:T(8,128)(2,1)S(1)} %collective-permute-done.1.other_ref), custom_call_target="tpu_custom_call" | custom-call | tf_op jit(solution)/shard_map/solve_held/pallas_call | solution.py:352
  139.5 11.9 %all_to_all.26 = f32[16,16,256]{2,1,0:T(8,128)S(1)} all-to-all(f32[16,16,256]{2,1,0:T(8,128)S(1)} %get-tuple-element.35), channel_id=1, replica_groups=mesh['z'=8,'c'=2,'y'=4,'x'=4] {'y','x'}, dimensions={0} | all-to-all | bytes 524288 | tf_op jit(solution)/shard_map/all_to_all | solution.py:425
  151.4 0.7 copy.15
  (21 shorter events, 0.1 us)
Async XLA Ops:
  0.6 55.6 %copy-start = (f32[512,256]{1,0:T(8,128)S(1)}, f32[512,256]{1,0:T(8,128)}, u32[]{:S(2)}) copy-start(f32[512,256]{1,0:T(8,128)} %param.11) | copy-start | bytes 1572868
  0.6 16.1 %copy-start.9 = (s32[1,1,16]{2,1,0:T(1,128)S(1)}, s32[1,1,16]{2,1,0:T(1,128)}, u32[]{:S(2)}) copy-start(s32[1,1,16]{2,1,0:T(1,128)} %param.14) | copy-start | bytes 196
  0.7 16.1 %copy-start.6 = (s32[1,1,16,2]{2,3,1,0:T(2,128)S(1)}, s32[1,1,16,2]{2,3,1,0:T(2,128)}, u32[]{:S(2)}) copy-start(s32[1,1,16,2]{2,3,1,0:T(2,128)} %param.13) | copy-start | bytes 388
  0.7 16.1 %copy-start.5 = (s32[1,1,16,2]{2,3,1,0:T(2,128)S(1)}, s32[1,1,16,2]{2,3,1,0:T(2,128)}, u32[]{:S(2)}) copy-start(s32[1,1,16,2]{2,3,1,0:T(2,128)} %param.12) | copy-start | bytes 388
  2.5 14.2 %copy-start.7 = (f32[1,256]{1,0:T(1,128)S(1)}, f32[1,256]{1,0:T(1,128)}, u32[]{:S(2)}) copy-start(f32[1,256]{1,0:T(1,128)} %get-tuple-element.19.extra_ref) | copy-start | bytes 3076
  2.5 16.9 %all-to-all-start = ((s16[8,32,256]{2,1,0:T(8,128)(2,1)}), s16[8,32,256]{2,1,0:T(8,128)(2,1)S(1)}, u32[]{:S(2)}, u32[]{:S(2)}) async-start(s16[8,32,256]{2,1,0:T(8,128)(2,1)} %get-tuple-element.20), calls=%async_computation | async-start | bytes 262144 | tf_op jit(solution)/shard_map/all_to_all | solution.py:391
  11.7 1.2 copy-start.1
  12.9 0.7 copy-start.3
  13.6 0.7 copy-start.4
  14.2 0.7 copy-start.8
  14.9 1.9 %copy-start.2 = (bf16[1,1,16,2,128,128]{5,4,3,2,1,0:T(8,128)(2,1)S(1)}, bf16[1,1,16,2,128,128]{5,4,3,2,1,0:T(8,128)(2,1)}, u32[]{:S(2)}) copy-start(bf16[1,1,16,2,128,128]{5,4,3,2,1,0:T(8,128)(2,1)} %param.15) | copy-start | bytes 3145732
  19.4 36.8 %all-to-all-start.1 = ((bf16[16,272,128]{2,1,0:T(8,128)(2,1)}), bf16[16,272,128]{2,1,0:T(8,128)(2,1)}, u32[]{:S(2)}, u32[]{:S(2)}) async-start(bf16[16,272,128]{2,1,0:T(8,128)(2,1)} %cut_items.1), calls=%async_computation.1 | async-start | bytes 2228224 | tf_op jit(solution)/shard_map/all_to_all | solution.py:405
  56.2 9.0 %collective-permute-start = (s16[16,8,32,256]{3,2,1,0:T(8,128)(2,1)S(1)}, s16[16,8,32,256]{3,2,1,0:T(8,128)(2,1)}, u32[]{:S(2)}, u32[]{:S(2)}) collective-permute-start(s16[16,8,32,256]{3,2,1,0:T(8,128)(2,1)S(1)} %bitcast.37), channel_id=1, source_target_pairs={{0,16},{16,0},{1,17},{17,1},{2,18},{18,2},{3,19},{19,3},{4,20},{20... | collective-permute-start | bytes 6291464 | tf_op jit(solution)/shard_map/ppermute | solution.py:408
  56.2 23.8 %all-to-all-start.2 = ((bf16[16,272,128]{2,1,0:T(8,128)(2,1)}), bf16[16,272,128]{2,1,0:T(8,128)(2,1)}, u32[]{:S(2)}, u32[]{:S(2)}) async-start(bf16[16,272,128]{2,1,0:T(8,128)(2,1)} %cut_held.1), calls=%async_computation.2 | async-start | bytes 2228224 | tf_op jit(solution)/shard_map/all_to_all | solution.py:409
  115.1 12.2 %collective-permute-start.1 = (s16[16,8,40,256]{3,2,1,0:T(8,128)(2,1)S(1)}, s16[16,8,40,256]{3,2,1,0:T(8,128)(2,1)S(1)}, u32[]{:S(2)}, u32[]{:S(2)}) collective-permute-start(s16[16,8,40,256]{3,2,1,0:T(8,128)(2,1)S(1)} %bitcast.35), channel_id=1, source_target_pairs={{0,16},{16,0},{1,17},{17,1},{2,18},{18,2},{3,19},{19,3},{4,20},{20... | collective-permute-start | bytes 7864328 | tf_op jit(solution)/shard_map/ppermute | solution.py:421

commit v6 on v5

--- a/solution.py
+++ b/solution.py
@@ -190,8 +190,9 @@
     return fold(both[:, :rank] + both[:, rank:])
 
 
-def columns(ref, first, count):
-    return jnp.concatenate([ref[first + k] for k in range(count)], axis=1)
+def columns(ref, first, count, rows):
+    spans = [pl.ds(pl.multiple_of((first + k) * rows, rows), rows) for k in range(count)]
+    return jnp.concatenate([ref[span, :] for span in spans], axis=1)
 
 
 def split(codes, step):
@@ -210,7 +211,7 @@
 
         def step(g, total):
             factors = factors_ref[pl.ds(pl.multiple_of(g * group, group), group), :]
-            weighted = columns(ones_ref, g * GROUP, GROUP) * scores(planes, factors)
+            weighted = columns(ones_ref, g * GROUP, GROUP, rows) * scores(planes, factors)
             return total + combine(weighted, factors)
 
         total = lax.fori_loop(0, steps, step, jnp.zeros((2 * rows, 2 * rank), f32))
@@ -218,7 +219,7 @@
 
     def energy(direction):
         score = scores(twice(two_planes(direction)), factors_ref[...])
-        weighted = columns(ones_ref, 0, factors_ref.shape[0] // BL) * score
+        weighted = columns(ones_ref, 0, factors_ref.shape[0] // BL, rows) * score
         return jnp.sum(score * weighted, axis=-1, keepdims=True) + LAM * jnp.sum(
             direction * direction, axis=-1, keepdims=True
         )
@@ -238,8 +239,12 @@
         norm_now = norm_next
 
 
-def item_kernel(start_ref, ones_ref, right_ref, step_ref, core_ref, own_ref, other_ref, out_ref, factors_ref, total_ref):
+def item_kernel(
+    slots, start_ref, strips_ref, core_ref, own_ref, other_ref, out_ref,
+    factors_ref, total_ref, ones_ref, right_ref, step_ref, wide_ref,
+):
     g = pl.program_id(0)
+    held = start_ref.shape[0]
     sources, chips, part, rank = own_ref.shape
     per = BL // part
     group = sources * 2 * chips * part
@@ -248,6 +253,7 @@
     @pl.when(g == 0)
     def _():
         total_ref[...] = jnp.zeros_like(total_ref)
+        dense_kernel(ones_ref.shape[0] // SUB, slots, strips_ref, ones_ref, right_ref, step_ref, wide_ref)
 
     for ref, which in ((own_ref, core), (other_ref, 1 - core)):
         for z in range(chips):
@@ -260,7 +266,7 @@
     factors = factors_ref[pl.ds(pl.multiple_of(g * group, group), group), :]
     count = group // BL
     score = scores(twice(two_planes(start_ref[...])), factors)
-    weighted = columns(right_ref, g * count, count) - columns(ones_ref, g * count, count) * score
+    weighted = columns(right_ref, g * count, count, held) - columns(ones_ref, g * count, count, held) * score
     total_ref[...] += combine(weighted, factors)
 
     @pl.when(g == pl.num_programs(0) - 1)
@@ -279,33 +285,36 @@
     return pl.BlockSpec((shape[0] // grid,) + shape[1:], lambda s: (s, 0, 0, 0))
 
 
-def solve_items(start, ones, right, step, core, own, other, copies):
+def solve_items(start, strips, slots, core, own, other, copies):
     rows, rank = start.shape
     whole = 2 * own.size // rank
     grid = whole // (GROUP * BL)
-    ones = ones.reshape(-1, rows, BL)
-    right = right.reshape(-1, rows, BL)
-    fixed3 = pl.BlockSpec(ones.shape, lambda s: (0, 0, 0), pipeline_mode=pl.Buffered(1))
+    dense_shape = (whole // BL * rows, BL)
     codes = gathered_spec(own.shape, grid)
     return pl.pallas_call(
-        item_kernel,
+        functools.partial(item_kernel, slots),
         grid=(grid,),
         out_shape=jax.ShapeDtypeStruct((copies, rows + SUB, rank), jnp.int16),
         in_specs=[
             pl.BlockSpec((rows, rank), lambda s: (0, 0)),
-            fixed3,
-            fixed3,
-            pl.BlockSpec(step.shape, lambda s: (0, 0)),
+            pl.BlockSpec(strips.shape, lambda s: (0, 0, 0), pipeline_mode=pl.Buffered(1)),
             pl.BlockSpec(memory_space=pltpu.SMEM),
             codes,
             codes,
         ],
         out_specs=pl.BlockSpec((copies, rows + SUB, rank), lambda s: (0, 0, 0)),
-        scratch_shapes=[pltpu.VMEM((whole, 2 * rank), bf16), pltpu.VMEM((2 * rows, 2 * rank), f32)],
+        scratch_shapes=[
+            pltpu.VMEM((whole, 2 * rank), bf16),
+            pltpu.VMEM((2 * rows, 2 * rank), f32),
+            pltpu.VMEM(dense_shape, f32),
+            pltpu.VMEM(dense_shape, f32),
+            pltpu.VMEM((strips.shape[0], 2 * BL), f32),
+            pltpu.VMEM((strips.shape[0] * slots * SUB, BL), f32),
+        ],
         compiler_params=params(),
         cost_estimate=pl.CostEstimate(flops=12 * 10**9, bytes_accessed=10**7, transcendentals=0),
         name="solve_items",
-    )(start, ones, right, step, core, own, other)
+    )(start, strips, core, own, other)
 
 
 def held_kernel(place_ref, ones_ref, right_ref, own_ref, other_ref, out_ref, items_ref, factors_ref):
@@ -336,7 +345,7 @@
     total = jnp.zeros((2 * out_ref.shape[1], 2 * rank), f32)
     for g in range(factors_ref.shape[0] // group):
         factors = factors_ref[g * group : (g + 1) * group, :]
-        total = total + combine(columns(right_ref, g * GROUP, GROUP), factors)
+        total = total + combine(columns(right_ref, g * GROUP, GROUP, out_ref.shape[1]), factors)
     mine = factors_ref[pl.ds(pl.multiple_of(place_ref[1] * shard, shard), shard), :]
     items_ref[...] = mine[:, :rank].astype(f32) + mine[:, rank:].astype(f32)
     residual = join(total)
@@ -357,7 +366,7 @@
         scratch_shapes=[pltpu.VMEM((whole, 2 * rank), bf16)],
         compiler_params=params(),
         name="solve_held",
-    )(place, ones.reshape(-1, rows, BL), right.reshape(-1, rows, BL), own, other)
+    )(place, ones, right, own, other)
 
 
 def shards(
@@ -407,12 +416,11 @@
     strips, own_users, held_strips = lax.optimization_barrier((strips, own_users, held_strips))
     other_users = lax.ppermute(own_users, "c", siblings)
     held_strips = lax.all_to_all(held_strips, ITEM, 0, 0, tiled=True)
-    ones, right, step = dense(strips, blocks, peers * slots, "dense_items")
 
     start = lax.dynamic_slice_in_dim(
         item_factors.reshape(item_blocks, peers, SUB, rank), core * chips + chip, 1, axis=1
     ).reshape(item_blocks * SUB, rank)
-    mine = solve_items(start, ones, right, step, core.reshape(1), own_users, other_users, chips)
+    mine = solve_items(start, strips, peers * slots, core.reshape(1), own_users, other_users, chips)
     mine, held_strips = lax.optimization_barrier((mine, held_strips))
     held_ones, held_right, _ = dense(held_strips, held_all, item_peers * held_slots, "dense_held")
 

time: 153 us -> 153 us (level)
    pallas_call x2 -> x1, Pallas kernels: 4.58 us -> 2.47 us  [dense(): pl.pallas_call(functools.partial(dense_kernel, blocks, slots), out_shape=...]
  transfers between devices with their start and end apart: 5 -> 5, of which waited for: 4 -> 4; matrix products, arithmetic and copies ran while one was open for 0% -> 0% of each run, Pallas kernels for 15% -> 14%
where the time goes in v6:
time: 153 us; the launch traced here: 152 us
  blocking collectives  71.7 us (47%)
  Pallas kernels  36 us (24%)
  starting transfers between devices  31.1 us (20%)
  waiting for transfers between devices  8.4 us (5%)
  local copies, waits for them, and re-layouts  3.99 us (3%)
    all_gather x1, blocking collectives, shards(): own_users = lax.all_gather(piece, ITEM, axis=0, tiled=False)  24.9 us
    all_gather x1, blocking collectives, shards(): own = lax.all_gather(mine, ITEM, axis=0, tiled=False)  21.8 us
    pallas_call x1, Pallas kernels, solve_items(): pl.pallas_call(functools.partial(item_kernel, slots), grid=(grid,), out_s...  15.7 us
    all_to_all x1, blocking collectives, shards(): mine = lax.all_to_all(mine, 'z', 0, 0, tiled=True)  13.3 us
    pallas_call x1, Pallas kernels, solve_held(): pl.pallas_call(held_kernel, out_shape=(jax.ShapeDtypeStruct((copies, rows...  12.2 us
    all_to_all x1, blocking collectives, shards(): folded = lax.all_to_all(folded, ITEM, 0, 0, tiled=True)  11.7 us
    all_to_all x1, starting transfers between devices, shards(): piece = lax.all_to_all(piece, 'z', 0, 0, tiled=True)  9.15 us
    ppermute x1, starting transfers between devices, shards(): other = lax.ppermute(own, 'c', siblings)  7.66 us
  transfers between devices with their start and end apart: 5, of which 4 were waited for; matrix products, arithmetic and copies ran while one was open for 0% of the time, Pallas kernels for 14%

profile of v6, /device:TPU:1, one launch (start us, length us, event | category | flops | bytes accessed | tf_op | source)
XLA Modules:
  0.0 151.9 jit_solution(7518943365020244026)
XLA Ops:
  0.7 1.8 %pack_users.1 = (s16[8,32,256]{2,1,0:T(8,128)(2,1)}, f32[1,256]{1,0:T(1,128)}) custom-call(s32[1]{0:T(128)} %bitcast.1.place_ref, f32[512,256]{1,0:T(8,128)} %rows_ref.1), custom_call_target="tpu_custom_call" | custom-call | tf_op jit(solution)/shard_map/pack_users/pallas_call | solution.py:68
  2.5 9.1 %all-to-all-start = ((s16[8,32,256]{2,1,0:T(8,128)(2,1)}), s16[8,32,256]{2,1,0:T(8,128)(2,1)S(1)}, u32[]{:S(2)}, u32[]{:S(2)}) async-start(s16[8,32,256]{2,1,0:T(8,128)(2,1)} %get-tuple-element.17), calls=%async_computation | async-start | bytes 262144 | tf_op jit(solution)/shard_map/all_to_all | solution.py:400
  11.7 1.2 copy-done.1
  12.9 0.7 copy-done.3
  13.6 0.7 copy-done.4
  14.3 0.7 copy-done.8
  14.9 1.8 %cut_held.1 = bf16[16,272,128]{2,1,0:T(8,128)(2,1)} custom-call(s32[1]{0:T(128)} %bitcast.1.place_ref, s32[2,16]{1,0:T(2,128)S(1)} %bitcast.37, s32[2,16]{1,0:T(2,128)S(1)} %bitcast.38, s32[16]{0:T(128)S(1)} %bitcast.41, bf16[32,128,128]{2,1,0:T(8,128)(2,1)S(1)} %bitcast.35, f32[1,256]{1,0:T(1,128)S(1)} %broadcast_in_dim.3.extra_ref), custom_call_target="tpu_custom_call" | custom-call | flops 1000000 | bytes 2000000 | tf_op jit(solution)/shard_map/cut_held/pallas_call | solution.py:111
  16.8 1.9 %cut_items.1 = bf16[16,272,128]{2,1,0:T(8,128)(2,1)} custom-call(s32[1]{0:T(128)} %bitcast.4.place_ref, s32[2,16]{1,0:T(2,128)S(1)} %bitcast.39, s32[2,16]{1,0:T(2,128)S(1)} %bitcast.40, s32[16]{0:T(128)S(1)} %bitcast.42, bf16[32,128,128]{2,1,0:T(8,128)(2,1)S(1)} %bitcast.36, f32[1,256]{1,0:T(1,128)S(1)} %copy-done.7), custom_call_target="tpu_custom_call" | custom-call | flops 1000000 | bytes 2000000 | tf_op jit(solution)/shard_map/cut_items/pallas_call | solution.py:111
  18.7 0.7 all-to-all-done
  19.4 7.4 %all-to-all-start.1 = ((bf16[16,272,128]{2,1,0:T(8,128)(2,1)}), bf16[16,272,128]{2,1,0:T(8,128)(2,1)}, u32[]{:S(2)}, u32[]{:S(2)}) async-start(bf16[16,272,128]{2,1,0:T(8,128)(2,1)} %cut_items.1), calls=%async_computation.1 | async-start | bytes 2228224 | tf_op jit(solution)/shard_map/all_to_all | solution.py:414
  26.9 24.9 %all-gather.4 = s16[128,32,256]{2,1,0:T(8,128)(2,1)S(1)} all-gather(s16[8,32,256]{2,1,0:T(8,128)(2,1)S(1)} %all-to-all-done), channel_id=2, replica_groups=mesh['z'=8,'c'=2,'y'=4,'x'=4] {'y','x'}, dimensions={0}, use_global_device_ids=true | all-gather | bytes 2228224 | tf_op jit(solution)/shard_map/all_gather | solution.py:415
  51.8 4.4 %all-to-all-done.1.strips_ref = bf16[16,272,128]{2,1,0:T(8,128)(2,1)} async-done(((bf16[16,272,128]{2,1,0:T(8,128)(2,1)}), bf16[16,272,128]{2,1,0:T(8,128)(2,1)}, u32[]{:S(2)}, u32[]{:S(2)}) %all-to-all-start.1) | async-done | bytes 1114144 | tf_op jit(solution)/shard_map/all_to_all | solution.py:414
  56.2 6.8 %all-to-all-start.2 = ((bf16[16,272,128]{2,1,0:T(8,128)(2,1)}), bf16[16,272,128]{2,1,0:T(8,128)(2,1)}, u32[]{:S(2)}, u32[]{:S(2)}) async-start(bf16[16,272,128]{2,1,0:T(8,128)(2,1)} %cut_held.1), calls=%async_computation.2 | async-start | bytes 2228224 | tf_op jit(solution)/shard_map/all_to_all | solution.py:418
  63.1 15.7 %solve_items.1 = s16[8,40,256]{2,1,0:T(8,128)(2,1)S(1)} custom-call(f32[32,256]{1,0:T(8,128)S(1)} %dynamic-slice_bitcast_fusion.start_ref, bf16[16,272,128]{2,1,0:T(8,128)(2,1)} %all-to-all-done.1.strips_ref, s32[1]{0:T(128)} %bitcast.core_ref, s16[16,8,32,256]{3,2,1,0:T(8,128)(2,1)S(1)} %bitcast.34, s16[16,8,32,256]{3,2,1,0:T(8,128)(2,1)} %collective-permute-done.other_ref), custom_call_target="tpu_custom_call" | custom-call | flops 12000000000 | bytes 10000000 | tf_op jit(solution)/shard_map/solve_items/pallas_call | solution.py:294
  78.8 1.2 all-to-all-done.2.strips_ref
  80.0 13.3 %all_to_all.25 = s16[8,40,256]{2,1,0:T(8,128)(2,1)S(1)} all-to-all(s16[8,40,256]{2,1,0:T(8,128)(2,1)S(1)} %solve_items.1), channel_id=1, replica_groups=mesh['z'=8,'c'=2,'y'=4,'x'=4] {'z'}, dimensions={0} | all-to-all | bytes 327680 | tf_op jit(solution)/shard_map/all_to_all | solution.py:427
  93.3 21.8 %all-gather.5 = s16[128,40,256]{2,1,0:T(8,128)(2,1)S(1)} all-gather(s16[8,40,256]{2,1,0:T(8,128)(2,1)S(1)} %all_to_all.25), channel_id=3, replica_groups=mesh['z'=8,'c'=2,'y'=4,'x'=4] {'y','x'}, dimensions={0}, use_global_device_ids=true | all-gather | bytes 2785280 | tf_op jit(solution)/shard_map/all_gather | solution.py:428
  115.1 7.7 %collective-permute-start.1 = (s16[16,8,40,256]{3,2,1,0:T(8,128)(2,1)S(1)}, s16[16,8,40,256]{3,2,1,0:T(8,128)(2,1)S(1)}, u32[]{:S(2)}, u32[]{:S(2)}) collective-permute-start(s16[16,8,40,256]{3,2,1,0:T(8,128)(2,1)S(1)} %bitcast.31), channel_id=1, source_target_pairs={{0,16},{16,0},{1,17},{17,1},{2,18},{18,2},{3,19},{19,3},{4,20},{20... | collective-permute-start | bytes 7864328 | tf_op jit(solution)/shard_map/ppermute | solution.py:429
  122.8 0.1 pad_add_fusion.place_ref
  122.8 2.5 %dense_held.1 = (f32[1024,128]{1,0:T(8,128)S(1)}, f32[1024,128]{1,0:T(8,128)S(1)}, f32[16,256]{1,0:T(8,128)}) custom-call(bf16[16,272,128]{2,1,0:T(8,128)(2,1)} %all-to-all-done.2.strips_ref), custom_call_target="tpu_custom_call" | custom-call | flops 400000000 | bytes 3000000 | tf_op jit(solution)/shard_map/dense_held/pallas_call | solution.py:150
  125.3 2.0 %collective-permute-done.1.other_ref = s16[16,8,40,256]{3,2,1,0:T(8,128)(2,1)S(1)} collective-permute-done((s16[16,8,40,256]{3,2,1,0:T(8,128)(2,1)S(1)}, s16[16,8,40,256]{3,2,1,0:T(8,128)(2,1)S(1)}, u32[]{:S(2)}, u32[]{:S(2)}) %collective-permute-start.1) | collective-permute-done | bytes 2621472 | tf_op jit(solution)/shard_map/ppermute | solution.py:429
  127.3 12.2 %solve_held.1 = (f32[16,16,256]{2,1,0:T(8,128)S(1)}, f32[512,256]{1,0:T(8,128)}) custom-call(s32[2]{0:T(128)S(1)} %pad_add_fusion.place_ref, f32[1024,128]{1,0:T(8,128)S(1)} %get-tuple-element.25.ones_ref, f32[1024,128]{1,0:T(8,128)S(1)} %get-tuple-element.26.right_ref, s16[16,8,40,256]{3,2,1,0:T(8,128)(2,1)S(1)} %bitcast.32, ...), custom_call_target="tpu_custom_call" | custom-call | tf_op jit(solution)/shard_map/solve_held/pallas_call | solution.py:361
  139.5 11.7 %all_to_all.26 = f32[16,16,256]{2,1,0:T(8,128)S(1)} all-to-all(f32[16,16,256]{2,1,0:T(8,128)S(1)} %get-tuple-element.29), channel_id=1, replica_groups=mesh['z'=8,'c'=2,'y'=4,'x'=4] {'y','x'}, dimensions={0} | all-to-all | bytes 524288 | tf_op jit(solution)/shard_map/all_to_all | solution.py:433
  151.2 0.7 copy.15
  (20 shorter events, 0.0 us)
Async XLA Ops:
  0.6 55.6 %copy-start = (f32[512,256]{1,0:T(8,128)S(1)}, f32[512,256]{1,0:T(8,128)}, u32[]{:S(2)}) copy-start(f32[512,256]{1,0:T(8,128)} %param.11) | copy-start | bytes 1572868
  0.6 16.1 %copy-start.9 = (s32[1,1,16]{2,1,0:T(1,128)S(1)}, s32[1,1,16]{2,1,0:T(1,128)}, u32[]{:S(2)}) copy-start(s32[1,1,16]{2,1,0:T(1,128)} %param.14) | copy-start | bytes 196
  0.7 16.1 %copy-start.6 = (s32[1,1,16,2]{2,3,1,0:T(2,128)S(1)}, s32[1,1,16,2]{2,3,1,0:T(2,128)}, u32[]{:S(2)}) copy-start(s32[1,1,16,2]{2,3,1,0:T(2,128)} %param.13) | copy-start | bytes 388
  0.7 16.1 %copy-start.5 = (s32[1,1,16,2]{2,3,1,0:T(2,128)S(1)}, s32[1,1,16,2]{2,3,1,0:T(2,128)}, u32[]{:S(2)}) copy-start(s32[1,1,16,2]{2,3,1,0:T(2,128)} %param.12) | copy-start | bytes 388
  2.5 14.3 %copy-start.7 = (f32[1,256]{1,0:T(1,128)S(1)}, f32[1,256]{1,0:T(1,128)}, u32[]{:S(2)}) copy-start(f32[1,256]{1,0:T(1,128)} %get-tuple-element.16.extra_ref) | copy-start | bytes 3076
  2.5 16.9 %all-to-all-start = ((s16[8,32,256]{2,1,0:T(8,128)(2,1)}), s16[8,32,256]{2,1,0:T(8,128)(2,1)S(1)}, u32[]{:S(2)}, u32[]{:S(2)}) async-start(s16[8,32,256]{2,1,0:T(8,128)(2,1)} %get-tuple-element.17), calls=%async_computation | async-start | bytes 262144 | tf_op jit(solution)/shard_map/all_to_all | solution.py:400
  11.7 1.2 copy-start.1
  12.9 0.7 copy-start.3
  13.6 0.7 copy-start.4
  14.2 0.7 copy-start.8
  14.9 1.9 %copy-start.2 = (bf16[1,1,16,2,128,128]{5,4,3,2,1,0:T(8,128)(2,1)S(1)}, bf16[1,1,16,2,128,128]{5,4,3,2,1,0:T(8,128)(2,1)}, u32[]{:S(2)}) copy-start(bf16[1,1,16,2,128,128]{5,4,3,2,1,0:T(8,128)(2,1)} %param.15) | copy-start | bytes 3145732
  19.4 36.8 %all-to-all-start.1 = ((bf16[16,272,128]{2,1,0:T(8,128)(2,1)}), bf16[16,272,128]{2,1,0:T(8,128)(2,1)}, u32[]{:S(2)}, u32[]{:S(2)}) async-start(bf16[16,272,128]{2,1,0:T(8,128)(2,1)} %cut_items.1), calls=%async_computation.1 | async-start | bytes 2228224 | tf_op jit(solution)/shard_map/all_to_all | solution.py:414
  56.2 6.8 %collective-permute-start = (s16[16,8,32,256]{3,2,1,0:T(8,128)(2,1)S(1)}, s16[16,8,32,256]{3,2,1,0:T(8,128)(2,1)}, u32[]{:S(2)}, u32[]{:S(2)}) collective-permute-start(s16[16,8,32,256]{3,2,1,0:T(8,128)(2,1)S(1)} %bitcast.33), channel_id=1, source_target_pairs={{0,16},{16,0},{1,17},{17,1},{2,18},{18,2},{3,19},{19,3},{4,20},{20... | collective-permute-start | bytes 6291464 | tf_op jit(solution)/shard_map/ppermute | solution.py:417
  56.2 23.8 %all-to-all-start.2 = ((bf16[16,272,128]{2,1,0:T(8,128)(2,1)}), bf16[16,272,128]{2,1,0:T(8,128)(2,1)}, u32[]{:S(2)}, u32[]{:S(2)}) async-start(bf16[16,272,128]{2,1,0:T(8,128)(2,1)} %cut_held.1), calls=%async_computation.2 | async-start | bytes 2228224 | tf_op jit(solution)/shard_map/all_to_all | solution.py:418
  115.1 12.2 %collective-permute-start.1 = (s16[16,8,40,256]{3,2,1,0:T(8,128)(2,1)S(1)}, s16[16,8,40,256]{3,2,1,0:T(8,128)(2,1)S(1)}, u32[]{:S(2)}, u32[]{:S(2)}) collective-permute-start(s16[16,8,40,256]{3,2,1,0:T(8,128)(2,1)S(1)} %bitcast.31), channel_id=1, source_target_pairs={{0,16},{16,0},{1,17},{17,1},{2,18},{18,2},{3,19},{19,3},{4,20},{20... | collective-permute-start | bytes 7864328 | tf_op jit(solution)/shard_map/ppermute | solution.py:429

commit v7 on v6

--- a/solution.py
+++ b/solution.py
@@ -214,7 +214,7 @@
             weighted = columns(ones_ref, g * GROUP, GROUP, rows) * scores(planes, factors)
             return total + combine(weighted, factors)
 
-        total = lax.fori_loop(0, steps, step, jnp.zeros((2 * rows, 2 * rank), f32))
+        total = lax.fori_loop(0, steps, step, jnp.zeros((2 * rows, 2 * rank), f32), unroll=True)
         return join(total) + LAM * direction
 
     def energy(direction):
@@ -341,7 +341,7 @@
                     factors_ref[rows, rank:] = (value - upper.astype(f32)).astype(bf16)
         return carry
 
-    lax.fori_loop(0, sources, decode, 0, unroll=4)
+    lax.fori_loop(0, sources, decode, 0, unroll=8)
     total = jnp.zeros((2 * out_ref.shape[1], 2 * rank), f32)
     for g in range(factors_ref.shape[0] // group):
         factors = factors_ref[g * group : (g + 1) * group, :]

time: 153 us -> 156 us (1.020)
  Pallas kernels: 36 us -> 40.4 us
  blocking collectives: 71.7 us -> 73.5 us
    pallas_call x1, Pallas kernels: 12.2 us -> 15 us  [solve_held(): pl.pallas_call(held_kernel, out_shape=(jax.ShapeDtypeStruct((copies, rows...]
    pallas_call x1, Pallas kernels: 15.7 us -> 17.3 us  [solve_items(): pl.pallas_call(functools.partial(item_kernel, slots), grid=(grid,), out_s...]
  transfers between devices with their start and end apart: 5 -> 5, of which waited for: 4 -> 3; matrix products, arithmetic and copies ran while one was open for 0% -> 0% of each run, Pallas kernels for 14% -> 15%
where the time goes in v7:
time: 156 us
  blocking collectives  73.5 us (47%)
  Pallas kernels  40.4 us (26%)
  starting transfers between devices  29.8 us (19%)
  waiting for transfers between devices  7.19 us (5%)
  local copies, waits for them, and re-layouts  3.99 us (3%)
    all_gather x1, blocking collectives, shards(): own_users = lax.all_gather(piece, ITEM, axis=0, tiled=False)  24.9 us
    all_gather x1, blocking collectives, shards(): own = lax.all_gather(mine, ITEM, axis=0, tiled=False)  23.3 us
    pallas_call x1, Pallas kernels, solve_items(): pl.pallas_call(functools.partial(item_kernel, slots), grid=(grid,), out_s...  17.3 us
    pallas_call x1, Pallas kernels, solve_held(): pl.pallas_call(held_kernel, out_shape=(jax.ShapeDtypeStruct((copies, rows...  15 us
    all_to_all x1, blocking collectives, shards(): mine = lax.all_to_all(mine, 'z', 0, 0, tiled=True)  12.9 us
    all_to_all x1, blocking collectives, shards(): folded = lax.all_to_all(folded, ITEM, 0, 0, tiled=True)  12.4 us
    all_to_all x1, starting transfers between devices, shards(): piece = lax.all_to_all(piece, 'z', 0, 0, tiled=True)  9.15 us
    all_to_all x1, starting transfers between devices, shards(): strips = lax.all_to_all(strips, USER, 0, 0, tiled=True)  7.43 us
  transfers between devices with their start and end apart: 5, of which 3 were waited for; matrix products, arithmetic and copies ran while one was open for 0% of the time, Pallas kernels for 15%

profile of v7, /device:TPU:1, one launch (start us, length us, event | category | flops | bytes accessed | tf_op | source)
XLA Modules:
  0.0 155.7 jit_solution(15017169726157577621)
XLA Ops:
  0.6 0.0 copy-start
  0.7 1.8 %pack_users.1 = (s16[8,32,256]{2,1,0:T(8,128)(2,1)}, f32[1,256]{1,0:T(1,128)}) custom-call(s32[1]{0:T(128)} %bitcast.1.place_ref, f32[512,256]{1,0:T(8,128)} %rows_ref.1), custom_call_target="tpu_custom_call" | custom-call | tf_op jit(solution)/shard_map/pack_users/pallas_call | solution.py:68
  2.5 9.1 %all-to-all-start = ((s16[8,32,256]{2,1,0:T(8,128)(2,1)}), s16[8,32,256]{2,1,0:T(8,128)(2,1)S(1)}, u32[]{:S(2)}, u32[]{:S(2)}) async-start(s16[8,32,256]{2,1,0:T(8,128)(2,1)} %get-tuple-element.17), calls=%async_computation | async-start | bytes 262144 | tf_op jit(solution)/shard_map/all_to_all | solution.py:400
  11.7 1.2 copy-done.1
  12.9 0.7 copy-done.3
  13.6 0.7 copy-done.4
  14.3 0.7 copy-done.8
  14.9 1.8 %cut_held.1 = bf16[16,272,128]{2,1,0:T(8,128)(2,1)} custom-call(s32[1]{0:T(128)} %bitcast.1.place_ref, s32[2,16]{1,0:T(2,128)S(1)} %bitcast.37, s32[2,16]{1,0:T(2,128)S(1)} %bitcast.38, s32[16]{0:T(128)S(1)} %bitcast.41, bf16[32,128,128]{2,1,0:T(8,128)(2,1)S(1)} %bitcast.35, f32[1,256]{1,0:T(1,128)S(1)} %broadcast_in_dim.3.extra_ref), custom_call_target="tpu_custom_call" | custom-call | flops 1000000 | bytes 2000000 | tf_op jit(solution)/shard_map/cut_held/pallas_call | solution.py:111
  16.8 1.9 %cut_items.1 = bf16[16,272,128]{2,1,0:T(8,128)(2,1)} custom-call(s32[1]{0:T(128)} %bitcast.4.place_ref, s32[2,16]{1,0:T(2,128)S(1)} %bitcast.39, s32[2,16]{1,0:T(2,128)S(1)} %bitcast.40, s32[16]{0:T(128)S(1)} %bitcast.42, bf16[32,128,128]{2,1,0:T(8,128)(2,1)S(1)} %bitcast.36, f32[1,256]{1,0:T(1,128)S(1)} %copy-done.7), custom_call_target="tpu_custom_call" | custom-call | flops 1000000 | bytes 2000000 | tf_op jit(solution)/shard_map/cut_items/pallas_call | solution.py:111
  18.7 0.7 all-to-all-done
  19.4 7.4 %all-to-all-start.1 = ((bf16[16,272,128]{2,1,0:T(8,128)(2,1)}), bf16[16,272,128]{2,1,0:T(8,128)(2,1)}, u32[]{:S(2)}, u32[]{:S(2)}) async-start(bf16[16,272,128]{2,1,0:T(8,128)(2,1)} %cut_items.1), calls=%async_computation.1 | async-start | bytes 2228224 | tf_op jit(solution)/shard_map/all_to_all | solution.py:414
  26.9 24.9 %all-gather.4 = s16[128,32,256]{2,1,0:T(8,128)(2,1)S(1)} all-gather(s16[8,32,256]{2,1,0:T(8,128)(2,1)S(1)} %all-to-all-done), channel_id=2, replica_groups=mesh['z'=8,'c'=2,'y'=4,'x'=4] {'y','x'}, dimensions={0}, use_global_device_ids=true | all-gather | bytes 2228224 | tf_op jit(solution)/shard_map/all_gather | solution.py:415
  51.8 4.4 %all-to-all-done.1.strips_ref = bf16[16,272,128]{2,1,0:T(8,128)(2,1)} async-done(((bf16[16,272,128]{2,1,0:T(8,128)(2,1)}), bf16[16,272,128]{2,1,0:T(8,128)(2,1)}, u32[]{:S(2)}, u32[]{:S(2)}) %all-to-all-start.1) | async-done | bytes 1114144 | tf_op jit(solution)/shard_map/all_to_all | solution.py:414
  56.2 6.8 %all-to-all-start.2 = ((bf16[16,272,128]{2,1,0:T(8,128)(2,1)}), bf16[16,272,128]{2,1,0:T(8,128)(2,1)}, u32[]{:S(2)}, u32[]{:S(2)}) async-start(bf16[16,272,128]{2,1,0:T(8,128)(2,1)} %cut_held.1), calls=%async_computation.2 | async-start | bytes 2228224 | tf_op jit(solution)/shard_map/all_to_all | solution.py:418
  63.1 17.3 %solve_items.1 = s16[8,40,256]{2,1,0:T(8,128)(2,1)S(1)} custom-call(f32[32,256]{1,0:T(8,128)S(1)} %dynamic-slice_bitcast_fusion.start_ref, bf16[16,272,128]{2,1,0:T(8,128)(2,1)} %all-to-all-done.1.strips_ref, s32[1]{0:T(128)} %bitcast.core_ref, s16[16,8,32,256]{3,2,1,0:T(8,128)(2,1)S(1)} %bitcast.34, s16[16,8,32,256]{3,2,1,0:T(8,128)(2,1)} %collective-permute-done.other_ref), custom_call_target="tpu_custom_call" | custom-call | flops 12000000000 | bytes 10000000 | tf_op jit(solution)/shard_map/solve_items/pallas_call | solution.py:294
  80.4 12.9 %all_to_all.25 = s16[8,40,256]{2,1,0:T(8,128)(2,1)S(1)} all-to-all(s16[8,40,256]{2,1,0:T(8,128)(2,1)S(1)} %solve_items.1), channel_id=1, replica_groups=mesh['z'=8,'c'=2,'y'=4,'x'=4] {'z'}, dimensions={0} | all-to-all | bytes 327680 | tf_op jit(solution)/shard_map/all_to_all | solution.py:427
  93.3 23.3 %all-gather.5 = s16[128,40,256]{2,1,0:T(8,128)(2,1)S(1)} all-gather(s16[8,40,256]{2,1,0:T(8,128)(2,1)S(1)} %all_to_all.25), channel_id=3, replica_groups=mesh['z'=8,'c'=2,'y'=4,'x'=4] {'y','x'}, dimensions={0}, use_global_device_ids=true | all-gather | bytes 2785280 | tf_op jit(solution)/shard_map/all_gather | solution.py:428
  116.6 6.4 %collective-permute-start.1 = (s16[16,8,40,256]{3,2,1,0:T(8,128)(2,1)S(1)}, s16[16,8,40,256]{3,2,1,0:T(8,128)(2,1)S(1)}, u32[]{:S(2)}, u32[]{:S(2)}) collective-permute-start(s16[16,8,40,256]{3,2,1,0:T(8,128)(2,1)S(1)} %bitcast.31), channel_id=1, source_target_pairs={{0,16},{16,0},{1,17},{17,1},{2,18},{18,2},{3,19},{19,3},{4,20},{20... | collective-permute-start | bytes 7864328 | tf_op jit(solution)/shard_map/ppermute | solution.py:429
  123.1 0.1 pad_add_fusion.place_ref
  123.2 2.5 %dense_held.1 = (f32[1024,128]{1,0:T(8,128)S(1)}, f32[1024,128]{1,0:T(8,128)S(1)}, f32[16,256]{1,0:T(8,128)}) custom-call(bf16[16,272,128]{2,1,0:T(8,128)(2,1)} %all-to-all-done.2.strips_ref), custom_call_target="tpu_custom_call" | custom-call | flops 400000000 | bytes 3000000 | tf_op jit(solution)/shard_map/dense_held/pallas_call | solution.py:150
  125.6 2.0 %collective-permute-done.1.other_ref = s16[16,8,40,256]{3,2,1,0:T(8,128)(2,1)S(1)} collective-permute-done((s16[16,8,40,256]{3,2,1,0:T(8,128)(2,1)S(1)}, s16[16,8,40,256]{3,2,1,0:T(8,128)(2,1)S(1)}, u32[]{:S(2)}, u32[]{:S(2)}) %collective-permute-start.1) | collective-permute-done | bytes 2621472 | tf_op jit(solution)/shard_map/ppermute | solution.py:429
  127.6 15.0 %solve_held.1 = (f32[16,16,256]{2,1,0:T(8,128)S(1)}, f32[512,256]{1,0:T(8,128)}) custom-call(s32[2]{0:T(128)S(1)} %pad_add_fusion.place_ref, f32[1024,128]{1,0:T(8,128)S(1)} %get-tuple-element.25.ones_ref, f32[1024,128]{1,0:T(8,128)S(1)} %get-tuple-element.26.right_ref, s16[16,8,40,256]{3,2,1,0:T(8,128)(2,1)S(1)} %bitcast.32, ...), custom_call_target="tpu_custom_call" | custom-call | tf_op jit(solution)/shard_map/solve_held/pallas_call | solution.py:361
  142.6 12.4 %all_to_all.26 = f32[16,16,256]{2,1,0:T(8,128)S(1)} all-to-all(f32[16,16,256]{2,1,0:T(8,128)S(1)} %get-tuple-element.29), channel_id=1, replica_groups=mesh['z'=8,'c'=2,'y'=4,'x'=4] {'y','x'}, dimensions={0} | all-to-all | bytes 524288 | tf_op jit(solution)/shard_map/all_to_all | solution.py:433
  155.0 0.7 copy.15
  (20 shorter events, 0.0 us)
Async XLA Ops:
  0.6 55.6 %copy-start = (f32[512,256]{1,0:T(8,128)S(1)}, f32[512,256]{1,0:T(8,128)}, u32[]{:S(2)}) copy-start(f32[512,256]{1,0:T(8,128)} %param.11) | copy-start | bytes 1572868
  0.6 16.1 %copy-start.9 = (s32[1,1,16]{2,1,0:T(1,128)S(1)}, s32[1,1,16]{2,1,0:T(1,128)}, u32[]{:S(2)}) copy-start(s32[1,1,16]{2,1,0:T(1,128)} %param.14) | copy-start | bytes 196
  0.7 16.1 %copy-start.6 = (s32[1,1,16,2]{2,3,1,0:T(2,128)S(1)}, s32[1,1,16,2]{2,3,1,0:T(2,128)}, u32[]{:S(2)}) copy-start(s32[1,1,16,2]{2,3,1,0:T(2,128)} %param.13) | copy-start | bytes 388
  0.7 16.1 %copy-start.5 = (s32[1,1,16,2]{2,3,1,0:T(2,128)S(1)}, s32[1,1,16,2]{2,3,1,0:T(2,128)}, u32[]{:S(2)}) copy-start(s32[1,1,16,2]{2,3,1,0:T(2,128)} %param.12) | copy-start | bytes 388
  2.5 14.3 %copy-start.7 = (f32[1,256]{1,0:T(1,128)S(1)}, f32[1,256]{1,0:T(1,128)}, u32[]{:S(2)}) copy-start(f32[1,256]{1,0:T(1,128)} %get-tuple-element.16.extra_ref) | copy-start | bytes 3076
  2.5 16.9 %all-to-all-start = ((s16[8,32,256]{2,1,0:T(8,128)(2,1)}), s16[8,32,256]{2,1,0:T(8,128)(2,1)S(1)}, u32[]{:S(2)}, u32[]{:S(2)}) async-start(s16[8,32,256]{2,1,0:T(8,128)(2,1)} %get-tuple-element.17), calls=%async_computation | async-start | bytes 262144 | tf_op jit(solution)/shard_map/all_to_all | solution.py:400
  11.7 1.2 copy-start.1
  12.9 0.7 copy-start.3
  13.6 0.7 copy-start.4
  14.2 0.7 copy-start.8
  14.9 1.9 %copy-start.2 = (bf16[1,1,16,2,128,128]{5,4,3,2,1,0:T(8,128)(2,1)S(1)}, bf16[1,1,16,2,128,128]{5,4,3,2,1,0:T(8,128)(2,1)}, u32[]{:S(2)}) copy-start(bf16[1,1,16,2,128,128]{5,4,3,2,1,0:T(8,128)(2,1)} %param.15) | copy-start | bytes 3145732
  19.4 36.8 %all-to-all-start.1 = ((bf16[16,272,128]{2,1,0:T(8,128)(2,1)}), bf16[16,272,128]{2,1,0:T(8,128)(2,1)}, u32[]{:S(2)}, u32[]{:S(2)}) async-start(bf16[16,272,128]{2,1,0:T(8,128)(2,1)} %cut_items.1), calls=%async_computation.1 | async-start | bytes 2228224 | tf_op jit(solution)/shard_map/all_to_all | solution.py:414
  56.2 6.8 %collective-permute-start = (s16[16,8,32,256]{3,2,1,0:T(8,128)(2,1)S(1)}, s16[16,8,32,256]{3,2,1,0:T(8,128)(2,1)}, u32[]{:S(2)}, u32[]{:S(2)}) collective-permute-start(s16[16,8,32,256]{3,2,1,0:T(8,128)(2,1)S(1)} %bitcast.33), channel_id=1, source_target_pairs={{0,16},{16,0},{1,17},{17,1},{2,18},{18,2},{3,19},{19,3},{4,20},{20... | collective-permute-start | bytes 6291464 | tf_op jit(solution)/shard_map/ppermute | solution.py:417
  56.2 24.2 %all-to-all-start.2 = ((bf16[16,272,128]{2,1,0:T(8,128)(2,1)}), bf16[16,272,128]{2,1,0:T(8,128)(2,1)}, u32[]{:S(2)}, u32[]{:S(2)}) async-start(bf16[16,272,128]{2,1,0:T(8,128)(2,1)} %cut_held.1), calls=%async_computation.2 | async-start | bytes 2228224 | tf_op jit(solution)/shard_map/all_to_all | solution.py:418
  116.6 11.0 %collective-permute-start.1 = (s16[16,8,40,256]{3,2,1,0:T(8,128)(2,1)S(1)}, s16[16,8,40,256]{3,2,1,0:T(8,128)(2,1)S(1)}, u32[]{:S(2)}, u32[]{:S(2)}) collective-permute-start(s16[16,8,40,256]{3,2,1,0:T(8,128)(2,1)S(1)} %bitcast.31), channel_id=1, source_target_pairs={{0,16},{16,0},{1,17},{17,1},{2,18},{18,2},{3,19},{19,3},{4,20},{20... | collective-permute-start | bytes 7864328 | tf_op jit(solution)/shard_map/ppermute | solution.py:429
